TPU v7x, 128 devices: a whole 4x4x4 slice. The times are simulated.
128 devices in a mesh: front: 8 (over z, core), panel: 16 (over x, y).
Axes of the slice: x: 4, y: 4, z: 4, core: 2. Of those that a mesh axis runs over, the one named last changes fastest.
Arguments:
- pivot_columns: float32 [8, 8192, 1024], P('front', 'panel')
- child_rows: bfloat16 [8, 16, 16, 4, 8192], P('front', 'panel'), may hold values from -0.375 to 0.375
- slot_rows: int32 [8, 16, 16, 4], P('front', 'panel'), may hold values from -1 to 511, as said below
- parents: int32 [8], replicated, may hold values from 0 to 7, as said below
- pivot_rhs: float32 [8, 1024, 128], P('front'), may hold values from -6 to 6
- boundary_solution: float32 [8, 8192, 128], P('front', 'panel'), may hold values from -6 to 6
Outputs:
- panel_factor: float32 [8, 8192, 1024], P('front', 'panel')
- update_matrix: bfloat16 [8, 8192, 7168], P('front', 'panel')
- front_solution: float32 [8, 8192, 128], P('front', 'panel')
- child_solution: float32 [8, 16, 16, 4, 128], P('front', 'panel')
Inputs may be any that keep to these rules, and one draw needn't show every extreme that they name: parents[c] is the front of this level into which child front c's rows are added; a front may take several children or none. `slot_rows`: the live slots of each tile of 4 slots come first; the rows that one child front sends to one destination device are distinct; for each child front one destination device receives full tiles from every source device.
All inputs are finite; a program needn't handle non-finite values.
Results may differ from a plain program's by a relative error of at most 0.007.
Values may be sent and summed in bfloat16 or wider, within the bound.
A program may use at most 192 MiB of HBM per device.

v0:
```python
import jax
import jax.numpy as jnp
from jax import lax
from jax.sharding import PartitionSpec as P

K = 512
NSTEP = 2


def spread(shard, axis, root):
    mine = lax.axis_index(axis) == root
    return lax.psum(jnp.where(mine, shard, jnp.zeros_like(shard)), axis)


def outer_rows(mine, piece):
    return lax.dot_general(
        mine, piece, (((1,), (1,)), ((), ())), preferred_element_type=jnp.float32
    )


def scatter_term(slots, rows, local_ids, width):
    onehot = (slots.reshape(-1)[None, :] == local_ids[:, None]).astype(jnp.bfloat16)
    return jnp.dot(onehot, rows.reshape(-1, width), preferred_element_type=jnp.float32)


def on_device(pivot_columns, child_rows, slot_rows, parents, pivot_rhs, boundary_solution):
    highest = lax.Precision.HIGHEST
    panel_index = lax.axis_index("panel")
    front_index = lax.axis_index("front")
    piv_cols = pivot_columns[0]
    row_count = piv_cols.shape[0]
    pivots = piv_cols.shape[1]
    width = child_rows.shape[-1]
    rhs_count = pivot_rhs.shape[-1]
    local_ids = jnp.arange(row_count, dtype=jnp.int32)
    glob_rows = panel_index * row_count + local_ids
    rows_out = child_rows[0, 0]
    slots_out = slot_rows[0, 0]
    routed_rows, routed_slots = (
        lax.all_to_all(rows_out, "panel", split_axis=0, concat_axis=0, tiled=True),
        lax.all_to_all(slots_out, "panel", split_axis=0, concat_axis=0, tiled=True),
    )
    piece_rows = lax.all_gather(routed_rows[None], "front", axis=0, tiled=True)
    piece_slots = lax.all_gather(routed_slots[None], "front", axis=0, tiled=True)
    keeping = parents == front_index

    def add_rows(current):
        kept_slots = jnp.where(keeping[:, None, None], piece_slots, -1)
        return scatter_term(kept_slots, piece_rows, local_ids, width)

    def keep_same(current):
        return current

    assembled = lax.cond(
        jnp.any(keeping), add_rows, keep_same, jnp.zeros((row_count, width), jnp.float32)
    )
    work = assembled + jnp.concatenate(
        [piv_cols, jnp.zeros((row_count, width - pivots), jnp.float32)], axis=1
    )
    identity_block = jnp.eye(K, dtype=jnp.float32)

    def factor_block(values):
        lower = jnp.linalg.cholesky(values)
        return lax.linalg.triangular_solve(lower, identity_block, left_side=True, lower=True)

    def empty_block(values):
        return jnp.zeros_like(values)

    factors = []
    inverses = []
    for panel_step in range(NSTEP):
        low_edge = panel_step * K
        high_edge = low_edge + K
        root_rank = low_edge // row_count
        offset = low_edge - root_rank * row_count
        pivot_block = work[offset : offset + K, low_edge:high_edge]
        inverse = lax.cond(panel_index == root_rank, factor_block, empty_block, pivot_block)
        inverse = spread(inverse, "panel", root_rank)
        column = jnp.dot(work[:, low_edge:high_edge], inverse.T, precision=highest)
        column = jnp.where(glob_rows[:, None] >= low_edge, column, 0.0)
        packed = column.astype(jnp.bfloat16)
        factors.append(column)
        inverses.append(inverse)
        work = work - outer_rows(packed, lax.all_gather(packed, "panel", axis=0, tiled=True))
    factor_all = jnp.concatenate(factors, axis=1)
    trailing = work[:, pivots:]
    update_matrix = jnp.where(glob_rows[:, None] >= pivots, trailing, 0.0).astype(jnp.bfloat16)
    known = boundary_solution[0]
    right_side = pivot_rhs[0]

    def local_values(solved):
        extended = jnp.concatenate([solved, jnp.zeros((row_count, rhs_count), jnp.float32)], axis=0)
        begin = jnp.minimum(panel_index * row_count, pivots)
        segment = lax.dynamic_slice_in_dim(extended, begin, row_count)
        return jnp.where(glob_rows[:, None] < pivots, segment, known)

    solved = jnp.zeros((pivots, rhs_count), jnp.float32)
    contract_rows = (((0,), (0,)), ((), ()))
    for panel_step in reversed(range(NSTEP)):
        low_edge = panel_step * K
        high_edge = low_edge + K
        current = local_values(solved)
        masked = jnp.where(glob_rows[:, None] >= high_edge, factors[panel_step], 0.0)
        partial_sum = lax.dot_general(masked, current, contract_rows, precision=highest)
        carried = lax.psum(partial_sum, "panel")
        value = lax.dot_general(
            inverses[panel_step],
            right_side[low_edge:high_edge] - carried,
            contract_rows,
            precision=highest,
        )
        solved = solved.at[low_edge:high_edge].set(value)
    front_values = local_values(solved)
    slot_onehot = (routed_slots[..., None] == local_ids).astype(jnp.float32)
    piece = lax.all_gather(front_values[None], "front", axis=0, tiled=True)
    piece_count = piece.shape[0]
    weights = (jnp.arange(piece_count, dtype=jnp.int32) == parents[front_index]).astype(jnp.float32)
    chosen = jnp.einsum("n,nrh->rh", weights, piece, precision=highest)
    slot_values = jnp.einsum("psr,rh->psh", slot_onehot, chosen, precision=highest)
    child_values = lax.all_to_all(slot_values, "panel", split_axis=0, concat_axis=0, tiled=True)
    return (factor_all[None], update_matrix[None], front_values[None], child_values[None, None])


def solution(mesh):
    in_specs = (
        P("front", "panel", None),
        P("front", "panel", None, None, None),
        P("front", "panel", None, None),
        P(),
        P("front", None, None),
        P("front", "panel", None),
    )
    out_specs = (
        P("front", "panel", None),
        P("front", "panel", None),
        P("front", "panel", None),
        P("front", "panel", None, None, None),
    )
    return jax.shard_map(
        on_device, mesh=mesh, in_specs=in_specs, out_specs=out_specs, check_vma=False
    )
```

profile of v0, /device:TPU:1, one launch (start us, length us, event | category | flops | bytes accessed | tf_op | source)
XLA Modules:
  0.0 1002.7 jit_solution(4517287727802942974)
XLA Ops:
  7.2 23.6 %all_to_all.19 = bf16[16,4,8192]{2,1,0:T(4,128)(2,1)} all-to-all(bf16[16,4,8192]{2,1,0:T(4,128)(2,1)} %bitcast.145), channel_id=1, replica_groups=mesh['front'=8,'panel'=16] {'panel'}, dimensions={0} | all-to-all | bytes 2097152 | tf_op jit(solution)/shard_map/all_to_all | solution.py:40
  30.8 1.4 copy.30
  32.2 3.6 all-to-all-start
  37.9 4.2 all-to-all-done
  42.1 17.1 %all-gather = s32[128,1,4]{2,1,0:T(1,128)S(1)} all-gather(s32[16,1,4]{2,1,0:T(1,128)S(1)} %all-to-all-done), channel_id=2, replica_groups=mesh['front'=8,'panel'=16] {'front'}, dimensions={0}, use_global_device_ids=true | all-gather | bytes 2304 | tf_op jit(solution)/shard_map/all_gather | solution.py:44
  59.2 22.8 %all-gather.12.cloned.1.call-done = bf16[128,4,8192]{2,1,0:T(4,128)(2,1)} async-done(((bf16[16,4,8192]{2,1,0:T(4,128)(2,1)}), bf16[128,4,8192]{2,1,0:T(4,128)(2,1)}) %all-gather.12.cloned.1.call-update) | async-done | bytes 8388624 | tf_op jit(solution)/shard_map/all_gather | solution.py:43
  82.0 7.8 conditional.3
  82.0 7.8 broadcast_in_dim.87
  89.8 7.0 pad_add_fusion
  96.8 5.7 copy-done
  102.6 141.4 %conditional.4 = (f32[512,512]{0,1:T(8,128)}) conditional(s32[]{:T(128)} %convert_element_type.27, () %tuple.38, (f32[512,512]{1,0:T(8,128)S(1)}, f32[512,512]{1,0:T(8,128)S(1)}) %tuple.39), branch_computations={%region_3.4_spmd, %region_4.15_spmd} | conditional | flops 1412760064 | bytes 26743068 | solution.py:77
  104.4 11.7 %cholesky.286 = f32[128,128]{1,0:T(8,128)S(1)} custom-call(f32[128,128]{1,0:T(8,128)S(1)} %cholesky.426), custom_call_target="Cholesky" | custom-call | tf_op jit(solution)/shard_map/cond/branch_1_fun/jit(cholesky)/cholesky | solution.py:63
  116.2 9.8 custom-call.27
  128.6 11.7 %cholesky.305 = f32[128,128]{1,0:T(8,128)S(1)} custom-call(f32[128,128]{1,0:T(8,128)S(1)} %cholesky.430), custom_call_target="Cholesky" | custom-call | tf_op jit(solution)/shard_map/cond/branch_1_fun/jit(cholesky)/cholesky | solution.py:63
  142.5 10.0 %custom-call.28 = f32[1,128,128]{1,2,0:T(8,128)S(1)} custom-call(f32[1,128,128]{2,1,0:T(8,128)S(1)} %get-tuple-element.139), custom_call_target="InvertDiagBlocksLowerTriangular" | custom-call | tf_op jit(solution)/shard_map/cond/branch_1_fun/jit(cholesky)/cholesky | solution.py:63
  154.1 11.7 %cholesky.326 = f32[128,128]{1,0:T(8,128)S(1)} custom-call(f32[128,128]{1,0:T(8,128)S(1)} %cholesky.435), custom_call_target="Cholesky" | custom-call | tf_op jit(solution)/shard_map/cond/branch_1_fun/jit(cholesky)/cholesky | solution.py:63
  167.1 9.8 custom-call.29
  178.4 11.7 %cholesky.343 = f32[128,128]{1,0:T(8,128)S(1)} custom-call(f32[128,128]{1,0:T(8,128)S(1)} %convolution_subtract_fusion.5), custom_call_target="Cholesky" | custom-call | tf_op jit(solution)/shard_map/cond/branch_1_fun/jit(cholesky)/cholesky | solution.py:63
  192.0 8.0 while.6
  192.6 1.4 bitcast_dynamic-update-slice_fusion.5
  194.6 1.4 bitcast_dynamic-update-slice_fusion.5
  196.6 1.4 bitcast_dynamic-update-slice_fusion.5
  198.6 1.4 bitcast_dynamic-update-slice_fusion.5
  200.0 39.3 %custom-call.30 = f32[4,128,128]{1,2,0:T(8,128)S(1)} custom-call(f32[4,128,128]{2,1,0:T(8,128)S(1)} %get-tuple-element.77), custom_call_target="InvertDiagBlocksLowerTriangular" | custom-call | tf_op jit(solution)/shard_map/cond/branch_1_fun/triangular_solve/custom-call.3 | solution.py:64
  242.6 1.3 copy.41
  244.0 2.3 broadcast_select_fusion.2
  246.4 96.5 %all-reduce.11.cloned.1.call-done = f32[512,512]{0,1:T(8,128)} async-done(((f32[512,512]{0,1:T(8,128)}), f32[512,512]{0,1:T(8,128)}) %all-reduce.11.cloned.1.call-update) | async-done | bytes 1048592 | tf_op jit(solution)/shard_map/psum | solution.py:12
  342.9 4.2 fusion.110
  347.2 78.2 %all-gather.8.cloned.1.call-done = bf16[8192,512]{0,1:T(8,128)(2,1)} async-done(((bf16[512,512]{0,1:T(8,128)(2,1)}), bf16[8192,512]{0,1:T(8,128)(2,1)}) %all-gather.8.cloned.1.call-update) | async-done | bytes 8388624 | tf_op jit(solution)/shard_map/all_gather | solution.py:84
  425.4 18.7 %convolution_subtract_fusion.12 = f32[512,8192]{1,0:T(8,128)} fusion(f32[512,8192]{1,0:T(8,128)} %copy-done, bf16[512,512]{0,1:T(8,128)(2,1)} %get-tuple-element.163, bf16[8192,512]{0,1:T(8,128)(2,1)} %all-gather.8.cloned.1.call-done), kind=kOutput, calls=%fused_computation.141 | convolution fusion | flops 4299161600 | bytes 42467328 | tf_op jit(solution)/shard_map/dot_general | solution.py:16
  445.4 8.3 conditional.5
  454.9 236.9 %all-reduce.13.cloned.1.call-done = f32[512,512]{0,1:T(8,128)} async-done(((f32[512,512]{0,1:T(8,128)}), f32[512,512]{0,1:T(8,128)}) %all-reduce.13.cloned.1.call-update) | async-done | bytes 1048592 | tf_op jit(solution)/shard_map/psum | solution.py:12
  691.8 4.2 fusion.111
  696.1 1.8 fusion.69
  698.0 83.6 %all-reduce.15.cloned.1.call-done = f32[512,128]{1,0:T(8,128)} async-done(((f32[512,128]{1,0:T(8,128)}), f32[512,128]{1,0:T(8,128)}) %all-reduce.15.cloned.1.call-update) | async-done | bytes 262160 | tf_op jit(solution)/shard_map/psum | solution.py:105
  781.5 2.3 fusion.85
  783.8 1.8 fusion.71
  785.7 83.5 %all-reduce.17.cloned.1.call-done = f32[512,128]{1,0:T(8,128)} async-done(((f32[512,128]{1,0:T(8,128)}), f32[512,128]{1,0:T(8,128)}) %all-reduce.17.cloned.1.call-update) | async-done | bytes 262160 | tf_op jit(solution)/shard_map/psum | solution.py:105
  869.1 2.3 fusion.86
  873.9 25.2 %all-gather.14.cloned.1.call-done = f32[4096,128]{1,0:T(8,128)} async-done(((f32[512,128]{1,0:T(8,128)}), f32[4096,128]{1,0:T(8,128)}) %all-gather.14.cloned.1.call-update) | async-done | bytes 2097168 | tf_op jit(solution)/shard_map/all_gather | solution.py:115
  899.1 4.4 fusion.67
  904.4 6.8 all-to-all-start.2
  911.2 1.5 maximum_bitcast_fusion
  912.7 2.9 copy.37
  915.6 2.1 all-to-all-done.2
  917.7 60.9 %all-gather.10.cloned.1.call-done = bf16[8192,512]{0,1:T(8,128)(2,1)} async-done(((bf16[512,512]{0,1:T(8,128)(2,1)}), bf16[8192,512]{0,1:T(8,128)(2,1)}) %all-gather.10.cloned.1.call-update) | async-done | bytes 8388624 | tf_op jit(solution)/shard_map/all_gather | solution.py:84
  978.6 7.1 fusion.112
  985.8 9.0 fusion.66
  (85 shorter events, 24.8 us)
Async XLA Ops:
  7.2 74.9 %all-gather.12.cloned.1.call-start = ((), (), s32[]{:S(2)}) async-start(), calls=%async_computation.9 | async-start | bytes 9437184 | tf_op jit(solution)/shard_map/all_gather | solution.py:43
  32.2 10.0 all-to-all-start
  35.8 307.1 %all-reduce.11.cloned.1.call-start = ((), (), s32[]{:S(2)}) async-start(), calls=%async_computation.3 | async-start | bytes 2097152 | tf_op jit(solution)/shard_map/psum | solution.py:12
  96.8 5.7 copy-start
  103.4 1.0 copy-start.2
  246.4 179.0 %all-gather.8.cloned.1.call-start = ((), (), s32[]{:S(2)}) async-start(), calls=%async_computation.4 | async-start | bytes 8912896 | tf_op jit(solution)/shard_map/all_gather | solution.py:84
  347.2 344.7 %all-reduce.13.cloned.1.call-start = ((), (), s32[]{:S(2)}) async-start(), calls=%async_computation.5 | async-start | bytes 2097152 | tf_op jit(solution)/shard_map/psum | solution.py:12
  445.3 250.7 %copy-start.4 = (f32[1,512,128]{2,1,0:T(8,128)S(1)}, f32[1,512,128]{2,1,0:T(8,128)}, u32[]{:S(2)}) copy-start(f32[1,512,128]{2,1,0:T(8,128)} %param.24) | copy-start | bytes 786436
  453.6 327.9 %copy-start.6 = (f32[1,1024,128]{2,1,0:T(8,128)S(1)}, f32[1,1024,128]{2,1,0:T(8,128)}, u32[]{:S(2)}) copy-start(f32[1,1024,128]{2,1,0:T(8,128)} %param.23) | copy-start | bytes 1572868
  453.6 419.6 %copy-start.7 = (s32[8]{0:T(128)S(1)}, s32[8]{0:T(128)}, u32[]{:S(2)}) copy-start(s32[8]{0:T(128)} %param.22) | copy-start | bytes 100
  454.7 326.8 %all-reduce.15.cloned.1.call-start = ((), (), s32[]{:S(2)}) async-start(), calls=%async_computation.7 | async-start | bytes 524288 | tf_op jit(solution)/shard_map/psum | solution.py:105
  697.9 171.2 %all-reduce.17.cloned.1.call-start = ((), (), s32[]{:S(2)}) async-start(), calls=%async_computation.8 | async-start | bytes 524288 | tf_op jit(solution)/shard_map/psum | solution.py:105
  783.8 194.8 %copy-start.1 = (bf16[512,512]{0,1:T(8,128)(2,1)S(1)}, bf16[512,512]{0,1:T(8,128)(2,1)}, u32[]{:S(2)}) copy-start(bf16[512,512]{0,1:T(8,128)(2,1)} %get-tuple-element.165) | copy-start | bytes 1572868
  785.6 113.5 %all-gather.14.cloned.1.call-start = ((), (), s32[]{:S(2)}) async-start(), calls=%async_computation.10 | async-start | bytes 2359296 | tf_op jit(solution)/shard_map/all_gather | solution.py:115
  872.4 106.2 %all-gather.10.cloned.1.call-start = ((), (), s32[]{:S(2)}) async-start(), calls=%async_computation.6 | async-start | bytes 8912896 | tf_op jit(solution)/shard_map/all_gather | solution.py:84
  904.4 13.3 %all-to-all-start.2 = ((f32[16,4,128]{2,1,0:T(4,128)}), f32[16,4,128]{2,1,0:T(4,128)S(1)}, u32[]{:S(2)}, u32[]{:S(2)}) async-start(f32[16,4,128]{2,1,0:T(4,128)} %copy.36), calls=%async_computation.2 | async-start | bytes 65536 | tf_op jit(solution)/shard_map/all_to_all | solution.py:120
Sparse Core Ops, SparseCore 0:
  30.9 51.0 all-gather.11
  246.5 96.4 all-reduce.10
  347.3 78.0 all-gather.7
  454.9 236.9 all-reduce.12
  698.0 83.4 all-reduce.14
  785.7 83.3 all-reduce.16
  872.5 26.4 all-gather.13
  901.2 77.4 all-gather.9
where the time goes:
time: 1010 us; the launch traced here: 1000 us
  waiting for transfers between devices  695 us (69%)
  other arithmetic  142 us (14%)
  matrix products  55.6 us (6%)
  blocking collectives  40.7 us (4%)
  local copies, waits for them, and re-layouts  32.9 us (3%)
  between operations  15.5 us (2%)
  starting transfers between devices  10.8 us (1%)
  loops' own time  10.5 us (1%)
    psum x2, waiting for transfers between devices, spread(): return lax.psum(jnp.where(mine, shard, jnp.zeros_like(shard)), axis)  333 us
    psum x2, waiting for transfers between devices, on_device(): carried = lax.psum(partial_sum, 'panel')  167 us
    all_gather x2, waiting for transfers between devices, on_device(): lax.all_gather(packed, 'panel', axis=0, tiled=True)  139 us
    another operation x14, other arithmetic, factor_block(): lower = jnp.linalg.cholesky(values)  78.6 us
    another operation x5, other arithmetic, factor_block(): lax.linalg.triangular_solve(lower, identity_block, left_side=True, lower=...  40 us
    dot_general x2, matrix products, outer_rows(): lax.dot_general(mine, piece, (((1,), (1,)), ((), ())), preferred_element_...  25.8 us
    all_gather x1, waiting for transfers between devices, on_device(): piece = lax.all_gather(front_values[None], 'front', axis=0, tiled=True)  25.2 us
    all_to_all x1, blocking collectives, on_device(): lax.all_to_all(rows_out, 'panel', split_axis=0, concat_axis=0, tiled=True)  23.6 us
  transfers between devices with their start and end apart: 10, of which 10 were waited for; matrix products, arithmetic and copies ran while one was open for 1% of the time, Pallas kernels for 0%

commit v1 on v0

v1 whole, which is shorter than its diff:
```python
import jax
import jax.numpy as jnp
from jax import lax
from jax.experimental import pallas as pl
from jax.experimental.pallas import tpu as pltpu
from jax.sharding import PartitionSpec as P

K = 512
NB = 128
PIV = 1024
HIGHEST = lax.Precision.HIGHEST
HIGH = lax.Precision.HIGH
MESH = pl.DeviceIdType.MESH
F32 = jnp.float32
BF16 = jnp.bfloat16


def product(left, right, left_dim, right_dim, precision=HIGHEST):
    dims = (((left_dim,), (right_dim,)), ((), ()))
    return lax.dot_general(left, right, dims, precision=precision, preferred_element_type=F32)


def base_inverse(work, inverse):
    sub = lax.broadcasted_iota(jnp.int32, (8, NB), 0)
    lane = lax.broadcasted_iota(jnp.int32, (8, NB), 1)
    for tile in range(NB // 8):
        inverse[8 * tile : 8 * tile + 8, :] = (lane == sub + 8 * tile).astype(F32)
    for step in range(NB // 8):
        low = 8 * step
        left = work[low : low + 8, :]
        right = inverse[low : low + 8, :]
        columns = [jnp.broadcast_to(left[:, low + i : low + i + 1], (8, NB)) for i in range(8)]
        pivots = jnp.ones((8, NB), F32)
        recips, splats, rows = [], [], []
        for i in range(8):
            pivot = jnp.broadcast_to(columns[i][i : i + 1, :], (8, NB))
            recip = 1.0 / pivot
            recips.append(recip)
            pivots = jnp.where(sub == i, pivot, pivots)
            ratio = jnp.where(sub > i, columns[i] * recip, 0.0)
            splat = {}
            for j in range(i + 1, 8):
                splat[j] = jnp.broadcast_to(columns[j][i : i + 1, :], (8, NB))
                columns[j] = columns[j] - ratio * splat[j]
            splats.append(splat)
            left_row = jnp.broadcast_to(left[i : i + 1, :], (8, NB))
            right_row = jnp.broadcast_to(right[i : i + 1, :], (8, NB))
            rows.append((left_row, right_row))
            left = left - ratio * left_row
            right = right - ratio * right_row
        for tile in range(step + 1, NB // 8):
            at = 8 * tile
            left_tile = work[at : at + 8, :]
            right_tile = inverse[at : at + 8, :]
            ratios = []
            for i in range(8):
                value = jnp.broadcast_to(left_tile[:, low + i : low + i + 1], (8, NB))
                for j in range(i):
                    value = value - ratios[j] * splats[j][i]
                ratios.append(value * recips[i])
            for i in range(8):
                left_tile = left_tile - ratios[i] * rows[i][0]
                right_tile = right_tile - ratios[i] * rows[i][1]
            work[at : at + 8, :] = left_tile
            inverse[at : at + 8, :] = right_tile
        inverse[low : low + 8, :] = right * lax.rsqrt(pivots)


def factor_inverse(work, inverse, base_work, base_out):
    inverse[...] = jnp.zeros_like(inverse)
    for block in range(K // NB):
        low, high = block * NB, block * NB + NB
        base_work[...] = work[low:high, low:high]
        base_inverse(base_work, base_out)
        base = base_out[...]
        if block:
            inverse[low:high, 0:low] = product(base, inverse[low:high, 0:low], 1, 0)
        inverse[low:high, low:high] = base
        if high < K:
            upper = product(base, work[low:high, high:], 1, 0)
            work[high:, high:] = work[high:, high:] - product(upper, upper, 0, 0)
            inverse[high:, 0:high] = inverse[high:, 0:high] - product(upper, inverse[low:high, 0:high], 0, 0)


def pivot_kernel(top, inverse0, inverse1, factor10, work, base_work, base_out):
    block = top[0, :, 0:K]
    work[...] = (block + block.T) * 0.5
    factor_inverse(work, inverse0, base_work, base_out)
    lower = product(top[1, :, 0:K], inverse0[...], 1, 1)
    factor10[...] = lower
    packed = lower.astype(BF16)
    block = top[1, :, K:] - product(packed, packed, 1, 1, None)
    work[...] = (block + block.T) * 0.5
    factor_inverse(work, inverse1, base_work, base_out)


def factor_pivots(top):
    square = jax.ShapeDtypeStruct((K, K), F32)
    return pl.pallas_call(
        pivot_kernel,
        out_shape=(square, square, square),
        in_specs=[pl.BlockSpec(memory_space=pltpu.VMEM)],
        out_specs=[pl.BlockSpec(memory_space=pltpu.VMEM)] * 3,
        scratch_shapes=[pltpu.VMEM((K, K), F32), pltpu.VMEM((NB, NB), F32), pltpu.VMEM((NB, NB), F32)],
        compiler_params=pltpu.CompilerParams(vmem_limit_bytes=40 << 20),
        cost_estimate=pl.CostEstimate(flops=60_000_000_000, bytes_accessed=8 << 20, transcendentals=0),
    )(top)


def spread_kernel(count, mine, top, chunk, scatter_send, scatter_recv, gather_send, gather_recv, local_sem):
    me = lax.axis_index("panel")
    part = mine.shape[0] // count
    barrier = pltpu.get_barrier_semaphore()
    for shift in range(1, count):
        peer = lax.rem(me + shift, count)
        pl.semaphore_signal(barrier, inc=1, device_id={"panel": peer}, device_id_type=MESH)
    pl.semaphore_wait(barrier, count - 1)

    def scatter(shift, root):
        peer = lax.rem(me + shift, count)
        return pltpu.make_async_remote_copy(
            src_ref=mine.at[pl.ds(pl.multiple_of(peer * part, 8), part)],
            dst_ref=chunk.at[root],
            send_sem=scatter_send.at[root, shift],
            recv_sem=scatter_recv.at[root],
            device_id={"panel": peer},
            device_id_type=MESH,
        )

    for root in range(2):

        @pl.when(me == root)
        def _():
            for shift in range(1, count):
                scatter(shift, root).start()
            own = pltpu.make_async_copy(
                mine.at[pl.ds(pl.multiple_of(me * part, 8), part)], chunk.at[root], local_sem
            )
            own.start()
            own.wait()

        @pl.when(me != root)
        def _():
            scatter(1, root).wait_recv()

    def gather(shift):
        peer = lax.rem(me + shift, count)
        return pltpu.make_async_remote_copy(
            src_ref=chunk,
            dst_ref=top.at[:, pl.ds(pl.multiple_of(me * part, 8), part)],
            send_sem=gather_send.at[shift],
            recv_sem=gather_recv.at[shift],
            device_id={"panel": peer},
            device_id_type=MESH,
        )

    for shift in range(1, count):
        gather(shift).start()
    own = pltpu.make_async_copy(chunk, top.at[:, pl.ds(pl.multiple_of(me * part, 8), part)], local_sem)
    own.start()
    own.wait()
    for shift in range(1, count):
        gather(shift).wait()
    for root in range(2):

        @pl.when(me == root)
        def _():
            for shift in range(1, count):
                scatter(shift, root).wait_send()


def spread_pivots(count, mine):
    rows, width = mine.shape
    return pl.pallas_call(
        lambda *refs: spread_kernel(count, *refs),
        name="spread",
        out_shape=jax.ShapeDtypeStruct((2, rows, width), F32),
        in_specs=[pl.BlockSpec(memory_space=pl.ANY)],
        out_specs=pl.BlockSpec(memory_space=pl.ANY),
        scratch_shapes=[
            pltpu.VMEM((2, rows // count, width), F32),
            pltpu.SemaphoreType.DMA((2, count)),
            pltpu.SemaphoreType.DMA((2,)),
            pltpu.SemaphoreType.DMA((count,)),
            pltpu.SemaphoreType.DMA((count,)),
            pltpu.SemaphoreType.DMA,
        ],
        compiler_params=pltpu.CompilerParams(collective_id=0, has_side_effects=True),
    )(mine)


def on_device(panel_count, pivot_columns, child_rows, slot_rows, parents, pivot_rhs, boundary_solution):
    panel_index = lax.axis_index("panel")
    front_index = lax.axis_index("front")
    piv_cols = pivot_columns[0]
    row_count = piv_cols.shape[0]
    pivots = piv_cols.shape[1]
    rows_out = child_rows[0, 0]
    cap = rows_out.shape[1]
    local_ids = jnp.arange(row_count, dtype=jnp.int32)

    def exchange(value):
        moved = lax.all_to_all(value, "panel", split_axis=0, concat_axis=0, tiled=True)
        return lax.all_gather(moved, "front", axis=0)

    slots = exchange(slot_rows[0, 0])
    keeping = parents == front_index
    kept = jnp.where(keeping[:, None, None], slots, -1).reshape(-1)
    onehot = (kept[None, :] == local_ids[:, None]).astype(BF16)
    early = exchange(rows_out[:, :, :pivots])
    known = boundary_solution[0]
    columns = piv_cols + jnp.dot(onehot, early.reshape(-1, pivots), preferred_element_type=F32)
    gathered = lax.all_gather(columns.astype(BF16), "panel", axis=0, tiled=True)
    late = exchange(rows_out[:, :, pivots:])
    below = panel_index >= pivots // row_count
    sums = lax.psum(product(columns, jnp.where(below, known, 0.0), 0, 0), "panel")

    top = spread_pivots(panel_count, columns)
    inverse0, inverse1, factor10 = factor_pivots(top)
    packed10 = factor10.astype(BF16)

    factor0 = product(columns[:, :K], inverse0, 1, 1, HIGH)
    current = columns[:, K:] - product(factor0.astype(BF16), packed10, 1, 1, None)
    factor1 = jnp.where(panel_index >= 1, product(current, inverse1, 1, 1, HIGH), 0.0)
    weight1 = product(factor1, inverse1, 1, 0, HIGH)
    weight0 = product(factor0 - product(weight1, factor10, 1, 0, HIGH), inverse0, 1, 0, HIGH)
    weights = jnp.concatenate([weight0, weight1], axis=1).astype(BF16)
    factor_all = jnp.concatenate([factor0, factor1], axis=1)

    trailing = jnp.dot(onehot, late.reshape(-1, late.shape[-1]), preferred_element_type=F32)
    trailing = trailing - product(weights, gathered[pivots:], 1, 1, None)
    update_matrix = jnp.where(below, trailing, 0.0).astype(BF16)

    sums0, sums1 = sums[:K], sums[K:]
    right_side = pivot_rhs[0]
    half = product(inverse0, sums0, 1, 0)
    carried1 = product(inverse1, sums1 - product(factor10, half, 1, 0), 1, 0)
    solved1 = product(inverse1, right_side[K:] - carried1, 0, 0)
    carried0 = half + product(factor10, solved1, 0, 0)
    solved0 = product(inverse0, right_side[:K] - carried0, 0, 0)
    front_values = jnp.where(below, known, jnp.where(panel_index == 0, solved0, solved1))

    pick = (kept[:, None] == local_ids[None, :]).astype(F32)
    picked = product(pick, front_values, 1, 0).reshape(slots.shape[0], -1, front_values.shape[-1])
    picked = jnp.sum(lax.all_to_all(picked, "front", split_axis=0, concat_axis=0, tiled=True), axis=0)
    picked = picked.reshape(-1, cap, picked.shape[-1])
    child_values = lax.all_to_all(picked, "panel", split_axis=0, concat_axis=0, tiled=True)
    return (factor_all[None], update_matrix[None], front_values[None], child_values[None, None])


def solution(mesh):
    in_specs = (
        P("front", "panel", None),
        P("front", "panel", None, None, None),
        P("front", "panel", None, None),
        P(),
        P("front", None, None),
        P("front", "panel", None),
    )
    out_specs = (
        P("front", "panel", None),
        P("front", "panel", None),
        P("front", "panel", None),
        P("front", "panel", None, None, None),
    )
    panel_count = mesh.shape["panel"]
    return jax.shard_map(
        lambda *arrays: on_device(panel_count, *arrays),
        mesh=mesh,
        in_specs=in_specs,
        out_specs=out_specs,
        check_vma=False,
    )
```

time: 1010 us -> 399 us (0.40)
  waiting for transfers between devices: 695 us -> 109 us
  other arithmetic: 142 us -> 2.86 us
  Pallas kernels: 0 us -> 123 us
  starting transfers between devices: 10.8 us -> 30.5 us
  loops' own time: 10.5 us -> 0 us
    psum x4 -> x1, waiting for transfers between devices: 500 us -> 7.57 us  [on_device(): lax.psum(product(columns, jnp.where(below, known, 0.0), 0, 0), 'panel')]
    pallas_call x0 -> x2, Pallas kernels: none -> 123 us  [the longest x1 82.1 us: spread_pivots(): pl.pallas_call(lambda *refs: spread_kernel(count, *refs), name='spread',...]
    another operation x19 -> x0, other arithmetic: 119 us -> none  [the longest x14 78.6 us: factor_block(): lower = jnp.linalg.cholesky(values)]
    all_gather x4 -> x3, waiting for transfers between devices: 187 us -> 88.6 us  [the longest x1 88.5 us: on_device(): gathered = lax.all_gather(columns.astype(BF16), 'panel', axis=0, tiled=True)]
    all_to_all x2 -> x4, starting transfers between devices: 10.5 us -> 30.3 us  [the longest x1 16.2 us: on_device(): lax.all_to_all(picked, 'panel', split_axis=0, concat_axis=0, tiled=True)]
    reshape x0 -> x2, local copies, waits for them, and re-layouts: none -> 13.5 us  [the longest x1 12.1 us: on_device(): late.reshape(-1, late.shape[-1])]
    another operation x4 -> x0, loops' own time: 10.5 us -> none  [the longest x2 10.4 us: on_device(): lax.cond(panel_index == root_rank, factor_block, empty_block, pivot_block)]
    dot_general x10 -> x17, matrix products: 47.1 us -> 56 us  [the longest x15 41.9 us: product(): lax.dot_general(left, right, dims, precision=precision, preferred_element...]
  transfers between devices with their start and end apart: 10 -> 8, of which waited for: 10 -> 5; matrix products, arithmetic and copies ran while one was open for 1% -> 16% of each run, Pallas kernels for 0% -> 31%
where the time goes in v1:
time: 399 us; the launch traced here: 393 us
  Pallas kernels  123 us (31%)
  waiting for transfers between devices  109 us (27%)
  matrix products  56 us (14%)
  blocking collectives  31.4 us (8%)
  starting transfers between devices  30.5 us (8%)
  local copies, waits for them, and re-layouts  25.7 us (6%)
  between operations  14.4 us (4%)
    all_gather x1, waiting for transfers between devices, on_device(): gathered = lax.all_gather(columns.astype(BF16), 'panel', axis=0, tiled=True)  88.5 us
    pallas_call x1, Pallas kernels, spread_pivots(): pl.pallas_call(lambda *refs: spread_kernel(count, *refs), name='spread',...  82.1 us
    dot_general x15, matrix products, product(): lax.dot_general(left, right, dims, precision=precision, preferred_element...  41.9 us
    pallas_call x1, Pallas kernels, factor_pivots(): pl.pallas_call(pivot_kernel, out_shape=(square, square, square), in_specs...  40.9 us
    all_gather x1, blocking collectives, exchange(): return lax.all_gather(moved, 'front', axis=0)  17 us
    all_to_all x1, starting transfers between devices, on_device(): lax.all_to_all(picked, 'panel', split_axis=0, concat_axis=0, tiled=True)  16.2 us
    all_to_all x1, blocking collectives, exchange(): lax.all_to_all(value, 'panel', split_axis=0, concat_axis=0, tiled=True)  14.4 us
    reshape x1, local copies, waits for them, and re-layouts, on_device(): late.reshape(-1, late.shape[-1])  12.1 us
  transfers between devices with their start and end apart: 8, of which 5 were waited for; matrix products, arithmetic and copies ran while one was open for 16% of the time, Pallas kernels for 31%

profile of v1, /device:TPU:1, one launch (start us, length us, event | category | flops | bytes accessed | tf_op | source)
XLA Modules:
  0.0 393.1 jit_solution(11471343663650133209)
XLA Ops:
  7.2 1.0 slice.44
  8.2 14.4 %all_to_all.29 = bf16[16,4,1024]{2,1,0:T(4,128)(2,1)} all-to-all(bf16[16,4,1024]{2,1,0:T(4,128)(2,1)S(1)} %slice.44), channel_id=1, replica_groups=mesh['front'=8,'panel'=16] {'panel'}, dimensions={0} | all-to-all | bytes 262144 | tf_op jit(solution)/shard_map/all_to_all | solution.py:203
  22.5 1.4 copy.13
  23.9 3.5 all-to-all-start
  27.4 2.4 slice.47
  29.8 0.7 broadcast_compare_fusion
  30.5 3.2 all-to-all-done
  33.7 4.3 %all-to-all-start.2 = ((bf16[16,4,7168]{2,1,0:T(4,128)(2,1)}), bf16[16,4,7168]{2,1,0:T(4,128)(2,1)}, u32[]{:S(2)}, u32[]{:S(2)}) async-start(bf16[16,4,7168]{2,1,0:T(4,128)(2,1)} %slice.47), calls=%async_computation.2 | async-start | bytes 1835008 | tf_op jit(solution)/shard_map/all_to_all | solution.py:203
  38.0 0.0 all-reduce.2.cloned.1.call-start
  38.0 17.0 %all-gather = s32[128,1,4]{2,1,0:T(1,128)S(1)} all-gather(s32[16,1,4]{2,1,0:T(1,128)S(1)} %all-to-all-done), channel_id=2, replica_groups=mesh['front'=8,'panel'=16] {'front'}, dimensions={0}, use_global_device_ids=true | all-gather | bytes 2304 | tf_op jit(solution)/shard_map/all_gather | solution.py:204
  55.0 0.1 bitcast_select_fusion.2
  55.1 0.1 eq.39
  55.3 1.4 reshape.29
  56.7 3.3 fusion.28
  60.0 4.2 %fusion.23 = f32[1024,128]{1,0:T(8,128)} fusion(f32[512,1024]{1,0:T(8,128)S(1)} %get-tuple-element.23.refs_0_, f32[1,512,128]{2,1,0:T(8,128)S(1)} %copy-done.7, pred[]{:T(512)S(6)} %ge.7), kind=kOutput, calls=%fused_computation.33 | convolution fusion | flops 805371904 | bytes 2883585 | tf_op jit(solution)/shard_map/dot_general | solution.py:20
  64.3 0.7 all-gather.11.cloned.1.call-update
  65.0 0.5 all-gather.7.cloned.1.call-update
  65.6 82.1 %spread.1.top = f32[2,512,1024]{2,1,0:T(8,128)} custom-call(f32[512,1024]{1,0:T(8,128)} %copy-done.1), custom_call_target="tpu_custom_call" | custom-call | tf_op jit(solution)/shard_map/spread/pallas_call | solution.py:174
  147.6 2.2 copy-done
  149.8 40.9 %shard_map.93 = (f32[512,512]{1,0:T(8,128)S(1)}, f32[512,512]{1,0:T(8,128)S(1)}, f32[512,512]{1,0:T(8,128)S(1)}) custom-call(f32[2,512,1024]{2,1,0:T(8,128)S(1)} %copy-done), custom_call_target="tpu_custom_call" | custom-call | flops 60000002048 | bytes 8388608 | tf_op jit(solution)/shard_map/pallas_call | solution.py:99
  190.8 1.0 fusion.9
  191.8 0.5 convolution_subtract_fusion.1
  192.3 1.0 convolution_select_fusion
  193.3 1.0 copy-done.5
  194.3 1.9 fusion.29
  196.2 2.3 convolution_subtract_fusion
  198.5 7.6 %all-reduce.2.cloned.1.call-done = f32[1024,128]{1,0:T(8,128)} async-done(((f32[1024,128]{1,0:T(8,128)}), f32[1024,128]{1,0:T(8,128)}) %all-reduce.2.cloned.1.call-update) | async-done | bytes 524304 | tf_op jit(solution)/shard_map/psum | solution.py:216
  206.0 2.0 fusion.21
  208.0 1.9 convolution_subtract_fusion.3
  210.0 1.9 convolution_subtract_fusion.2
  211.9 1.8 fusion.30
  213.8 1.8 fusion.8
  215.6 1.8 fusion.7
  217.4 0.7 copy-done.8
  218.1 1.4 fusion.15
  219.5 6.4 %all-to-all-start.3 = ((f32[8,64,128]{2,1,0:T(8,128)}), f32[8,64,128]{2,1,0:T(8,128)S(1)}, u32[]{:S(2)}, u32[]{:S(2)}) async-start(f32[8,64,128]{2,1,0:T(8,128)} %bitcast.49), calls=%async_computation.3 | async-start | bytes 524288 | tf_op jit(solution)/shard_map/all_to_all | solution.py:245
  225.8 3.1 convolution_convert_fusion
  228.9 6.7 %all-to-all-done.3 = f32[8,64,128]{2,1,0:T(8,128)S(1)} async-done(((f32[8,64,128]{2,1,0:T(8,128)}), f32[8,64,128]{2,1,0:T(8,128)S(1)}, u32[]{:S(2)}, u32[]{:S(2)}) %all-to-all-start.3) | async-done | bytes 262176 | tf_op jit(solution)/shard_map/all_to_all | solution.py:245
  235.6 0.6 reduce_sum.9
  236.2 16.2 %all-to-all-start.4 = ((f32[16,4,128]{2,1,0:T(4,128)}), f32[16,4,128]{2,1,0:T(4,128)S(1)}, u32[]{:S(2)}, u32[]{:S(2)}) async-start(f32[16,4,128]{2,1,0:T(4,128)} %bitcast.11), calls=%async_computation.4 | async-start | bytes 65536 | tf_op jit(solution)/shard_map/all_to_all | solution.py:247
  252.4 1.5 maximum_bitcast_fusion
  253.9 2.9 copy.15
  256.8 2.1 all-to-all-done.4
  258.9 12.1 %reshape.30 = bf16[512,7168]{1,0:T(8,128)(2,1)} reshape(bf16[128,4,7168]{2,1,0:T(4,128)(2,1)} %all-gather.11.cloned.1.call-done) | data formatting | bytes 14680064 | tf_op jit(solution)/shard_map/reshape | solution.py:230
  271.0 10.7 %fusion.14 = f32[512,7168]{1,0:T(8,128)} fusion(bf16[512,7168]{1,0:T(8,128)(2,1)} %reshape.30, s32[512]{0:T(512)S(1)} %eq.39), kind=kOutput, calls=%fused_computation.23 | convolution fusion | flops 3758358528 | bytes 22022144 | tf_op jit(solution)/shard_map/dot_general | solution.py:230
  281.8 88.5 %all-gather.7.cloned.1.call-done = bf16[8192,1024]{1,0:T(8,128)(2,1)} async-done(((bf16[512,1024]{1,0:T(8,128)(2,1)}), bf16[8192,1024]{1,0:T(8,128)(2,1)}) %all-gather.7.cloned.1.call-update) | async-done | bytes 16777232 | tf_op jit(solution)/shard_map/all_gather | solution.py:213
  370.3 15.2 %fusion.4 = bf16[1,512,7168]{2,1,0:T(8,128)(2,1)} fusion(f32[512,7168]{1,0:T(8,128)} %fusion.14, bf16[8192,1024]{1,0:T(8,128)(2,1)} %all-gather.7.cloned.1.call-done, pred[]{:T(512)S(6)} %ge.7, bf16[512,512]{0,1:T(8,128)(2,1)S(1)} %copy-done.9, bf16[512,512]{0,1:T(8,128)(2,1)S(1)} %copy-done.10), kind=kOutput, calls=%fused_computation.3 | convolution fusion | flops 7529299968 | bytes 37748736 | tf_op jit(solution)/shard_map/dot_general | solution.py:20
  385.5 0.6 copy.19
  (29 shorter events, 0.2 us)
Async XLA Ops:
  7.2 48.1 %all-gather.9.cloned.1.call-start = ((), (), s32[]{:S(2)}) async-start(), calls=%async_computation.7 | async-start | bytes 1179648 | tf_op jit(solution)/shard_map/all_gather | solution.py:204
  23.9 9.8 %all-to-all-start = ((s32[16,1,4]{2,1,0:T(1,128)}), s32[16,1,4]{2,1,0:T(1,128)S(1)}, u32[]{:S(2)}, u32[]{:S(2)}) async-start(s32[16,1,4]{2,1,0:T(1,128)} %copy.13), calls=%async_computation | async-start | bytes 16384 | tf_op jit(solution)/shard_map/all_to_all | solution.py:203
  33.7 30.6 %all-to-all-start.2 = ((bf16[16,4,7168]{2,1,0:T(4,128)(2,1)}), bf16[16,4,7168]{2,1,0:T(4,128)(2,1)}, u32[]{:S(2)}, u32[]{:S(2)}) async-start(bf16[16,4,7168]{2,1,0:T(4,128)(2,1)} %slice.47), calls=%async_computation.2 | async-start | bytes 1835008 | tf_op jit(solution)/shard_map/all_to_all | solution.py:203
  38.0 168.0 %all-reduce.2.cloned.1.call-start = ((), (), s32[]{:S(2)}) async-start(), calls=%async_computation.6 | async-start | bytes 1048576 | tf_op jit(solution)/shard_map/psum | solution.py:216
  55.2 4.7 %copy-start.7 = (f32[1,512,128]{2,1,0:T(8,128)S(1)}, f32[1,512,128]{2,1,0:T(8,128)}, u32[]{:S(2)}) copy-start(f32[1,512,128]{2,1,0:T(8,128)} %param.11) | copy-start | bytes 786436
  60.0 5.6 %copy-start.1 = (f32[512,1024]{1,0:T(8,128)}, f32[512,1024]{1,0:T(8,128)S(1)}, u32[]{:S(2)}) copy-start(f32[512,1024]{1,0:T(8,128)S(1)} %get-tuple-element.23.refs_0_) | copy-start | bytes 6291460
  64.2 194.6 %all-gather.11.cloned.1.call-start = ((), (), s32[]{:S(2)}) async-start(), calls=%async_computation.8 | async-start | bytes 8257536 | tf_op jit(solution)/shard_map/all_gather | solution.py:204
  65.0 305.3 %all-gather.7.cloned.1.call-start = ((), (), s32[]{:S(2)}) async-start(), calls=%async_computation.5 | async-start | bytes 17825792 | tf_op jit(solution)/shard_map/all_gather | solution.py:213
  147.6 2.2 copy-start
  149.8 40.9 %copy-start.2 = (f32[512,1024]{1,0:T(8,128)S(1)}, f32[512,1024]{1,0:T(8,128)}, u32[]{:S(2)}) copy-start(f32[512,1024]{1,0:T(8,128)} %copy-done.1) | copy-start | bytes 6291460
  191.8 4.4 %copy-start.3 = (f32[512,512]{0,1:T(8,128)}, f32[512,512]{0,1:T(8,128)S(1)}, u32[]{:S(2)}) copy-start(f32[512,512]{0,1:T(8,128)S(1)} %fusion.9) | copy-start | bytes 3145732
  193.3 1.0 copy-start.5
  206.0 7.7 %copy-start.11 = (f32[1,1024,128]{2,1,0:T(8,128)S(1)}, f32[1,1024,128]{2,1,0:T(8,128)}, u32[]{:S(2)}) copy-start(f32[1,1024,128]{2,1,0:T(8,128)} %param.10) | copy-start | bytes 1572868
  213.8 38.7 %copy-start.4 = (f32[512,512]{0,1:T(8,128)S(1)}, f32[512,512]{0,1:T(8,128)}, u32[]{:S(2)}) copy-start(f32[512,512]{0,1:T(8,128)} %copy-done.3) | copy-start | bytes 3145732
  215.6 36.9 %copy-start.6 = (f32[512,512]{0,1:T(8,128)S(1)}, f32[512,512]{0,1:T(8,128)}, u32[]{:S(2)}) copy-start(f32[512,512]{0,1:T(8,128)} %copy-done.5) | copy-start | bytes 3145732
  217.4 0.7 copy-start.8
  219.5 16.1 %all-to-all-start.3 = ((f32[8,64,128]{2,1,0:T(8,128)}), f32[8,64,128]{2,1,0:T(8,128)S(1)}, u32[]{:S(2)}, u32[]{:S(2)}) async-start(f32[8,64,128]{2,1,0:T(8,128)} %bitcast.49), calls=%async_computation.3 | async-start | bytes 524288 | tf_op jit(solution)/shard_map/all_to_all | solution.py:245
  236.2 22.7 %all-to-all-start.4 = ((f32[16,4,128]{2,1,0:T(4,128)}), f32[16,4,128]{2,1,0:T(4,128)S(1)}, u32[]{:S(2)}, u32[]{:S(2)}) async-start(f32[16,4,128]{2,1,0:T(4,128)} %bitcast.11), calls=%async_computation.4 | async-start | bytes 65536 | tf_op jit(solution)/shard_map/all_to_all | solution.py:247
  271.0 99.3 %copy-start.9 = (bf16[512,512]{0,1:T(8,128)(2,1)S(1)}, bf16[512,512]{0,1:T(8,128)(2,1)}, u32[]{:S(2)}) copy-start(bf16[512,512]{0,1:T(8,128)(2,1)} %get-tuple-element.24) | copy-start | bytes 1572868
  271.0 99.3 %copy-start.10 = (bf16[512,512]{0,1:T(8,128)(2,1)S(1)}, bf16[512,512]{0,1:T(8,128)(2,1)}, u32[]{:S(2)}) copy-start(bf16[512,512]{0,1:T(8,128)(2,1)} %convolution_convert_fusion) | copy-start | bytes 1572868
Sparse Core Ops, SparseCore 0:
  22.7 24.1 all-gather.8
  64.4 141.6 all-reduce.1
  207.8 49.4 all-gather.10
  259.6 110.6 all-gather.6

commit v2 on v1

v2 whole, which is shorter than its diff:
```python
import math

import jax
import jax.numpy as jnp
from jax import lax
from jax.experimental import pallas as pl
from jax.experimental.pallas import tpu as pltpu
from jax.sharding import PartitionSpec as P

K = 512
NB = 128
PIV = 1024
HIGHEST = lax.Precision.HIGHEST
HIGH = lax.Precision.HIGH
MESH = pl.DeviceIdType.MESH
F32 = jnp.float32
BF16 = jnp.bfloat16


def product(left, right, left_dim, right_dim, precision=HIGHEST):
    dims = (((left_dim,), (right_dim,)), ((), ()))
    return lax.dot_general(left, right, dims, precision=precision, preferred_element_type=F32)


def base_inverse(work, inverse):
    sub = lax.broadcasted_iota(jnp.int32, (8, NB), 0)
    lane = lax.broadcasted_iota(jnp.int32, (NB, NB), 1)
    row = lax.broadcasted_iota(jnp.int32, (NB, NB), 0)
    inverse[...] = (lane == row).astype(F32)
    for step in range(NB // 8):
        low = 8 * step
        left = work[low : low + 8, :]
        right = inverse[low : low + 8, :]
        columns = [jnp.broadcast_to(left[:, low + i : low + i + 1], (8, NB)) for i in range(8)]
        pivots = jnp.ones((8, NB), F32)
        recips, splats, rows = [], [], []
        for i in range(8):
            pivot = columns[i][i : i + 1, :]
            recip = 1.0 / pivot
            recips.append(recip)
            pivots = jnp.where(sub == i, pivot, pivots)
            ratio = jnp.where(sub > i, columns[i] * recip, 0.0)
            splat = {}
            for j in range(i + 1, 8):
                splat[j] = columns[j][i : i + 1, :]
                columns[j] = columns[j] - ratio * splat[j]
            splats.append(splat)
            rows.append((left[i : i + 1, :], right[i : i + 1, :]))
            left = left - ratio * rows[i][0]
            right = right - ratio * rows[i][1]
        at = low + 8
        while at < NB:
            size = min(32 - at % 32, NB - at)
            left_tile = work[at : at + size, :]
            right_tile = inverse[at : at + size, :]
            ratios = []
            for i in range(8):
                value = jnp.broadcast_to(left_tile[:, low + i : low + i + 1], (size, NB))
                for j in range(i):
                    value = value - ratios[j] * splats[j][i]
                ratios.append(value * recips[i])
            for i in range(8):
                left_tile = left_tile - ratios[i] * rows[i][0]
                right_tile = right_tile - ratios[i] * rows[i][1]
            work[at : at + size, :] = left_tile
            inverse[at : at + size, :] = right_tile
            at += size
        inverse[low : low + 8, :] = right * lax.rsqrt(pivots)


def symmetric_part(block):
    return (block + block.T) * 0.5


def factor_block(low, work, inverse, base_work, base_out):
    rows = pl.ds(low, NB)
    base_work[...] = work[rows, rows]
    base_inverse(base_work, base_out)
    base = base_out[...]
    upper = product(base, work[rows, :], 1, 0)
    lane = lax.broadcasted_iota(jnp.int32, upper.shape, 1)
    upper = jnp.where(lane >= low + NB, upper, 0.0)
    solved = product(base, inverse[rows, :], 1, 0)
    work[...] = work[...] - product(upper, upper, 0, 0)
    inverse[...] = inverse[...] - product(upper, solved, 0, 0)
    inverse[rows, :] = solved


def exchange_kernel(
    counts, rows, slots, early, late, table, send_a, recv_a, send_b, recv_b, send_s, recv_s,
    front_send, front_recv, front_send_s, front_recv_s, local_sem
):
    panels, fronts = counts
    me = lax.axis_index("panel")
    front = lax.axis_index("front")
    tiles = early.shape[1]
    barrier = pltpu.get_barrier_semaphore()
    for shift in range(1, panels):
        peer = lax.rem(me + shift, panels)
        pl.semaphore_signal(barrier, inc=1, device_id={"panel": peer}, device_id_type=MESH)
    for shift in range(1, fronts):
        peer = lax.rem(front + shift, fronts)
        pl.semaphore_signal(barrier, inc=1, device_id={"front": peer}, device_id_type=MESH)
    pl.semaphore_wait(barrier, panels + fronts - 2)

    def to_panel(source, target, send, recv, shift):
        peer = lax.rem(me + shift, panels)
        return pltpu.make_async_remote_copy(
            src_ref=source(peer),
            dst_ref=target,
            send_sem=send.at[shift],
            recv_sem=recv.at[shift],
            device_id={"panel": peer},
            device_id_type=MESH,
        )

    def early_copy(shift):
        return to_panel(lambda p: rows.at[p, pl.ds(0, tiles)], early.at[front, :, me], send_a, recv_a, shift)

    def slot_copy(shift):
        return to_panel(lambda p: slots.at[p], table.at[front, me], send_s, recv_s, shift)

    def late_copy(shift):
        return to_panel(lambda p: rows.at[p, pl.ds(tiles, late.shape[0])], late.at[:, me], send_b, recv_b, shift)

    for shift in range(1, panels):
        slot_copy(shift).start()
        early_copy(shift).start()
    own = [
        pltpu.make_async_copy(rows.at[me, pl.ds(0, tiles)], early.at[front, :, me], local_sem.at[0]),
        pltpu.make_async_copy(slots.at[me], table.at[front, me], local_sem.at[1]),
        pltpu.make_async_copy(rows.at[me, pl.ds(tiles, late.shape[0])], late.at[:, me], local_sem.at[2]),
    ]
    for copy in own:
        copy.start()
    for shift in range(1, panels):
        late_copy(shift).start()
    for copy in own:
        copy.wait()
    for shift in range(1, panels):
        slot_copy(shift).wait_recv()
        early_copy(shift).wait_recv()

    def to_front(array, send, recv, shift):
        peer = lax.rem(front + shift, fronts)
        return pltpu.make_async_remote_copy(
            src_ref=array.at[front],
            dst_ref=array.at[front],
            send_sem=send.at[shift],
            recv_sem=recv.at[shift],
            device_id={"front": peer},
            device_id_type=MESH,
        )

    for shift in range(1, fronts):
        to_front(table, front_send_s, front_recv_s, shift).start()
        to_front(early, front_send, front_recv, shift).start()
    for shift in range(1, panels):
        slot_copy(shift).wait_send()
        early_copy(shift).wait_send()
        late_copy(shift).wait()
    for shift in range(1, fronts):
        to_front(table, front_send_s, front_recv_s, shift).wait()
        to_front(early, front_send, front_recv, shift).wait()


def exchange_rows(panels, fronts, rows, slots, tiles):
    _, all_tiles, cap, lanes = rows.shape
    sem = pltpu.SemaphoreType.DMA
    return pl.pallas_call(
        lambda *refs: exchange_kernel((panels, fronts), *refs),
        name="exchange",
        out_shape=(
            jax.ShapeDtypeStruct((fronts, tiles, panels, cap, lanes), BF16),
            jax.ShapeDtypeStruct((all_tiles - tiles, panels, cap, lanes), BF16),
            jax.ShapeDtypeStruct((fronts, panels, cap, lanes), jnp.int32),
        ),
        in_specs=[pl.BlockSpec(memory_space=pl.ANY)] * 2,
        out_specs=[pl.BlockSpec(memory_space=pl.ANY)] * 3,
        scratch_shapes=[sem((panels,))] * 6 + [sem((fronts,))] * 4 + [sem((3,))],
        compiler_params=pltpu.CompilerParams(collective_id=1, has_side_effects=True),
    )(rows, slots)


def panel_kernel(
    counts, side, halves, columns, partial, late, blocks, inverses, factor10, sums, late_all,
    top, chunk, pieces, work, base_work, base_out,
    scatter_send, scatter_recv, whole_send, whole_recv, half_send, half_recv,
    far_send, far_recv, farther_send, farther_recv,
    piece_send, piece_recv, sum_send, sum_recv, late_send, late_recv, local_sem,
):
    panels, fronts = counts
    me = lax.axis_index("panel")
    front = lax.axis_index("front")
    across, along = me // side, lax.rem(me, side)
    part = top.shape[1] // panels
    barrier = pltpu.get_barrier_semaphore()
    for shift in range(1, panels):
        peer = lax.rem(me + shift, panels)
        pl.semaphore_signal(barrier, inc=1, device_id={"panel": peer}, device_id_type=MESH)
    for shift in range(1, fronts):
        peer = lax.rem(front + shift, fronts)
        pl.semaphore_signal(barrier, inc=1, device_id={"front": peer}, device_id_type=MESH)
    pl.semaphore_wait(barrier, panels + fronts - 2)

    def chunk_rows(who):
        return pl.ds(pl.multiple_of(who * part, 8), part)

    def scatter(shift, index):
        peer = lax.rem(me + shift, panels)
        lanes = pl.ds(K if index == 2 else 0, K)
        return pltpu.make_async_remote_copy(
            src_ref=columns.at[chunk_rows(peer), lanes],
            dst_ref=chunk.at[index],
            send_sem=scatter_send.at[index, shift],
            recv_sem=scatter_recv.at[index],
            device_id={"panel": peer},
            device_id_type=MESH,
        )

    def own_chunk(index):
        lanes = pl.ds(K if index == 2 else 0, K)
        return pltpu.make_async_copy(columns.at[chunk_rows(me), lanes], chunk.at[index], local_sem.at[index])

    roots = ((0, (0,)), (1, (1, 2)))
    for root, indices in roots:

        @pl.when(me == root)
        def _():
            for shift in range(1, panels):
                for index in indices:
                    scatter(shift, index).start()
            for index in indices:
                own_chunk(index).start()

    def place(half, first, second):
        first, second = lax.rem(first + side, side), lax.rem(second + side, side)
        return first * side + second if half == 0 else second * side + first

    spots = (across, along), (along, across)

    def view(kind, half, who, rows):
        if kind == 0:
            size = part if rows is None else part // 2
            low = who * part + (part // 2 if rows == 1 else 0)
            return top.at[:, pl.ds(pl.multiple_of(low, 8), size), pl.ds(half * (K // 2), K // 2)]
        ref = blocks.at[half, who]
        return ref if rows is None else ref.at[pl.ds(rows * (K // 2), K // 2)]

    def move(kind, half, who, rows, target, send, recv, slot):
        ref = view(kind, half, who, rows)
        return pltpu.make_async_remote_copy(
            src_ref=ref,
            dst_ref=ref,
            send_sem=send.at[slot],
            recv_sem=recv.at[slot],
            device_id={"panel": target},
            device_id_type=MESH,
        )

    def whole(kind, half, way):
        u, v = spots[half]
        target = place(half, u + (1 if way == 0 else -1), v)
        return move(kind, half, me, None, target, whole_send, whole_recv, (kind, half, way))

    def halved(kind, half, way):
        u, v = spots[half]
        step = 1 if way == 0 else -1
        return move(
            kind, half, place(half, u - step, v), way, place(half, u + step, v), half_send, half_recv, (kind, half, way)
        )

    def far(kind, half, offset, way):
        u, v = spots[half]
        target = place(half, u, v + (1 if way == 0 else -1))
        return move(
            kind, half, place(half, u + offset, v), None, target, far_send, far_recv, (kind, half, offset, way)
        )

    def farther(kind, half, offset, way):
        u, v = spots[half]
        step = 1 if way == 0 else -1
        return move(
            kind, half, place(half, u + offset, v - step), way, place(half, u, v + step),
            farther_send, farther_recv, (kind, half, offset, way),
        )

    both = [(half, way) for half in range(2) for way in range(2)]

    def begin(kind):
        for half, way in both:
            whole(kind, half, way).start()
        for half, way in both:
            far(kind, half, 0, way).start()

    def second(kind):
        for half, way in both:
            whole(kind, half, way).wait_recv()
            halved(kind, half, way).start()
        for half, way in both:
            far(kind, half, 1, way).start()
            far(kind, half, 3, way).start()

    def third(kind):
        for half in range(2):
            for way in range(2):
                halved(kind, half, way).wait_recv()
            for way in range(2):
                far(kind, half, 2, way).start()

    def relay(kind, offset):
        for half, way in both:
            far(kind, half, offset, way).wait_recv()
            farther(kind, half, offset, way).start()

    def finish(kind):
        for half, way in both:
            for offset in range(4):
                farther(kind, half, offset, way).wait_recv()

    def drain(kind):
        for half, way in both:
            whole(kind, half, way).wait_send()
            halved(kind, half, way).wait_send()
            for offset in range(4):
                far(kind, half, offset, way).wait_send()
                farther(kind, half, offset, way).wait_send()

    def late_copy(shift):
        peer = lax.rem(front + shift, fronts)
        return pltpu.make_async_remote_copy(
            src_ref=late,
            dst_ref=late_all.at[front],
            send_sem=late_send.at[shift],
            recv_sem=late_recv.at[shift],
            device_id={"front": peer},
            device_id_type=MESH,
        )

    def piece_copy(shift):
        peer = lax.rem(me + shift, panels)
        return pltpu.make_async_remote_copy(
            src_ref=partial.at[peer],
            dst_ref=pieces.at[me],
            send_sem=piece_send.at[shift],
            recv_sem=piece_recv.at[shift],
            device_id={"panel": peer},
            device_id_type=MESH,
        )

    def sum_copy(shift):
        peer = lax.rem(me + shift, panels)
        return pltpu.make_async_remote_copy(
            src_ref=sums.at[me],
            dst_ref=sums.at[me],
            send_sem=sum_send.at[shift],
            recv_sem=sum_recv.at[shift],
            device_id={"panel": peer},
            device_id_type=MESH,
        )

    own = [
        pltpu.make_async_copy(halves, blocks.at[:, me], local_sem.at[3]),
        pltpu.make_async_copy(partial.at[me], pieces.at[me], local_sem.at[4]),
        pltpu.make_async_copy(late, late_all.at[front], local_sem.at[5]),
    ]
    for copy in own:
        copy.start()
    for copy in own:
        copy.wait()
    for root, indices in roots:
        for index in indices:

            @pl.when(me == root)
            def _():
                own_chunk(index).wait()

            @pl.when(me != root)
            def _():
                scatter(1, index).wait_recv()

    top[:, chunk_rows(me), :] = chunk[...]
    begin(0)
    begin(1)
    for shift in range(1, fronts):
        late_copy(shift).start()
    for shift in range(1, panels):
        piece_copy(shift).start()
    second(0)
    third(0)
    for offset in (0, 1, 3, 2):
        relay(0, offset)
    finish(0)
    second(1)

    lane = lax.broadcasted_iota(jnp.int32, (K, K), 1)
    row = lax.broadcasted_iota(jnp.int32, (K, K), 0)

    def block_step(index, carry):
        which = index // (K // NB)

        @pl.when(index == 0)
        def _():
            work[...] = symmetric_part(top[0])
            inverses[0] = (lane == row).astype(F32)

        @pl.when(index == K // NB)
        def _():
            lower = product(top[1], inverses[0], 1, 1)
            factor10[...] = lower
            packed = lower.astype(BF16)
            work[...] = symmetric_part(top[2] - product(packed, packed, 1, 1, None))
            inverses[1] = (lane == row).astype(F32)

        low = pl.multiple_of((index - which * (K // NB)) * NB, NB)
        factor_block(low, work, inverses.at[which], base_work, base_out)

        @pl.when(index == 1)
        def _():
            third(1)
            relay(1, 0)

        @pl.when(index == 2)
        def _():
            for shift in range(1, panels):
                piece_copy(shift).wait_recv()
            total = pieces[0]
            for who in range(1, panels):
                total = total + pieces[who]
            sums[me] = total
            for shift in range(1, panels):
                sum_copy(shift).start()

        @pl.when(index == 3)
        def _():
            relay(1, 1)
            relay(1, 3)

        @pl.when(index == 6)
        def _():
            relay(1, 2)

        return carry

    lax.fori_loop(0, 2 * (K // NB), block_step, 0)
    finish(1)
    drain(0)
    drain(1)
    for shift in range(1, panels):
        piece_copy(shift).wait_send()
        sum_copy(shift).wait()
    for shift in range(1, fronts):
        late_copy(shift).wait()
    for root, indices in roots:

        @pl.when(me == root)
        def _():
            for shift in range(1, panels):
                for index in indices:
                    scatter(shift, index).wait_send()


def panel_step(panels, fronts, side, halves, columns, partial, late):
    sem = pltpu.SemaphoreType.DMA
    part = K // panels
    anywhere = pl.BlockSpec(memory_space=pl.ANY)
    vmem = pl.BlockSpec(memory_space=pltpu.VMEM)
    return pl.pallas_call(
        lambda *refs: panel_kernel((panels, fronts), side, *refs),
        name="panel_step",
        out_shape=(
            jax.ShapeDtypeStruct((2, panels, K, K), BF16),
            jax.ShapeDtypeStruct((2, K, K), F32),
            jax.ShapeDtypeStruct((K, K), F32),
            jax.ShapeDtypeStruct(partial.shape, F32),
            jax.ShapeDtypeStruct((fronts,) + late.shape, BF16),
        ),
        in_specs=[anywhere] * 4,
        out_specs=[anywhere, vmem, vmem, vmem, anywhere],
        scratch_shapes=[
            pltpu.VMEM((3, K, K), F32),
            pltpu.VMEM((3, part, K), F32),
            pltpu.VMEM(partial.shape, F32),
            pltpu.VMEM((K, K), F32),
            pltpu.VMEM((NB, NB), F32),
            pltpu.VMEM((NB, NB), F32),
            sem((3, panels)),
            sem((3,)),
        ]
        + [sem((2, 2, 2))] * 4
        + [sem((2, 2, 4, 2))] * 4
        + [sem((panels,))] * 4
        + [sem((fronts,))] * 2
        + [sem((6,))],
        compiler_params=pltpu.CompilerParams(
            collective_id=2, has_side_effects=True, vmem_limit_bytes=40 << 20
        ),
    )(halves, columns, partial, late)


def on_device(sizes, pivot_columns, child_rows, slot_rows, parents, pivot_rhs, boundary_solution):
    panels, fronts, side = sizes
    panel_index = lax.axis_index("panel")
    front_index = lax.axis_index("front")
    piv_cols = pivot_columns[0]
    row_count, pivots = piv_cols.shape
    rows_out = child_rows[0, 0]
    cap, width = rows_out.shape[1:]
    lanes = NB
    local_ids = jnp.arange(row_count, dtype=jnp.int32)

    rows_tiled = rows_out.reshape(panels, cap, width // lanes, lanes).transpose(0, 2, 1, 3)
    slots_wide = jnp.broadcast_to(slot_rows[0, 0][:, :, None], (panels, cap, lanes))
    early, late, table = exchange_rows(panels, fronts, rows_tiled, slots_wide, pivots // lanes)
    slots = table[:, :, :, 0].reshape(fronts, panels * cap)
    keeping = parents == front_index
    kept = jnp.where(keeping[:, None], slots, -1).reshape(-1)
    onehot = (kept[None, :] == local_ids[:, None]).astype(BF16)
    early = early.reshape(fronts, pivots // lanes, panels * cap, lanes)
    spread = jnp.einsum(
        "rck,ctkl->rtl", onehot.reshape(row_count, fronts, panels * cap), early, preferred_element_type=F32
    )
    columns = piv_cols + spread.reshape(row_count, pivots)
    known = boundary_solution[0]
    below = panel_index >= pivots // row_count
    halves = jnp.stack([columns[:, :K], columns[:, K:]]).astype(BF16)
    partial = product(columns, jnp.where(below, known, 0.0), 0, 0, HIGH)
    partial = partial.reshape(panels, pivots // panels, -1)

    blocks, inverses, factor10, sums, late_all = panel_step(
        panels, fronts, side, halves, columns, partial, late
    )
    inverse0, inverse1 = inverses[0], inverses[1]
    packed10 = factor10.astype(BF16)

    factor0 = product(columns[:, :K], inverse0, 1, 1, HIGH)
    current = columns[:, K:] - product(factor0.astype(BF16), packed10, 1, 1, None)
    factor1 = jnp.where(panel_index >= 1, product(current, inverse1, 1, 1, HIGH), 0.0)
    weight1 = product(factor1, inverse1, 1, 0, HIGH)
    weight0 = product(factor0 - product(weight1, factor10, 1, 0, HIGH), inverse0, 1, 0, HIGH)
    factor_all = jnp.concatenate([factor0, factor1], axis=1)
    first = pivots // K
    trailing = jnp.einsum(
        "rck,ctkl->rtl",
        onehot.reshape(row_count, fronts, panels * cap),
        late_all.reshape(fronts, -1, panels * cap, lanes),
        preferred_element_type=F32,
    ).reshape(row_count, -1)
    gathered = blocks[:, first:].reshape(2, -1, K)
    trailing = trailing - product(weight0.astype(BF16), gathered[0], 1, 1, None)
    trailing = trailing - product(weight1.astype(BF16), gathered[1], 1, 1, None)
    update_matrix = jnp.where(below, trailing, 0.0).astype(BF16)

    sums = sums.reshape(pivots, -1)
    sums0, sums1 = sums[:K], sums[K:]
    right_side = pivot_rhs[0]
    half = product(inverse0, sums0, 1, 0)
    carried1 = product(inverse1, sums1 - product(factor10, half, 1, 0), 1, 0)
    solved1 = product(inverse1, right_side[K:] - carried1, 0, 0)
    carried0 = half + product(factor10, solved1, 0, 0)
    solved0 = product(inverse0, right_side[:K] - carried0, 0, 0)
    front_values = jnp.where(below, known, jnp.where(panel_index == 0, solved0, solved1))

    pick = (kept[:, None] == local_ids[None, :]).astype(F32)
    picked = product(pick, front_values, 1, 0).reshape(fronts, panels * cap, -1)
    picked = jnp.sum(lax.all_to_all(picked, "front", split_axis=0, concat_axis=0, tiled=True), axis=0)
    picked = picked.reshape(panels, cap, -1)
    child_values = lax.all_to_all(picked, "panel", split_axis=0, concat_axis=0, tiled=True)
    return (factor_all[None], update_matrix[None], front_values[None], child_values[None, None])


def solution(mesh):
    in_specs = (
        P("front", "panel", None),
        P("front", "panel", None, None, None),
        P("front", "panel", None, None),
        P(),
        P("front", None, None),
        P("front", "panel", None),
    )
    out_specs = (
        P("front", "panel", None),
        P("front", "panel", None),
        P("front", "panel", None),
        P("front", "panel", None, None, None),
    )
    panels, fronts = mesh.shape["panel"], mesh.shape["front"]
    sizes = (panels, fronts, math.isqrt(panels))
    return jax.shard_map(
        lambda *arrays: on_device(sizes, *arrays),
        mesh=mesh,
        in_specs=in_specs,
        out_specs=out_specs,
        check_vma=False,
    )
```

time: 399 us -> 282 us (0.71)
  waiting for transfers between devices: 109 us -> 2.07 us
  Pallas kernels: 123 us -> 184 us
  blocking collectives: 31.4 us -> 0 us
  starting transfers between devices: 30.5 us -> 10.7 us
  between operations: 14.4 us -> 1.16 us
  local copies, waits for them, and re-layouts: 25.7 us -> 19.3 us
    all_gather x3 -> x0, waiting for transfers between devices: 88.6 us -> none  [the longest x1 88.5 us: on_device(): gathered = lax.all_gather(columns.astype(BF16), 'panel', axis=0, tiled=True)]
    pallas_call x2, Pallas kernels: 123 us -> 184 us  [the longest x1 151 us: panel_step(): pl.pallas_call(lambda *refs: panel_kernel((panels, fronts), side, *refs),...]
    all_gather x1 -> x0, blocking collectives: 17 us -> none  [exchange(): return lax.all_gather(moved, 'front', axis=0)]
    all_to_all x1 -> x0, blocking collectives: 14.4 us -> none  [exchange(): lax.all_to_all(value, 'panel', split_axis=0, concat_axis=0, tiled=True)]
    reshape x2 -> x0, local copies, waits for them, and re-layouts: 13.5 us -> none  [the longest x1 12.1 us: on_device(): late.reshape(-1, late.shape[-1])]
    all_to_all x1, starting transfers between devices: 16.2 us -> 5.81 us  [on_device(): lax.all_to_all(picked, 'panel', split_axis=0, concat_axis=0, tiled=True)]
    all_to_all x2 -> x0, starting transfers between devices: 7.77 us -> none  [exchange(): lax.all_to_all(value, 'panel', split_axis=0, concat_axis=0, tiled=True)]
    psum x1 -> x0, waiting for transfers between devices: 7.57 us -> none  [on_device(): lax.psum(product(columns, jnp.where(below, known, 0.0), 0, 0), 'panel')]
  transfers between devices with their start and end apart: 8 -> 2, of which waited for: 5 -> 1; matrix products, arithmetic and copies ran while one was open for 16% -> 19% of each run, Pallas kernels for 31% -> 0%
where the time goes in v2:
time: 282 us; the launch traced here: 277 us
  Pallas kernels  184 us (65%)
  matrix products  56.3 us (20%)
  local copies, waits for them, and re-layouts  19.3 us (7%)
  starting transfers between devices  10.7 us (4%)
  other arithmetic  2.91 us (1%)
    pallas_call x1, Pallas kernels, panel_step(): pl.pallas_call(lambda *refs: panel_kernel((panels, fronts), side, *refs),...  151 us
    dot_general x16, matrix products, product(): lax.dot_general(left, right, dims, precision=precision, preferred_element...  36.3 us
    pallas_call x1, Pallas kernels, exchange_rows(): pl.pallas_call(lambda *refs: exchange_kernel((panels, fronts), *refs), na...  33.2 us
    dot_general x2, matrix products, on_device(): jnp.einsum('rck,ctkl->rtl', onehot.reshape(row_count, fronts, panels * ca...  20 us
    slice x1, local copies, waits for them, and re-layouts, on_device(): trailing = trailing - product(weight0.astype(BF16), gathered[0], 1, 1, None)  6.24 us
    all_to_all x1, starting transfers between devices, on_device(): lax.all_to_all(picked, 'panel', split_axis=0, concat_axis=0, tiled=True)  5.81 us
  transfers between devices with their start and end apart: 2, of which 1 were waited for; matrix products, arithmetic and copies ran while one was open for 19% of the time, Pallas kernels for 0%

profile of v2, /device:TPU:1, one launch (start us, length us, event | category | flops | bytes accessed | tf_op | source)
XLA Modules:
  0.0 276.6 jit_solution(13125074974781969204)
XLA Ops:
  0.6 0.7 broadcast_compare_fusion
  1.3 0.1 broadcast_in_dim.50.clone
  1.4 0.1 broadcast_in_dim.60
  1.5 0.8 copy.22
  2.2 0.7 broadcast_in_dim.52.refs_1_
  2.9 33.2 %exchange.1 = (bf16[8,8,16,4,128]{4,3,2,1,0:T(4,128)(2,1)}, bf16[56,16,4,128]{3,2,1,0:T(4,128)(2,1)}, s32[8,16,4,128]{3,2,1,0:T(4,128)}) custom-call(bf16[16,64,4,128]{3,2,1,0:T(4,128)(2,1)} %bitcast.105, s32[16,4,128]{2,1,0:T(4,128)} %broadcast_in_dim.52.refs_1_), custom_call_target="tpu_custom_call" | custom-call | tf_op jit(solution)/shard_map/exchange/pallas_call | solution.py:170
  36.2 3.2 %slice_reduce_fusion = (s32[8,16,4]{2,1,0:T(8,128)S(1)}, s32[8,16,4,1]{3,2,1,0:T(4,128)S(1)}) fusion(s32[8,16,4,128]{3,2,1,0:T(4,128)} %get-tuple-element.12), kind=kLoop, calls=%fused_computation.67 | loop fusion | bytes 6144 | tf_op jit(solution)/shard_map/slice | solution.py:515
  39.3 0.1 reshape_squeeze.10
  39.5 0.5 copy.23
  39.9 0.1 copy.24
  40.0 2.8 bitcast_add_fusion.refs_1_
  42.8 0.0 copy-start
  42.8 0.1 fusion.35
  42.9 1.9 copy.26
  44.8 0.1 pad_maximum_fusion.refs_0_
  44.9 0.8 copy-done.9
  45.7 2.6 fusion.44.refs_2_
  48.4 150.9 %panel_step.1 = (bf16[2,16,512,512]{3,2,1,0:T(8,128)(2,1)}, f32[2,512,512]{2,1,0:T(8,128)S(1)}, f32[512,512]{1,0:T(8,128)S(1)}, f32[16,64,128]{2,1,0:T(8,128)S(1)}, bf16[8,56,16,4,128]{4,3,2,1,0:T(4,128)(2,1)}) custom-call(bf16[2,512,512]{2,1,0:T(8,128)(2,1)S(1)} %pad_maximum_fusion.refs_0_, f32[512,1024]{1,0:T(8,128)S(1)} %copy-done.1, ...), custom_call_target="tpu_custom_call" | custom-call | tf_op jit(solution)/shard_map/panel_step/pallas_call | solution.py:468
  199.2 0.0 copy-start.11
  199.3 1.0 fusion.17
  200.3 1.0 convolution_subtract_fusion.3
  201.3 1.0 convolution_subtract_fusion.2
  202.3 1.8 fusion.10
  204.1 1.8 fusion.7
  205.9 1.8 fusion.6
  207.7 0.0 copy-start.10
  207.7 0.7 copy-done.10
  208.4 1.4 fusion.25
  209.8 4.9 %all-to-all-start = ((f32[8,64,128]{2,1,0:T(8,128)}), f32[8,64,128]{2,1,0:T(8,128)S(1)}, u32[]{:S(2)}, u32[]{:S(2)}) async-start(f32[8,64,128]{2,1,0:T(8,128)} %bitcast.106), calls=%async_computation | async-start | bytes 524288 | tf_op jit(solution)/shard_map/all_to_all | solution.py:566
  214.7 3.3 %fusion.20 = f32[512,512]{0,1:T(8,128)} fusion(f32[512,1024]{1,0:T(8,128)} %copy-done, f32[2,512,512]{2,1,0:T(8,128)S(1)} %get-tuple-element.15), kind=kOutput, calls=%fused_computation.32 | convolution fusion | flops 805306368 | bytes 3145728 | tf_op jit(solution)/shard_map/dot_general | solution.py:22
  218.0 2.0 convolution_subtract_fusion.1
  220.0 1.0 convolution_select_fusion
  221.0 0.0 copy-start.7
  221.0 1.0 fusion.13
  222.1 0.6 copy-done.3
  222.6 1.0 convolution_subtract_fusion
  223.7 1.0 convolution_convert_fusion
  224.7 0.0 copy-start.6
  224.7 6.2 %fusion.50 = (bf16[1,14,512,512]{3,2,1,0:T(8,128)(2,1)S(1)}, bf16[1,14,512,512]{3,2,1,0:T(8,128)(2,1)S(1)}) fusion(bf16[2,16,512,512]{3,2,1,0:T(8,128)(2,1)} %get-tuple-element.18), kind=kLoop, calls=%fused_computation.68 | loop fusion | bytes 29360128 | tf_op jit(solution)/shard_map/slice | solution.py:550
  231.0 7.3 %fusion.38 = f32[512,7168]{1,0:T(8,128)} fusion(bf16[7168,512]{1,0:T(8,128)(2,1)S(1)} %bitcast.103, f32[512,512]{1,0:T(8,128)S(1)} %copy-done.6), kind=kOutput, calls=%fused_computation.52 | convolution fusion | flops 3758358528 | bytes 23068672 | tf_op jit(solution)/shard_map/dot_general | solution.py:22
  238.3 7.3 %fusion.52 = f32[512,7168]{1,0:T(8,128)} fusion(bf16[512,512]{1,0:T(8,128)(2,1)S(1)} %convolution_convert_fusion, bf16[7168,512]{1,0:T(8,128)(2,1)S(1)} %bitcast.102), kind=kOutput, calls=%fused_computation.70 | convolution fusion | flops 3758096384 | bytes 22544384 | tf_op jit(solution)/shard_map/dot_general | solution.py:22
  245.6 17.3 %fusion.3 = bf16[1,512,7168]{2,1,0:T(8,128)(2,1)} fusion(f32[512,7168]{1,0:T(8,128)} %fusion.38, f32[512,7168]{1,0:T(8,128)} %fusion.52, bf16[8,56,8,8,128]{4,3,2,1,0:T(8,128)(2,1)} %bitcast.113, pred[]{:T(512)S(6)} %ge.6, s32[8,64]{1,0:T(8,128)S(1)} %copy.24), kind=kOutput, calls=%fused_computation.4 | convolution fusion | flops 3773038592 | bytes 44042240 | tf_op jit(solution)/shard_map/rck,ctkl->rtl/dot_general | solution.py:543
  262.8 0.6 reduce_sum.9
  263.5 5.8 %all-to-all-start.1 = ((f32[16,4,128]{2,1,0:T(4,128)}), f32[16,4,128]{2,1,0:T(4,128)S(1)}, u32[]{:S(2)}, u32[]{:S(2)}) async-start(f32[16,4,128]{2,1,0:T(4,128)} %bitcast.31), calls=%async_computation.1 | async-start | bytes 65536 | tf_op jit(solution)/shard_map/all_to_all | solution.py:568
  269.3 1.5 maximum_bitcast_fusion
  270.8 2.9 %copy.30 = f32[1,512,1024]{2,1,0:T(8,128)} copy(f32[1,512,1024]{1,2,0:T(8,128)} %maximum_bitcast_fusion) | data formatting | bytes 4194304
  273.7 2.1 all-to-all-done.1
  275.8 0.6 copy.43
  (20 shorter events, 0.1 us)
Async XLA Ops:
  42.8 2.0 copy-start
  44.8 1.0 copy-start.9
  44.8 3.6 %copy-start.1 = (f32[512,1024]{1,0:T(8,128)S(1)}, f32[512,1024]{1,0:T(8,128)}, u32[]{:S(2)}) copy-start(f32[512,1024]{1,0:T(8,128)} %copy-done) | copy-start | bytes 6291460
  44.8 3.6 %copy-start.2 = (bf16[56,16,4,128]{3,2,1,0:T(4,128)(2,1)S(1)}, bf16[56,16,4,128]{3,2,1,0:T(4,128)(2,1)}, u32[]{:S(2)}) copy-start(bf16[56,16,4,128]{3,2,1,0:T(4,128)(2,1)} %get-tuple-element.14.refs_3_) | copy-start | bytes 2752516
  199.2 2.0 copy-start.11
  207.7 0.7 copy-start.10
  209.8 53.1 %all-to-all-start = ((f32[8,64,128]{2,1,0:T(8,128)}), f32[8,64,128]{2,1,0:T(8,128)S(1)}, u32[]{:S(2)}, u32[]{:S(2)}) async-start(f32[8,64,128]{2,1,0:T(8,128)} %bitcast.106), calls=%async_computation | async-start | bytes 524288 | tf_op jit(solution)/shard_map/all_to_all | solution.py:566
  221.0 2.6 copy-start.7
  221.0 1.6 copy-start.3
  222.6 1.0 copy-start.5
  224.7 6.3 %copy-start.6 = (f32[512,512]{1,0:T(8,128)S(1)}, f32[512,512]{1,0:T(8,128)}, u32[]{:S(2)}) copy-start(f32[512,512]{1,0:T(8,128)} %copy-done.5) | copy-start | bytes 3145732
  245.6 23.7 %copy-start.4 = (f32[512,512]{0,1:T(8,128)S(1)}, f32[512,512]{0,1:T(8,128)}, u32[]{:S(2)}) copy-start(f32[512,512]{0,1:T(8,128)} %fusion.20) | copy-start | bytes 3145732
  245.6 23.7 %copy-start.8 = (f32[512,512]{0,1:T(8,128)S(1)}, f32[512,512]{0,1:T(8,128)}, u32[]{:S(2)}) copy-start(f32[512,512]{0,1:T(8,128)} %copy-done.7) | copy-start | bytes 3145732
  263.5 12.3 %all-to-all-start.1 = ((f32[16,4,128]{2,1,0:T(4,128)}), f32[16,4,128]{2,1,0:T(4,128)S(1)}, u32[]{:S(2)}, u32[]{:S(2)}) async-start(f32[16,4,128]{2,1,0:T(4,128)} %bitcast.31), calls=%async_computation.1 | async-start | bytes 65536 | tf_op jit(solution)/shard_map/all_to_all | solution.py:568

commit v3 on v2

--- a/solution.py
+++ b/solution.py
@@ -87,8 +87,8 @@
 
 
 def exchange_kernel(
-    counts, rows, slots, early, late, table, send_a, recv_a, send_b, recv_b, send_s, recv_s,
-    front_send, front_recv, front_send_s, front_recv_s, local_sem
+    counts, rows, slots, early, late, table, own_table, send_a, recv_a, send_b, recv_b, send_s, recv_s,
+    front_send, front_recv, front_send_s, front_recv_s, own_send, own_recv, local_sem
 ):
     panels, fronts = counts
     me = lax.axis_index("panel")
@@ -123,10 +123,26 @@
     def late_copy(shift):
         return to_panel(lambda p: rows.at[p, pl.ds(tiles, late.shape[0])], late.at[:, me], send_b, recv_b, shift)
 
+    lead = own_table.shape[1]
+
+    def own_copy(shift):
+        peer = lax.rem(front + shift, fronts)
+        return pltpu.make_async_remote_copy(
+            src_ref=slots.at[pl.ds(0, lead)],
+            dst_ref=own_table.at[front],
+            send_sem=own_send.at[shift],
+            recv_sem=own_recv.at[shift],
+            device_id={"front": peer},
+            device_id_type=MESH,
+        )
+
     for shift in range(1, panels):
         slot_copy(shift).start()
         early_copy(shift).start()
+    for shift in range(1, fronts):
+        own_copy(shift).start()
     own = [
+        pltpu.make_async_copy(slots.at[pl.ds(0, lead)], own_table.at[front], local_sem.at[3]),
         pltpu.make_async_copy(rows.at[me, pl.ds(0, tiles)], early.at[front, :, me], local_sem.at[0]),
         pltpu.make_async_copy(slots.at[me], table.at[front, me], local_sem.at[1]),
         pltpu.make_async_copy(rows.at[me, pl.ds(tiles, late.shape[0])], late.at[:, me], local_sem.at[2]),
@@ -162,9 +178,10 @@
     for shift in range(1, fronts):
         to_front(table, front_send_s, front_recv_s, shift).wait()
         to_front(early, front_send, front_recv, shift).wait()
-
-
-def exchange_rows(panels, fronts, rows, slots, tiles):
+        own_copy(shift).wait()
+
+
+def exchange_rows(panels, fronts, lead, rows, slots, tiles):
     _, all_tiles, cap, lanes = rows.shape
     sem = pltpu.SemaphoreType.DMA
     return pl.pallas_call(
@@ -174,20 +191,80 @@
             jax.ShapeDtypeStruct((fronts, tiles, panels, cap, lanes), BF16),
             jax.ShapeDtypeStruct((all_tiles - tiles, panels, cap, lanes), BF16),
             jax.ShapeDtypeStruct((fronts, panels, cap, lanes), jnp.int32),
+            jax.ShapeDtypeStruct((fronts, lead, cap, lanes), jnp.int32),
         ),
         in_specs=[pl.BlockSpec(memory_space=pl.ANY)] * 2,
-        out_specs=[pl.BlockSpec(memory_space=pl.ANY)] * 3,
-        scratch_shapes=[sem((panels,))] * 6 + [sem((fronts,))] * 4 + [sem((3,))],
+        out_specs=[pl.BlockSpec(memory_space=pl.ANY)] * 4,
+        scratch_shapes=[sem((panels,))] * 6 + [sem((fronts,))] * 6 + [sem((4,))],
         compiler_params=pltpu.CompilerParams(collective_id=1, has_side_effects=True),
     )(rows, slots)
 
 
+def assembly_kernel(parents, table, own_table, early, piv_cols, known, columns, halves, onehot, pick, picked):
+    front = lax.axis_index("front")
+    fronts, _, each, lanes = early.shape
+    owners = [parents[child] == front for child in range(fronts)]
+
+    def masked(ref, size):
+        return jnp.concatenate(
+            [jnp.where(owners[c], ref[c * size : (c + 1) * size, :], -1) for c in range(fronts)], axis=0
+        )
+
+    kept = masked(table, each)
+    lane = lax.broadcasted_iota(jnp.int32, kept.shape, 1)
+    chosen = jnp.concatenate(
+        [(kept == lane + t * lanes).astype(F32) for t in range(known.shape[0] // lanes)], axis=1
+    )
+    small = chosen.astype(BF16)
+    onehot[...] = small
+    half = piv_cols.shape[1] // 2
+    for h in range(2):
+        tiles = half // lanes
+        rows = jnp.concatenate(
+            [early[:, h * tiles + t].reshape(fronts * each, lanes) for t in range(tiles)], axis=1
+        )
+        value = piv_cols[:, h * half : (h + 1) * half] + product(small, rows, 0, 0, None)
+        columns[:, h * half : (h + 1) * half] = value
+        halves[h] = value.astype(BF16)
+    picked[...] = product(chosen, known[...], 1, 0)
+    size = own_table.shape[0] // fronts
+    own = masked(own_table, size)
+    cap = size * K // piv_cols.shape[1]
+    where = lax.rem(lax.broadcasted_iota(jnp.int32, own.shape, 0), size) // cap
+    target = jnp.where(own >= 0, own + where * K, -1)
+    lane = lax.broadcasted_iota(jnp.int32, own.shape, 1)
+    for t in range(pick.shape[1] // lanes):
+        pick[:, t * lanes : (t + 1) * lanes] = (target == lane + t * lanes).astype(F32)
+
+
+def assemble(parents, table, own_table, early, piv_cols, known):
+    rows, pivots = piv_cols.shape
+    vmem = pl.BlockSpec(memory_space=pltpu.VMEM)
+    return pl.pallas_call(
+        assembly_kernel,
+        name="assemble",
+        out_shape=(
+            jax.ShapeDtypeStruct((rows, pivots), F32),
+            jax.ShapeDtypeStruct((2, rows, pivots // 2), BF16),
+            jax.ShapeDtypeStruct((table.shape[0], rows), BF16),
+            jax.ShapeDtypeStruct((own_table.shape[0], pivots), F32),
+            jax.ShapeDtypeStruct((table.shape[0], known.shape[1]), F32),
+        ),
+        in_specs=[pl.BlockSpec(memory_space=pltpu.SMEM)] + [vmem] * 5,
+        out_specs=[vmem] * 5,
+        compiler_params=pltpu.CompilerParams(vmem_limit_bytes=40 << 20),
+    )(parents, table, own_table, early, piv_cols, known)
+
+
 def panel_kernel(
-    counts, side, halves, columns, partial, late, blocks, inverses, factor10, sums, late_all,
+    counts, side, halves, columns, known, right_side, pick, picked, late,
+    blocks, late_all, factor, weights, front_values, child_values,
+    inverses, factor10, partial, sums, solved, chosen, chosen_in, from_fronts, onward, inward,
     top, chunk, pieces, work, base_work, base_out,
     scatter_send, scatter_recv, whole_send, whole_recv, half_send, half_recv,
     far_send, far_recv, farther_send, farther_recv,
-    piece_send, piece_recv, sum_send, sum_recv, late_send, late_recv, local_sem,
+    piece_send, piece_recv, sum_send, sum_recv, inward_send, inward_recv,
+    late_send, late_recv, over_send, over_recv, pick_send, pick_recv, local_sem,
 ):
     panels, fronts = counts
     me = lax.axis_index("panel")
@@ -260,71 +337,121 @@
 
     def whole(kind, half, way):
         u, v = spots[half]
-        target = place(half, u + (1 if way == 0 else -1), v)
-        return move(kind, half, me, None, target, whole_send, whole_recv, (kind, half, way))
+        step = 1 if way == 0 else -1
+        copy = move(kind, half, me, None, place(half, u + step, v), whole_send, whole_recv, (kind, half, way))
+        return kind, copy, me, place(half, u - step, v)
 
     def halved(kind, half, way):
         u, v = spots[half]
         step = 1 if way == 0 else -1
-        return move(
-            kind, half, place(half, u - step, v), way, place(half, u + step, v), half_send, half_recv, (kind, half, way)
-        )
+        who = place(half, u - step, v)
+        copy = move(kind, half, who, way, place(half, u + step, v), half_send, half_recv, (kind, half, way))
+        return kind, copy, who, place(half, u + 2, v)
 
     def far(kind, half, offset, way):
         u, v = spots[half]
-        target = place(half, u, v + (1 if way == 0 else -1))
-        return move(
-            kind, half, place(half, u + offset, v), None, target, far_send, far_recv, (kind, half, offset, way)
-        )
+        step = 1 if way == 0 else -1
+        who = place(half, u + offset, v)
+        copy = move(kind, half, who, None, place(half, u, v + step), far_send, far_recv, (kind, half, offset, way))
+        return kind, copy, who, place(half, u + offset, v - step)
 
     def farther(kind, half, offset, way):
         u, v = spots[half]
         step = 1 if way == 0 else -1
-        return move(
-            kind, half, place(half, u + offset, v - step), way, place(half, u, v + step),
-            farther_send, farther_recv, (kind, half, offset, way),
-        )
+        who = place(half, u + offset, v - step)
+        copy = move(
+            kind, half, who, way, place(half, u, v + step), farther_send, farther_recv, (kind, half, offset, way)
+        )
+        return kind, copy, who, place(half, u + offset, v + 2)
+
+    def guarded(kind, who, act):
+        if kind == 0:
+            act()
+        else:
+            pl.when(who >= 2)(act)
+
+    def start(hop):
+        guarded(hop[0], hop[2], hop[1].start)
+
+    def sent(hop):
+        guarded(hop[0], hop[2], hop[1].wait_send)
+
+    def arrived(hop):
+        guarded(hop[0], hop[3], hop[1].wait_recv)
 
     both = [(half, way) for half in range(2) for way in range(2)]
 
     def begin(kind):
         for half, way in both:
-            whole(kind, half, way).start()
+            start(whole(kind, half, way))
         for half, way in both:
-            far(kind, half, 0, way).start()
+            start(far(kind, half, 0, way))
 
     def second(kind):
         for half, way in both:
-            whole(kind, half, way).wait_recv()
-            halved(kind, half, way).start()
+            arrived(whole(kind, half, way))
+            start(halved(kind, half, way))
         for half, way in both:
-            far(kind, half, 1, way).start()
-            far(kind, half, 3, way).start()
+            start(far(kind, half, 1, way))
+            start(far(kind, half, 3, way))
 
     def third(kind):
         for half in range(2):
             for way in range(2):
-                halved(kind, half, way).wait_recv()
+                arrived(halved(kind, half, way))
             for way in range(2):
-                far(kind, half, 2, way).start()
+                start(far(kind, half, 2, way))
 
     def relay(kind, offset):
         for half, way in both:
-            far(kind, half, offset, way).wait_recv()
-            farther(kind, half, offset, way).start()
+            arrived(far(kind, half, offset, way))
+            start(farther(kind, half, offset, way))
 
     def finish(kind):
         for half, way in both:
             for offset in range(4):
-                farther(kind, half, offset, way).wait_recv()
+                arrived(farther(kind, half, offset, way))
 
     def drain(kind):
         for half, way in both:
-            whole(kind, half, way).wait_send()
-            halved(kind, half, way).wait_send()
+            sent(whole(kind, half, way))
+            sent(halved(kind, half, way))
             for offset in range(4):
-                far(kind, half, offset, way).wait_send()
-                farther(kind, half, offset, way).wait_send()
+                sent(far(kind, half, offset, way))
+                sent(farther(kind, half, offset, way))
+
+    def over_copy(shift):
+        peer = lax.rem(front + shift, fronts)
+        return pltpu.make_async_remote_copy(
+            src_ref=picked.at[peer],
+            dst_ref=from_fronts.at[front],
+            send_sem=over_send.at[shift],
+            recv_sem=over_recv.at[shift],
+            device_id={"front": peer},
+            device_id_type=MESH,
+        )
+
+    def inward_copy(shift):
+        peer = lax.rem(me + shift, panels)
+        return pltpu.make_async_remote_copy(
+            src_ref=onward.at[peer],
+            dst_ref=inward.at[me],
+            send_sem=inward_send.at[shift],
+            recv_sem=inward_recv.at[shift],
+            device_id={"panel": peer},
+            device_id_type=MESH,
+        )
+
+    def pick_copy(shift):
+        peer = lax.rem(front + shift, fronts)
+        return pltpu.make_async_remote_copy(
+            src_ref=chosen.at[peer],
+            dst_ref=chosen_in.at[front],
+            send_sem=pick_send.at[shift],
+            recv_sem=pick_recv.at[shift],
+            device_id={"front": peer},
+            device_id_type=MESH,
+        )
 
     def late_copy(shift):
         peer = lax.rem(front + shift, fronts)
@@ -361,13 +488,18 @@
 
     own = [
         pltpu.make_async_copy(halves, blocks.at[:, me], local_sem.at[3]),
-        pltpu.make_async_copy(partial.at[me], pieces.at[me], local_sem.at[4]),
+        pltpu.make_async_copy(picked.at[front], from_fronts.at[front], local_sem.at[4]),
         pltpu.make_async_copy(late, late_all.at[front], local_sem.at[5]),
     ]
     for copy in own:
         copy.start()
+    for shift in range(1, fronts):
+        over_copy(shift).start()
     for copy in own:
         copy.wait()
+    begin(1)
+    for shift in range(1, fronts):
+        late_copy(shift).start()
     for root, indices in roots:
         for index in indices:
 
@@ -381,11 +513,16 @@
 
     top[:, chunk_rows(me), :] = chunk[...]
     begin(0)
-    begin(1)
-    for shift in range(1, fronts):
-        late_copy(shift).start()
+    below = me >= 2
+    boundary = jnp.where(below, known[...], 0.0)
+    width = partial.shape[1]
+    for half in range(2):
+        value = product(columns[:, half * K : (half + 1) * K], boundary, 0, 0)
+        for piece in range(panels // 2):
+            partial[half * (panels // 2) + piece] = value[piece * width : (piece + 1) * width, :]
     for shift in range(1, panels):
         piece_copy(shift).start()
+    pieces[me] = partial[me]
     second(0)
     third(0)
     for offset in (0, 1, 3, 2):
@@ -419,6 +556,14 @@
         def _():
             third(1)
             relay(1, 0)
+            for shift in range(1, fronts):
+                over_copy(shift).wait_recv()
+            total = from_fronts[0]
+            for who in range(1, fronts):
+                total = total + from_fronts[who]
+            onward[...] = total
+            for shift in range(1, panels):
+                inward_copy(shift).start()
 
         @pl.when(index == 2)
         def _():
@@ -436,19 +581,67 @@
             relay(1, 1)
             relay(1, 3)
 
-        @pl.when(index == 6)
+        @pl.when(index == 5)
         def _():
             relay(1, 2)
 
         return carry
 
     lax.fori_loop(0, 2 * (K // NB), block_step, 0)
+
+    for shift in range(1, panels):
+        sum_copy(shift).wait_recv()
+    inverse0, inverse1, lower = inverses[0], inverses[1], factor10[...]
+    count = panels // 2
+    sums0 = jnp.concatenate([sums[piece] for piece in range(count)], axis=0)
+    sums1 = jnp.concatenate([sums[count + piece] for piece in range(count)], axis=0)
+    carried0 = product(inverse0, sums0, 1, 0)
+    carried1 = product(inverse1, sums1 - product(lower, carried0, 1, 0), 1, 0)
+    solved1 = product(inverse1, right_side[K:, :] - carried1, 0, 0)
+    solved0 = product(inverse0, right_side[0:K, :] - carried0 - product(lower, solved1, 0, 0), 0, 0)
+    solved[0:K, :] = solved0
+    solved[K:, :] = solved1
+    values = product(pick[...], solved[...], 1, 0)
+    size = chosen.shape[1]
+    for child in range(fronts):
+        chosen[child] = values[child * size : (child + 1) * size, :]
+    for shift in range(1, fronts):
+        pick_copy(shift).start()
+    chosen_in[front] = chosen[front]
+    front_values[...] = jnp.where(below, known[...], jnp.where(me == 0, solved0, solved1))
+
+    factor0 = product(columns[:, 0:K], inverse0, 1, 1)
+    current = columns[:, K:] - product(factor0.astype(BF16), lower.astype(BF16), 1, 1, None)
+    factor1 = jnp.where(me >= 1, product(current, inverse1, 1, 1), 0.0)
+    factor[:, 0:K] = factor0
+    factor[:, K:] = factor1
+    weight1 = product(factor1, inverse1, 1, 0)
+    weight0 = product(factor0 - product(weight1, lower, 1, 0), inverse0, 1, 0)
+    weights[0] = weight0.astype(BF16)
+    weights[1] = weight1.astype(BF16)
+
+    for shift in range(1, panels):
+        inward_copy(shift).wait_recv()
+    child_values[...] = inward[...]
+    child_values[me] = onward[me]
+    for shift in range(1, fronts):
+        pick_copy(shift).wait_recv()
+    total = chosen_in[0]
+    for who in range(1, fronts):
+        total = total + chosen_in[who]
+    cap = child_values.shape[1]
+    for lead in range(size // cap):
+        child_values[lead] = total[lead * cap : (lead + 1) * cap, :]
     finish(1)
     drain(0)
     drain(1)
     for shift in range(1, panels):
         piece_copy(shift).wait_send()
-        sum_copy(shift).wait()
+        sum_copy(shift).wait_send()
+        inward_copy(shift).wait_send()
+    for shift in range(1, fronts):
+        over_copy(shift).wait_send()
+        pick_copy(shift).wait_send()
     for shift in range(1, fronts):
         late_copy(shift).wait()
     for root, indices in roots:
@@ -460,113 +653,145 @@
                     scatter(shift, index).wait_send()
 
 
-def panel_step(panels, fronts, side, halves, columns, partial, late):
+def panel_step(sizes, halves, columns, known, right_side, pick, picked, late):
+    panels, fronts, side = sizes
     sem = pltpu.SemaphoreType.DMA
     part = K // panels
+    rows, pivots = columns.shape
+    rhs = known.shape[1]
+    cap = picked.shape[2]
     anywhere = pl.BlockSpec(memory_space=pl.ANY)
     vmem = pl.BlockSpec(memory_space=pltpu.VMEM)
+    wide = pltpu.VMEM((panels, pivots // panels, rhs), F32)
+    few = pltpu.VMEM((fronts, pick.shape[0] // fronts, rhs), F32)
+    slot = pltpu.VMEM((panels, cap, rhs), F32)
+    square = pltpu.VMEM((K, K), F32)
+    tile = pltpu.VMEM((NB, NB), F32)
     return pl.pallas_call(
         lambda *refs: panel_kernel((panels, fronts), side, *refs),
         name="panel_step",
         out_shape=(
             jax.ShapeDtypeStruct((2, panels, K, K), BF16),
-            jax.ShapeDtypeStruct((2, K, K), F32),
-            jax.ShapeDtypeStruct((K, K), F32),
-            jax.ShapeDtypeStruct(partial.shape, F32),
             jax.ShapeDtypeStruct((fronts,) + late.shape, BF16),
+            jax.ShapeDtypeStruct((rows, pivots), F32),
+            jax.ShapeDtypeStruct((2, K, K), BF16),
+            jax.ShapeDtypeStruct((rows, rhs), F32),
+            jax.ShapeDtypeStruct((panels, cap, rhs), F32),
         ),
-        in_specs=[anywhere] * 4,
-        out_specs=[anywhere, vmem, vmem, vmem, anywhere],
+        in_specs=[anywhere] + [vmem] * 5 + [anywhere],
+        out_specs=[anywhere] * 2 + [vmem] * 4,
         scratch_shapes=[
+            pltpu.VMEM((2, K, K), F32),
+            square,
+            wide,
+            wide,
+            pltpu.VMEM((pivots, rhs), F32),
+            few,
+            few,
+            pltpu.VMEM((fronts, panels, cap, rhs), F32),
+            slot,
+            slot,
             pltpu.VMEM((3, K, K), F32),
             pltpu.VMEM((3, part, K), F32),
-            pltpu.VMEM(partial.shape, F32),
-            pltpu.VMEM((K, K), F32),
-            pltpu.VMEM((NB, NB), F32),
-            pltpu.VMEM((NB, NB), F32),
+            wide,
+            square,
+            tile,
+            tile,
             sem((3, panels)),
             sem((3,)),
         ]
         + [sem((2, 2, 2))] * 4
         + [sem((2, 2, 4, 2))] * 4
-        + [sem((panels,))] * 4
-        + [sem((fronts,))] * 2
+        + [sem((panels,))] * 6
+        + [sem((fronts,))] * 6
         + [sem((6,))],
         compiler_params=pltpu.CompilerParams(
-            collective_id=2, has_side_effects=True, vmem_limit_bytes=40 << 20
+            collective_id=2, has_side_effects=True, vmem_limit_bytes=50 << 20
         ),
-    )(halves, columns, partial, late)
+    )(halves, columns, known, right_side, pick, picked, late)
+
+
+def update_kernel(late, blocks, weights, onehot, factor, front_values, child_values, update, *rest):
+    outs, sem = rest[:3], rest[3]
+    step = pl.program_id(0)
+    results = (factor, front_values, child_values)
+
+    @pl.when(step == 0)
+    def _():
+        for i in range(3):
+            pltpu.make_async_copy(results[i], outs[i], sem.at[i]).start()
+
+    fronts, tiles, each, lanes = late.shape
+    rows = jnp.concatenate([late[:, t].reshape(fronts * each, lanes) for t in range(tiles)], axis=1)
+    value = product(onehot[...], rows, 0, 0, None)
+    for half in range(2):
+        value = value - product(weights[half], blocks[half, 0], 1, 1, None)
+    update[...] = jnp.where(lax.axis_index("panel") >= 2, value, 0.0).astype(BF16)
+
+    @pl.when(step == pl.num_programs(0) - 1)
+    def _():
+        for i in range(3):
+            pltpu.make_async_copy(results[i], outs[i], sem.at[i]).wait()
+
+
+def update_step(late_all, blocks, weights, onehot, factor, front_values, child_values):
+    fronts, all_tiles, each, lanes = late_all.shape
+    tiles = K // lanes
+    steps = all_tiles // tiles
+    first = blocks.shape[1] - steps
+    rows = weights.shape[1]
+    anywhere = pl.BlockSpec(memory_space=pl.ANY)
+    fixed = pl.BlockSpec(memory_space=pltpu.VMEM)
+    like = [jax.ShapeDtypeStruct(x.shape, x.dtype) for x in (factor, front_values, child_values)]
+    return pl.pallas_call(
+        update_kernel,
+        name="update",
+        grid=(steps,),
+        out_shape=[jax.ShapeDtypeStruct((rows, steps * K), BF16)] + like,
+        in_specs=[
+            pl.BlockSpec((fronts, tiles, each, lanes), lambda j: (0, j, 0, 0)),
+            pl.BlockSpec((2, 1, K, K), lambda j: (0, j + first, 0, 0)),
+            fixed,
+            fixed,
+            anywhere,
+            anywhere,
+            anywhere,
+        ],
+        out_specs=[pl.BlockSpec((rows, K), lambda j: (0, j))] + [anywhere] * 3,
+        scratch_shapes=[pltpu.SemaphoreType.DMA((3,))],
+        compiler_params=pltpu.CompilerParams(vmem_limit_bytes=40 << 20),
+    )(late_all, blocks, weights, onehot, factor, front_values, child_values)
 
 
 def on_device(sizes, pivot_columns, child_rows, slot_rows, parents, pivot_rhs, boundary_solution):
-    panels, fronts, side = sizes
-    panel_index = lax.axis_index("panel")
-    front_index = lax.axis_index("front")
+    panels, fronts, _ = sizes
     piv_cols = pivot_columns[0]
-    row_count, pivots = piv_cols.shape
+    pivots = piv_cols.shape[1]
     rows_out = child_rows[0, 0]
     cap, width = rows_out.shape[1:]
     lanes = NB
-    local_ids = jnp.arange(row_count, dtype=jnp.int32)
+    lead = pivots // K
+    each = panels * cap
+    known = boundary_solution[0]
 
     rows_tiled = rows_out.reshape(panels, cap, width // lanes, lanes).transpose(0, 2, 1, 3)
     slots_wide = jnp.broadcast_to(slot_rows[0, 0][:, :, None], (panels, cap, lanes))
-    early, late, table = exchange_rows(panels, fronts, rows_tiled, slots_wide, pivots // lanes)
-    slots = table[:, :, :, 0].reshape(fronts, panels * cap)
-    keeping = parents == front_index
-    kept = jnp.where(keeping[:, None], slots, -1).reshape(-1)
-    onehot = (kept[None, :] == local_ids[:, None]).astype(BF16)
-    early = early.reshape(fronts, pivots // lanes, panels * cap, lanes)
-    spread = jnp.einsum(
-        "rck,ctkl->rtl", onehot.reshape(row_count, fronts, panels * cap), early, preferred_element_type=F32
+    early, late, table, own_table = exchange_rows(panels, fronts, lead, rows_tiled, slots_wide, pivots // lanes)
+    columns, halves, onehot, pick, picked = assemble(
+        parents,
+        table.reshape(fronts * each, lanes),
+        own_table.reshape(fronts * lead * cap, lanes),
+        early.reshape(fronts, pivots // lanes, each, lanes),
+        piv_cols,
+        known,
     )
-    columns = piv_cols + spread.reshape(row_count, pivots)
-    known = boundary_solution[0]
-    below = panel_index >= pivots // row_count
-    halves = jnp.stack([columns[:, :K], columns[:, K:]]).astype(BF16)
-    partial = product(columns, jnp.where(below, known, 0.0), 0, 0, HIGH)
-    partial = partial.reshape(panels, pivots // panels, -1)
-
-    blocks, inverses, factor10, sums, late_all = panel_step(
-        panels, fronts, side, halves, columns, partial, late
+    blocks, late_all, factor, weights, front_values, child_values = panel_step(
+        sizes, halves, columns, known, pivot_rhs[0], pick, picked.reshape(fronts, panels, cap, -1), late
     )
-    inverse0, inverse1 = inverses[0], inverses[1]
-    packed10 = factor10.astype(BF16)
-
-    factor0 = product(columns[:, :K], inverse0, 1, 1, HIGH)
-    current = columns[:, K:] - product(factor0.astype(BF16), packed10, 1, 1, None)
-    factor1 = jnp.where(panel_index >= 1, product(current, inverse1, 1, 1, HIGH), 0.0)
-    weight1 = product(factor1, inverse1, 1, 0, HIGH)
-    weight0 = product(factor0 - product(weight1, factor10, 1, 0, HIGH), inverse0, 1, 0, HIGH)
-    factor_all = jnp.concatenate([factor0, factor1], axis=1)
-    first = pivots // K
-    trailing = jnp.einsum(
-        "rck,ctkl->rtl",
-        onehot.reshape(row_count, fronts, panels * cap),
-        late_all.reshape(fronts, -1, panels * cap, lanes),
-        preferred_element_type=F32,
-    ).reshape(row_count, -1)
-    gathered = blocks[:, first:].reshape(2, -1, K)
-    trailing = trailing - product(weight0.astype(BF16), gathered[0], 1, 1, None)
-    trailing = trailing - product(weight1.astype(BF16), gathered[1], 1, 1, None)
-    update_matrix = jnp.where(below, trailing, 0.0).astype(BF16)
-
-    sums = sums.reshape(pivots, -1)
-    sums0, sums1 = sums[:K], sums[K:]
-    right_side = pivot_rhs[0]
-    half = product(inverse0, sums0, 1, 0)
-    carried1 = product(inverse1, sums1 - product(factor10, half, 1, 0), 1, 0)
-    solved1 = product(inverse1, right_side[K:] - carried1, 0, 0)
-    carried0 = half + product(factor10, solved1, 0, 0)
-    solved0 = product(inverse0, right_side[:K] - carried0, 0, 0)
-    front_values = jnp.where(below, known, jnp.where(panel_index == 0, solved0, solved1))
-
-    pick = (kept[:, None] == local_ids[None, :]).astype(F32)
-    picked = product(pick, front_values, 1, 0).reshape(fronts, panels * cap, -1)
-    picked = jnp.sum(lax.all_to_all(picked, "front", split_axis=0, concat_axis=0, tiled=True), axis=0)
-    picked = picked.reshape(panels, cap, -1)
-    child_values = lax.all_to_all(picked, "panel", split_axis=0, concat_axis=0, tiled=True)
-    return (factor_all[None], update_matrix[None], front_values[None], child_values[None, None])
+    update_matrix, factor, front_values, child_values = update_step(
+        late_all.reshape(fronts, -1, each, lanes), blocks, weights, onehot, factor, front_values, child_values
+    )
+    return (factor[None], update_matrix[None], front_values[None], child_values[None, None])
 
 
 def solution(mesh):

time: 282 us -> 243 us (0.86); the launches traced: 277 us -> 242 us
  matrix products: 56.3 us -> 0 us
  Pallas kernels: 184 us -> 227 us
  starting transfers between devices: 10.7 us -> 0 us
  local copies, waits for them, and re-layouts: 19.3 us -> 14.5 us
  other arithmetic: 2.91 us -> 0 us
    dot_general x18 -> x0, matrix products: 56.3 us -> none  [the longest x16 36.3 us: product(): lax.dot_general(left, right, dims, precision=precision, preferred_element...]
    pallas_call x0 -> x2, Pallas kernels: none -> 21.4 us  [the longest x1 19.1 us: update_step(): pl.pallas_call(update_kernel, name='update', grid=(steps,), out_shape=[ja...]
    pallas_call x1, Pallas kernels: 151 us -> 172 us  [panel_step(): pl.pallas_call(lambda *refs: panel_kernel((panels, fronts), side, *refs),...]
    all_to_all x2 -> x0, starting transfers between devices: 10.7 us -> none  [the longest x1 5.81 us: on_device(): lax.all_to_all(picked, 'panel', split_axis=0, concat_axis=0, tiled=True)]
    slice x4 -> x0, local copies, waits for them, and re-layouts: 9.94 us -> none  [the longest x1 6.24 us: on_device(): trailing = trailing - product(weight0.astype(BF16), gathered[0], 1, 1, None)]
    unnamed x26, local copies, waits for them, and re-layouts: 5.64 us -> 13.1 us
  transfers between devices with their start and end apart: 2 -> 0, of which waited for: 1 -> 0; matrix products, arithmetic and copies ran while one was open for 19% -> 0% of each run, Pallas kernels for 0% -> 0%
where the time goes in v3:
time: 243 us; the launch traced here: 242 us
  Pallas kernels  227 us (93%)
  local copies, waits for them, and re-layouts  14.5 us (6%)
    pallas_call x1, Pallas kernels, panel_step(): pl.pallas_call(lambda *refs: panel_kernel((panels, fronts), side, *refs),...  172 us
    pallas_call x1, Pallas kernels, exchange_rows(): pl.pallas_call(lambda *refs: exchange_kernel((panels, fronts), *refs), na...  33.4 us
    pallas_call x1, Pallas kernels, update_step(): pl.pallas_call(update_kernel, name='update', grid=(steps,), out_shape=[ja...  19.1 us
    unnamed x26, local copies, waits for them, and re-layouts  13.1 us

profile of v3, /device:TPU:1, one launch (start us, length us, event | category | flops | bytes accessed | tf_op | source)
XLA Modules:
  0.0 242.1 jit_solution(463876348584922124)
XLA Ops:
  0.6 0.8 copy.10
  1.4 0.7 broadcast_in_dim.20.refs_1_
  2.1 0.0 copy-start.7
  2.1 0.0 copy-start.9
  2.1 33.4 %exchange.1 = (bf16[8,8,16,4,128]{4,3,2,1,0:T(4,128)(2,1)}, bf16[56,16,4,128]{3,2,1,0:T(4,128)(2,1)}, s32[8,16,4,128]{3,2,1,0:T(4,128)}, s32[8,2,4,128]{3,2,1,0:T(4,128)}) custom-call(bf16[16,64,4,128]{3,2,1,0:T(4,128)(2,1)} %bitcast.25, s32[16,4,128]{2,1,0:T(4,128)} %broadcast_in_dim.20.refs_1_), custom_call_target="tpu_custom_call" | custom-call | tf_op jit(solution)/shard_map/exchange/pallas_call | solution.py:187
  35.5 0.0 copy-start.1
  35.5 1.6 copy-done.1
  37.1 0.0 copy-start.5
  37.1 1.2 copy-done.5
  38.3 0.0 copy-start.6
  38.3 0.9 copy-done.6
  39.3 0.0 copy-start.10
  39.3 0.9 copy-done.10
  40.2 0.0 copy-start.11
  40.2 0.8 copy-done.11
  41.0 0.0 copy-start.12
  41.0 0.7 copy-done.12
  41.6 0.0 copy-start.8
  41.6 2.2 assemble.1
  43.9 0.0 copy-start.2
  43.9 1.3 copy-done.2
  45.2 0.0 copy-start.4
  45.2 1.0 copy-done.4
  46.2 0.0 copy-done.7
  46.2 0.0 copy-done.9
  46.2 0.0 copy-done.8
  46.2 171.9 %panel_step.1 = (bf16[2,16,512,512]{3,2,1,0:T(8,128)(2,1)}, bf16[8,56,16,4,128]{4,3,2,1,0:T(4,128)(2,1)}, f32[512,1024]{1,0:T(8,128)}, bf16[2,512,512]{2,1,0:T(8...) custom-call(bf16[2,512,512]{2,1,0:T(8,128)(2,1)} %copy-done.4, f32[512,1024]{1,0:T(8,128)} %copy-done.2, ...), custom_call_target="tpu_custom_call" | custom-call | tf_op jit(solution)/shard_map/panel_step/pallas_call | solution.py:670
  218.1 0.0 copy-start
  218.1 3.1 %copy-done = bf16[8,56,16,4,128]{4,3,2,1,0:T(4,128)(2,1)S(1)} copy-done((bf16[8,56,16,4,128]{4,3,2,1,0:T(4,128)(2,1)S(1)}, bf16[8,56,16,4,128]{4,3,2,1,0:T(4,128)(2,1)}, u32[]{:S(2)}) %copy-start) | copy-done | bytes 7340056
  221.2 0.0 copy-start.3
  221.2 1.6 copy-done.3
  222.8 19.1 %update.1 = (bf16[512,7168]{1,0:T(8,128)(2,1)}, f32[512,1024]{1,0:T(8,128)}, f32[512,128]{1,0:T(8,128)}, f32[16,4,128]{2,1,0:T(4,128)}) custom-call(bf16[8,56,64,128]{3,2,1,0:T(8,128)(2,1)S(1)} %bitcast.16, bf16[2,16,512,512]{3,2,1,0:T(8,128)(2,1)} %get-tuple-element.32.blocks, bf16[2,512,512]{2,1,0:T(8,128)(2,1)S(1)} %get-tuple-element.33.weights, ...), custom_call_target="tpu_custom_call" | custom-call | tf_op jit(solution)/shard_map/update/pallas_call | solution.py:746
Async XLA Ops:
  2.1 44.1 %copy-start.7 = (f32[1,512,128]{2,1,0:T(8,128)S(1)}, f32[1,512,128]{2,1,0:T(8,128)}, u32[]{:S(2)}) copy-start(f32[1,512,128]{2,1,0:T(8,128)} %param.11) | copy-start | bytes 786436
  2.1 44.1 %copy-start.9 = (f32[1,1024,128]{2,1,0:T(8,128)S(1)}, f32[1,1024,128]{2,1,0:T(8,128)}, u32[]{:S(2)}) copy-start(f32[1,1024,128]{2,1,0:T(8,128)} %param.10) | copy-start | bytes 1572868
  35.5 1.6 copy-start.1
  37.1 1.2 copy-start.5
  38.3 0.9 copy-start.6
  39.3 0.9 copy-start.10
  40.2 0.8 copy-start.11
  41.0 0.7 copy-start.12
  41.6 4.5 %copy-start.8 = (bf16[56,16,4,128]{3,2,1,0:T(4,128)(2,1)S(1)}, bf16[56,16,4,128]{3,2,1,0:T(4,128)(2,1)}, u32[]{:S(2)}) copy-start(bf16[56,16,4,128]{3,2,1,0:T(4,128)(2,1)} %get-tuple-element.30.refs_6_) | copy-start | bytes 2752516
  43.9 1.3 copy-start.2
  45.2 1.0 copy-start.4
  218.1 3.1 %copy-start = (bf16[8,56,16,4,128]{4,3,2,1,0:T(4,128)(2,1)S(1)}, bf16[8,56,16,4,128]{4,3,2,1,0:T(4,128)(2,1)}, u32[]{:S(2)}) copy-start(bf16[8,56,16,4,128]{4,3,2,1,0:T(4,128)(2,1)} %get-tuple-element.31) | copy-start | bytes 22020100
  221.2 1.6 copy-start.3

commit v4 on v3

--- a/solution.py
+++ b/solution.py
@@ -72,18 +72,21 @@
     return (block + block.T) * 0.5
 
 
-def factor_block(low, work, inverse, base_work, base_out):
+def factor_block(low, joined, staged, base_work, base_out):
     rows = pl.ds(low, NB)
-    base_work[...] = work[rows, rows]
+    high = low + NB
+    base_work[...] = joined[rows, rows]
     base_inverse(base_work, base_out)
     base = base_out[...]
-    upper = product(base, work[rows, :], 1, 0)
-    lane = lax.broadcasted_iota(jnp.int32, upper.shape, 1)
-    upper = jnp.where(lane >= low + NB, upper, 0.0)
-    solved = product(base, inverse[rows, :], 1, 0)
-    work[...] = work[...] - product(upper, upper, 0, 0)
-    inverse[...] = inverse[...] - product(upper, solved, 0, 0)
-    inverse[rows, :] = solved
+    solved = product(base, joined[rows, :], 1, 0)
+    lane = lax.broadcasted_iota(jnp.int32, solved.shape, 1)
+    upper = jnp.where(lane >= high, solved, 0.0)
+    staged[...] = solved
+    staged[:, rows] = base
+    strip = joined[:, rows]
+    joined[:, rows] = jnp.where(lax.broadcasted_iota(jnp.int32, strip.shape, 0) >= high, 0.0, strip)
+    joined[...] = joined[...] - product(upper, staged[...], 0, 0)
+    joined[rows, :] = jnp.where(lane < high, staged[...], 0.0)
 
 
 def exchange_kernel(
@@ -194,13 +197,13 @@
             jax.ShapeDtypeStruct((fronts, lead, cap, lanes), jnp.int32),
         ),
         in_specs=[pl.BlockSpec(memory_space=pl.ANY)] * 2,
-        out_specs=[pl.BlockSpec(memory_space=pl.ANY)] * 4,
+        out_specs=[pl.BlockSpec(memory_space=space) for space in (pltpu.VMEM, pl.ANY, pltpu.VMEM, pltpu.VMEM)],
         scratch_shapes=[sem((panels,))] * 6 + [sem((fronts,))] * 6 + [sem((4,))],
-        compiler_params=pltpu.CompilerParams(collective_id=1, has_side_effects=True),
+        compiler_params=pltpu.CompilerParams(collective_id=1, has_side_effects=True, vmem_limit_bytes=8 << 20),
     )(rows, slots)
 
 
-def assembly_kernel(parents, table, own_table, early, piv_cols, known, columns, halves, onehot, pick, picked):
+def assemble(parents, table, own_table, early, piv_cols, known, columns, halves, onehot, pick, picked):
     front = lax.axis_index("front")
     fronts, _, each, lanes = early.shape
     owners = [parents[child] == front for child in range(fronts)]
@@ -226,7 +229,9 @@
         value = piv_cols[:, h * half : (h + 1) * half] + product(small, rows, 0, 0, None)
         columns[:, h * half : (h + 1) * half] = value
         halves[h] = value.astype(BF16)
-    picked[...] = product(chosen, known[...], 1, 0)
+    found = product(chosen, known[...], 1, 0)
+    for child in range(fronts):
+        picked[child] = found[child * each : (child + 1) * each, :]
     size = own_table.shape[0] // fronts
     own = masked(own_table, size)
     cap = size * K // piv_cols.shape[1]
@@ -237,30 +242,12 @@
         pick[:, t * lanes : (t + 1) * lanes] = (target == lane + t * lanes).astype(F32)
 
 
-def assemble(parents, table, own_table, early, piv_cols, known):
-    rows, pivots = piv_cols.shape
-    vmem = pl.BlockSpec(memory_space=pltpu.VMEM)
-    return pl.pallas_call(
-        assembly_kernel,
-        name="assemble",
-        out_shape=(
-            jax.ShapeDtypeStruct((rows, pivots), F32),
-            jax.ShapeDtypeStruct((2, rows, pivots // 2), BF16),
-            jax.ShapeDtypeStruct((table.shape[0], rows), BF16),
-            jax.ShapeDtypeStruct((own_table.shape[0], pivots), F32),
-            jax.ShapeDtypeStruct((table.shape[0], known.shape[1]), F32),
-        ),
-        in_specs=[pl.BlockSpec(memory_space=pltpu.SMEM)] + [vmem] * 5,
-        out_specs=[vmem] * 5,
-        compiler_params=pltpu.CompilerParams(vmem_limit_bytes=40 << 20),
-    )(parents, table, own_table, early, piv_cols, known)
-
-
 def panel_kernel(
-    counts, side, halves, columns, known, right_side, pick, picked, late,
-    blocks, late_all, factor, weights, front_values, child_values,
+    counts, side, parents, table, own_table, early, piv_cols, known, right_side, late,
+    blocks, late_all, factor, weights, front_values, child_values, onehot,
+    columns, halves, pick, picked,
     inverses, factor10, partial, sums, solved, chosen, chosen_in, from_fronts, onward, inward,
-    top, chunk, pieces, work, base_work, base_out,
+    top, chunk, pieces, staged, base_work, base_out,
     scatter_send, scatter_recv, whole_send, whole_recv, half_send, half_recv,
     far_send, far_recv, farther_send, farther_recv,
     piece_send, piece_recv, sum_send, sum_recv, inward_send, inward_recv,
@@ -278,6 +265,15 @@
     for shift in range(1, fronts):
         peer = lax.rem(front + shift, fronts)
         pl.semaphore_signal(barrier, inc=1, device_id={"front": peer}, device_id_type=MESH)
+    assemble(parents, table, own_table, early, piv_cols, known, columns, halves, onehot, pick, picked)
+    below = me >= 2
+    boundary = jnp.where(below, known[...], 0.0)
+    width = partial.shape[1]
+    for half in range(2):
+        value = product(columns[:, half * K : (half + 1) * K], boundary, 0, 0, HIGH)
+        for piece in range(panels // 2):
+            partial[half * (panels // 2) + piece] = value[piece * width : (piece + 1) * width, :]
+    pieces[me] = partial[me]
     pl.semaphore_wait(barrier, panels + fronts - 2)
 
     def chunk_rows(who):
@@ -317,10 +313,10 @@
     spots = (across, along), (along, across)
 
     def view(kind, half, who, rows):
-        if kind == 0:
+        if kind != 1:
             size = part if rows is None else part // 2
             low = who * part + (part // 2 if rows == 1 else 0)
-            return top.at[:, pl.ds(pl.multiple_of(low, 8), size), pl.ds(half * (K // 2), K // 2)]
+            return top.at[pl.ds(kind // 2, kind // 2 + 1), pl.ds(pl.multiple_of(low, 8), size), pl.ds(half * (K // 2), K // 2)]
         ref = blocks.at[half, who]
         return ref if rows is None else ref.at[pl.ds(rows * (K // 2), K // 2)]
 
@@ -365,7 +361,7 @@
         return kind, copy, who, place(half, u + offset, v + 2)
 
     def guarded(kind, who, act):
-        if kind == 0:
+        if kind != 1:
             act()
         else:
             pl.when(who >= 2)(act)
@@ -381,9 +377,11 @@
 
     both = [(half, way) for half in range(2) for way in range(2)]
 
-    def begin(kind):
+    def near(kind):
         for half, way in both:
             start(whole(kind, half, way))
+
+    def own_far(kind):
         for half, way in both:
             start(far(kind, half, 0, way))
 
@@ -497,76 +495,85 @@
         over_copy(shift).start()
     for copy in own:
         copy.wait()
-    begin(1)
     for shift in range(1, fronts):
         late_copy(shift).start()
-    for root, indices in roots:
-        for index in indices:
-
-            @pl.when(me == root)
-            def _():
-                own_chunk(index).wait()
-
-            @pl.when(me != root)
-            def _():
-                scatter(1, index).wait_recv()
-
-    top[:, chunk_rows(me), :] = chunk[...]
-    begin(0)
-    below = me >= 2
-    boundary = jnp.where(below, known[...], 0.0)
-    width = partial.shape[1]
-    for half in range(2):
-        value = product(columns[:, half * K : (half + 1) * K], boundary, 0, 0)
-        for piece in range(panels // 2):
-            partial[half * (panels // 2) + piece] = value[piece * width : (piece + 1) * width, :]
     for shift in range(1, panels):
         piece_copy(shift).start()
-    pieces[me] = partial[me]
+
+    def own_rows(root, index):
+
+        @pl.when(me == root)
+        def _():
+            own_chunk(index).wait()
+
+        @pl.when(me != root)
+        def _():
+            scatter(1, index).wait_recv()
+
+        top[index, chunk_rows(me), :] = chunk[index]
+
+    own_rows(0, 0)
+    near(0)
+    own_far(0)
+    own_rows(1, 1)
+    own_rows(1, 2)
     second(0)
     third(0)
     for offset in (0, 1, 3, 2):
         relay(0, offset)
+    near(2)
+    own_far(2)
+    near(1)
     finish(0)
-    second(1)
-
-    lane = lax.broadcasted_iota(jnp.int32, (K, K), 1)
-    row = lax.broadcasted_iota(jnp.int32, (K, K), 0)
 
     def block_step(index, carry):
         which = index // (K // NB)
 
         @pl.when(index == 0)
         def _():
-            work[...] = symmetric_part(top[0])
-            inverses[0] = (lane == row).astype(F32)
+            inverses[0] = symmetric_part(top[0])
 
         @pl.when(index == K // NB)
         def _():
+            finish(2)
             lower = product(top[1], inverses[0], 1, 1)
             factor10[...] = lower
             packed = lower.astype(BF16)
-            work[...] = symmetric_part(top[2] - product(packed, packed, 1, 1, None))
-            inverses[1] = (lane == row).astype(F32)
+            inverses[1] = symmetric_part(top[2] - product(packed, packed, 1, 1, None))
 
         low = pl.multiple_of((index - which * (K // NB)) * NB, NB)
-        factor_block(low, work, inverses.at[which], base_work, base_out)
-
-        @pl.when(index == 1)
-        def _():
-            third(1)
-            relay(1, 0)
+        factor_block(low, inverses.at[which], staged, base_work, base_out)
+
+        @pl.when(index == 0)
+        def _():
+            second(2)
+
+        @pl.when(index == 2)
+        def _():
+            third(2)
+            for offset in (0, 1):
+                relay(2, offset)
+            second(1)
+            own_far(1)
+
+        @pl.when(index == 3)
+        def _():
+            relay(2, 3)
+            relay(2, 2)
             for shift in range(1, fronts):
                 over_copy(shift).wait_recv()
             total = from_fronts[0]
             for who in range(1, fronts):
                 total = total + from_fronts[who]
-            onward[...] = total
+            cap = onward.shape[1]
+            for who in range(panels):
+                onward[who] = total[who * cap : (who + 1) * cap, :]
             for shift in range(1, panels):
                 inward_copy(shift).start()
 
-        @pl.when(index == 2)
-        def _():
+        @pl.when(index == 4)
+        def _():
+            third(1)
             for shift in range(1, panels):
                 piece_copy(shift).wait_recv()
             total = pieces[0]
@@ -576,14 +583,9 @@
             for shift in range(1, panels):
                 sum_copy(shift).start()
 
-        @pl.when(index == 3)
-        def _():
-            relay(1, 1)
-            relay(1, 3)
-
-        @pl.when(index == 5)
-        def _():
-            relay(1, 2)
+        @pl.when(index == 6)
+        def _():
+            relay(1, 0)
 
         return carry
 
@@ -595,10 +597,10 @@
     count = panels // 2
     sums0 = jnp.concatenate([sums[piece] for piece in range(count)], axis=0)
     sums1 = jnp.concatenate([sums[count + piece] for piece in range(count)], axis=0)
-    carried0 = product(inverse0, sums0, 1, 0)
-    carried1 = product(inverse1, sums1 - product(lower, carried0, 1, 0), 1, 0)
-    solved1 = product(inverse1, right_side[K:, :] - carried1, 0, 0)
-    solved0 = product(inverse0, right_side[0:K, :] - carried0 - product(lower, solved1, 0, 0), 0, 0)
+    carried0 = product(inverse0, sums0, 1, 0, HIGH)
+    carried1 = product(inverse1, sums1 - product(lower, carried0, 1, 0, HIGH), 1, 0, HIGH)
+    solved1 = product(inverse1, right_side[K:, :] - carried1, 0, 0, HIGH)
+    solved0 = product(inverse0, right_side[0:K, :] - carried0 - product(lower, solved1, 0, 0, HIGH), 0, 0, HIGH)
     solved[0:K, :] = solved0
     solved[K:, :] = solved1
     values = product(pick[...], solved[...], 1, 0)
@@ -610,15 +612,18 @@
     chosen_in[front] = chosen[front]
     front_values[...] = jnp.where(below, known[...], jnp.where(me == 0, solved0, solved1))
 
-    factor0 = product(columns[:, 0:K], inverse0, 1, 1)
+    relay(1, 1)
+    factor0 = product(columns[:, 0:K], inverse0, 1, 1, HIGH)
     current = columns[:, K:] - product(factor0.astype(BF16), lower.astype(BF16), 1, 1, None)
-    factor1 = jnp.where(me >= 1, product(current, inverse1, 1, 1), 0.0)
+    factor1 = jnp.where(me >= 1, product(current, inverse1, 1, 1, HIGH), 0.0)
     factor[:, 0:K] = factor0
     factor[:, K:] = factor1
-    weight1 = product(factor1, inverse1, 1, 0)
-    weight0 = product(factor0 - product(weight1, lower, 1, 0), inverse0, 1, 0)
+    relay(1, 3)
+    weight1 = product(factor1, inverse1, 1, 0, HIGH)
+    weight0 = product(factor0 - product(weight1, lower, 1, 0, HIGH), inverse0, 1, 0, HIGH)
     weights[0] = weight0.astype(BF16)
     weights[1] = weight1.astype(BF16)
+    relay(1, 2)
 
     for shift in range(1, panels):
         inward_copy(shift).wait_recv()
@@ -633,8 +638,8 @@
     for lead in range(size // cap):
         child_values[lead] = total[lead * cap : (lead + 1) * cap, :]
     finish(1)
-    drain(0)
-    drain(1)
+    for kind in range(3):
+        drain(kind)
     for shift in range(1, panels):
         piece_copy(shift).wait_send()
         sum_copy(shift).wait_send()
@@ -653,17 +658,18 @@
                     scatter(shift, index).wait_send()
 
 
-def panel_step(sizes, halves, columns, known, right_side, pick, picked, late):
+def panel_step(sizes, parents, table, own_table, early, piv_cols, known, right_side, late):
     panels, fronts, side = sizes
     sem = pltpu.SemaphoreType.DMA
     part = K // panels
-    rows, pivots = columns.shape
+    rows, pivots = piv_cols.shape
     rhs = known.shape[1]
-    cap = picked.shape[2]
+    cap = early.shape[2] // panels
     anywhere = pl.BlockSpec(memory_space=pl.ANY)
     vmem = pl.BlockSpec(memory_space=pltpu.VMEM)
     wide = pltpu.VMEM((panels, pivots // panels, rhs), F32)
-    few = pltpu.VMEM((fronts, pick.shape[0] // fronts, rhs), F32)
+    few = pltpu.VMEM((fronts, own_table.shape[0] // fronts, rhs), F32)
+    over = pltpu.VMEM((fronts, panels * cap, rhs), F32)
     slot = pltpu.VMEM((panels, cap, rhs), F32)
     square = pltpu.VMEM((K, K), F32)
     tile = pltpu.VMEM((NB, NB), F32)
@@ -677,10 +683,15 @@
             jax.ShapeDtypeStruct((2, K, K), BF16),
             jax.ShapeDtypeStruct((rows, rhs), F32),
             jax.ShapeDtypeStruct((panels, cap, rhs), F32),
+            jax.ShapeDtypeStruct((table.shape[0], rows), BF16),
         ),
-        in_specs=[anywhere] + [vmem] * 5 + [anywhere],
-        out_specs=[anywhere] * 2 + [vmem] * 4,
+        in_specs=[pl.BlockSpec(memory_space=pltpu.SMEM)] + [vmem] * 6 + [anywhere],
+        out_specs=[anywhere] * 2 + [vmem] * 5,
         scratch_shapes=[
+            pltpu.VMEM((rows, pivots), F32),
+            pltpu.VMEM((2, rows, K), BF16),
+            pltpu.VMEM((own_table.shape[0], pivots), F32),
+            over,
             pltpu.VMEM((2, K, K), F32),
             square,
             wide,
@@ -688,27 +699,27 @@
             pltpu.VMEM((pivots, rhs), F32),
             few,
             few,
-            pltpu.VMEM((fronts, panels, cap, rhs), F32),
+            over,
             slot,
             slot,
             pltpu.VMEM((3, K, K), F32),
             pltpu.VMEM((3, part, K), F32),
             wide,
-            square,
+            pltpu.VMEM((NB, K), F32),
             tile,
             tile,
             sem((3, panels)),
             sem((3,)),
         ]
-        + [sem((2, 2, 2))] * 4
-        + [sem((2, 2, 4, 2))] * 4
+        + [sem((3, 2, 2))] * 4
+        + [sem((3, 2, 4, 2))] * 4
         + [sem((panels,))] * 6
         + [sem((fronts,))] * 6
         + [sem((6,))],
         compiler_params=pltpu.CompilerParams(
-            collective_id=2, has_side_effects=True, vmem_limit_bytes=50 << 20
+            collective_id=2, has_side_effects=True, vmem_limit_bytes=40 << 20
         ),
-    )(halves, columns, known, right_side, pick, picked, late)
+    )(parents, table, own_table, early, piv_cols, known, right_side, late)
 
 
 def update_kernel(late, blocks, weights, onehot, factor, front_values, child_values, update, *rest):
@@ -759,7 +770,7 @@
         ],
         out_specs=[pl.BlockSpec((rows, K), lambda j: (0, j))] + [anywhere] * 3,
         scratch_shapes=[pltpu.SemaphoreType.DMA((3,))],
-        compiler_params=pltpu.CompilerParams(vmem_limit_bytes=40 << 20),
+        compiler_params=pltpu.CompilerParams(vmem_limit_bytes=56 << 20),
     )(late_all, blocks, weights, onehot, factor, front_values, child_values)
 
 
@@ -777,16 +788,16 @@
     rows_tiled = rows_out.reshape(panels, cap, width // lanes, lanes).transpose(0, 2, 1, 3)
     slots_wide = jnp.broadcast_to(slot_rows[0, 0][:, :, None], (panels, cap, lanes))
     early, late, table, own_table = exchange_rows(panels, fronts, lead, rows_tiled, slots_wide, pivots // lanes)
-    columns, halves, onehot, pick, picked = assemble(
+    blocks, late_all, factor, weights, front_values, child_values, onehot = panel_step(
+        sizes,
         parents,
         table.reshape(fronts * each, lanes),
         own_table.reshape(fronts * lead * cap, lanes),
         early.reshape(fronts, pivots // lanes, each, lanes),
         piv_cols,
         known,
-    )
-    blocks, late_all, factor, weights, front_values, child_values = panel_step(
-        sizes, halves, columns, known, pivot_rhs[0], pick, picked.reshape(fronts, panels, cap, -1), late
+        pivot_rhs[0],
+        late,
     )
     update_matrix, factor, front_values, child_values = update_step(
         late_all.reshape(fronts, -1, each, lanes), blocks, weights, onehot, factor, front_values, child_values

time: 243 us -> 289 us (1.19)
  Pallas kernels: 227 us -> 275 us
  local copies, waits for them, and re-layouts: 14.5 us -> 10.8 us
    pallas_call x1, Pallas kernels: 19.1 us -> 76.2 us  [update_step(): pl.pallas_call(update_kernel, name='update', grid=(steps,), out_shape=[ja...]
    pallas_call x1, Pallas kernels: 172 us -> 166 us  [panel_step(): pl.pallas_call(lambda *refs: panel_kernel((panels, fronts), side, *refs),...]
    unnamed x26 -> x20, local copies, waits for them, and re-layouts: 13.1 us -> 9.94 us
where the time goes in v4:
time: 289 us; the launch traced here: 286 us
  Pallas kernels  275 us (95%)
  local copies, waits for them, and re-layouts  10.8 us (4%)
    pallas_call x1, Pallas kernels, panel_step(): pl.pallas_call(lambda *refs: panel_kernel((panels, fronts), side, *refs),...  166 us
    pallas_call x1, Pallas kernels, update_step(): pl.pallas_call(update_kernel, name='update', grid=(steps,), out_shape=[ja...  76.2 us
    pallas_call x1, Pallas kernels, exchange_rows(): pl.pallas_call(lambda *refs: exchange_kernel((panels, fronts), *refs), na...  32.8 us
    unnamed x20, local copies, waits for them, and re-layouts  9.94 us

profile of v4, /device:TPU:1, one launch (start us, length us, event | category | flops | bytes accessed | tf_op | source)
XLA Modules:
  0.0 286.1 jit_solution(7877115643352861787)
XLA Ops:
  0.6 0.8 copy.10
  1.4 0.1 broadcast_in_dim.20.refs_1_
  1.5 0.0 copy-start.2
  1.5 1.2 copy-done.2
  2.7 32.8 %exchange.1 = (bf16[8,8,16,4,128]{4,3,2,1,0:T(4,128)(2,1)S(1)}, bf16[56,16,4,128]{3,2,1,0:T(4,128)(2,1)S(1)}, s32[8,16,4,128]{3,2,1,0:T(4,128)S(1)}, s32[8,2,4,128]{3,2,1,0:T(4,128)S(1)}) custom-call(bf16[16,64,4,128]{3,2,1,0:T(4,128)(2,1)S(1)} %bitcast.16, s32[16,4,128]{2,1,0:T(4,128)S(1)} %broadcast_in_dim.20.refs_1_), custom_call_target="tpu_custom_call" | custom-call | tf_op jit(solution)/shard_map/exchange/pallas_call | solution.py:190
  35.5 0.0 copy-start
  35.5 1.6 copy-done
  37.1 0.0 copy-start.5
  37.1 1.0 copy-done.5
  38.1 0.0 copy-start.7
  38.1 0.9 copy-done.7
  39.1 0.0 copy-start.9
  39.1 0.7 copy-done.9
  39.7 165.5 %panel_step.1 = (bf16[2,16,512,512]{3,2,1,0:T(8,128)(2,1)}, bf16[8,56,16,4,128]{4,3,2,1,0:T(4,128)(2,1)}, f32[512,1024]{1,0:T(8,128)S(1)}, bf16[2,512,512]{2,1,0...) custom-call(s32[8]{0:T(128)S(1)} %copy-done.9, ...), custom_call_target="tpu_custom_call" | custom-call | tf_op jit(solution)/shard_map/panel_step/pallas_call | solution.py:676
  205.2 0.0 copy-start.1
  205.3 1.4 copy-done.1
  206.6 0.0 copy-start.3
  206.6 1.0 copy-done.3
  207.6 0.0 copy-start.4
  207.6 0.8 copy-done.4
  208.4 0.0 copy-start.6
  208.4 0.7 copy-done.6
  209.1 0.0 copy-start.8
  209.1 0.6 copy-done.8
  209.7 76.2 %update.1 = (bf16[512,7168]{1,0:T(8,128)(2,1)}, f32[512,1024]{1,0:T(8,128)}, f32[512,128]{1,0:T(8,128)}, f32[16,4,128]{2,1,0:T(4,128)}) custom-call(bf16[8,56,64,128]{3,2,1,0:T(8,128)(2,1)} %bitcast.22, bf16[2,16,512,512]{3,2,1,0:T(8,128)(2,1)} %get-tuple-element.24.blocks, bf16[2,512,512]{2,1,0:T(8,128)(2,1)} %copy-done.3, bf16[512,512]{1,0:T(8,128)(2,1)} %copy-done.4, ...), custom_call_target="tpu_custom_call" | custom-call | tf_op jit(solution)/shard_map/update/pallas_call | solution.py:757
Async XLA Ops:
  1.5 1.2 copy-start.2
  35.5 1.6 copy-start
  37.1 1.0 copy-start.5
  38.1 0.9 copy-start.7
  39.1 0.7 copy-start.9
  205.2 1.4 copy-start.1
  206.6 1.0 copy-start.3
  207.6 0.8 copy-start.4
  208.4 0.7 copy-start.6
  209.1 0.6 copy-start.8

commit v5 on v4

--- a/solution.py
+++ b/solution.py
@@ -306,17 +306,18 @@
             for index in indices:
                 own_chunk(index).start()
 
+    coords = [[lax.rem(at + step, side) for step in range(side)] for at in (across, along)]
+
     def place(half, first, second):
-        first, second = lax.rem(first + side, side), lax.rem(second + side, side)
+        near_axis, far_axis = (coords[0], coords[1]) if half == 0 else (coords[1], coords[0])
+        first, second = near_axis[first % side], far_axis[second % side]
         return first * side + second if half == 0 else second * side + first
 
-    spots = (across, along), (along, across)
-
     def view(kind, half, who, rows):
-        if kind != 1:
+        if kind == 0:
             size = part if rows is None else part // 2
             low = who * part + (part // 2 if rows == 1 else 0)
-            return top.at[pl.ds(kind // 2, kind // 2 + 1), pl.ds(pl.multiple_of(low, 8), size), pl.ds(half * (K // 2), K // 2)]
+            return top.at[:, pl.ds(pl.multiple_of(low, 8), size), pl.ds(half * (K // 2), K // 2)]
         ref = blocks.at[half, who]
         return ref if rows is None else ref.at[pl.ds(rows * (K // 2), K // 2)]
 
@@ -332,36 +333,32 @@
         )
 
     def whole(kind, half, way):
-        u, v = spots[half]
         step = 1 if way == 0 else -1
-        copy = move(kind, half, me, None, place(half, u + step, v), whole_send, whole_recv, (kind, half, way))
-        return kind, copy, me, place(half, u - step, v)
+        copy = move(kind, half, me, None, place(half, step, 0), whole_send, whole_recv, (kind, half, way))
+        return kind, copy, me, place(half, -step, 0)
 
     def halved(kind, half, way):
-        u, v = spots[half]
         step = 1 if way == 0 else -1
-        who = place(half, u - step, v)
-        copy = move(kind, half, who, way, place(half, u + step, v), half_send, half_recv, (kind, half, way))
-        return kind, copy, who, place(half, u + 2, v)
+        who = place(half, -step, 0)
+        copy = move(kind, half, who, way, place(half, step, 0), half_send, half_recv, (kind, half, way))
+        return kind, copy, who, place(half, 2, 0)
 
     def far(kind, half, offset, way):
-        u, v = spots[half]
         step = 1 if way == 0 else -1
-        who = place(half, u + offset, v)
-        copy = move(kind, half, who, None, place(half, u, v + step), far_send, far_recv, (kind, half, offset, way))
-        return kind, copy, who, place(half, u + offset, v - step)
+        who = place(half, offset, 0)
+        copy = move(kind, half, who, None, place(half, 0, step), far_send, far_recv, (kind, half, offset, way))
+        return kind, copy, who, place(half, offset, -step)
 
     def farther(kind, half, offset, way):
-        u, v = spots[half]
         step = 1 if way == 0 else -1
-        who = place(half, u + offset, v - step)
+        who = place(half, offset, -step)
         copy = move(
-            kind, half, who, way, place(half, u, v + step), farther_send, farther_recv, (kind, half, offset, way)
-        )
-        return kind, copy, who, place(half, u + offset, v + 2)
+            kind, half, who, way, place(half, 0, step), farther_send, farther_recv, (kind, half, offset, way)
+        )
+        return kind, copy, who, place(half, offset, 2)
 
     def guarded(kind, who, act):
-        if kind != 1:
+        if kind == 0:
             act()
         else:
             pl.when(who >= 2)(act)
@@ -385,15 +382,16 @@
         for half, way in both:
             start(far(kind, half, 0, way))
 
-    def second(kind):
+    def halves_on(kind):
         for half, way in both:
             arrived(whole(kind, half, way))
             start(halved(kind, half, way))
+
+    def far_on(kind, offset):
         for half, way in both:
-            start(far(kind, half, 1, way))
-            start(far(kind, half, 3, way))
-
-    def third(kind):
+            start(far(kind, half, offset, way))
+
+    def last_far_on(kind):
         for half in range(2):
             for way in range(2):
                 arrived(halved(kind, half, way))
@@ -487,18 +485,19 @@
     own = [
         pltpu.make_async_copy(halves, blocks.at[:, me], local_sem.at[3]),
         pltpu.make_async_copy(picked.at[front], from_fronts.at[front], local_sem.at[4]),
-        pltpu.make_async_copy(late, late_all.at[front], local_sem.at[5]),
     ]
+    own_late = pltpu.make_async_copy(late, late_all.at[front], local_sem.at[5])
     for copy in own:
         copy.start()
+    own_late.start()
     for shift in range(1, fronts):
         over_copy(shift).start()
     for copy in own:
         copy.wait()
+    near(1)
+    own_far(1)
     for shift in range(1, fronts):
         late_copy(shift).start()
-    for shift in range(1, panels):
-        piece_copy(shift).start()
 
     def own_rows(root, index):
 
@@ -513,17 +512,23 @@
         top[index, chunk_rows(me), :] = chunk[index]
 
     own_rows(0, 0)
+    own_rows(1, 1)
+    own_rows(1, 2)
     near(0)
     own_far(0)
-    own_rows(1, 1)
-    own_rows(1, 2)
-    second(0)
-    third(0)
+    for shift in range(1, panels):
+        piece_copy(shift).start()
+    halves_on(1)
+    halves_on(0)
+    far_on(0, 1)
+    far_on(0, 3)
+    far_on(1, 1)
+    last_far_on(0)
     for offset in (0, 1, 3, 2):
         relay(0, offset)
-    near(2)
-    own_far(2)
-    near(1)
+    far_on(1, 3)
+    last_far_on(1)
+    relay(1, 0)
     finish(0)
 
     def block_step(index, carry):
@@ -535,7 +540,6 @@
 
         @pl.when(index == K // NB)
         def _():
-            finish(2)
             lower = product(top[1], inverses[0], 1, 1)
             factor10[...] = lower
             packed = lower.astype(BF16)
@@ -544,22 +548,8 @@
         low = pl.multiple_of((index - which * (K // NB)) * NB, NB)
         factor_block(low, inverses.at[which], staged, base_work, base_out)
 
-        @pl.when(index == 0)
-        def _():
-            second(2)
-
-        @pl.when(index == 2)
-        def _():
-            third(2)
-            for offset in (0, 1):
-                relay(2, offset)
-            second(1)
-            own_far(1)
-
-        @pl.when(index == 3)
-        def _():
-            relay(2, 3)
-            relay(2, 2)
+        @pl.when(index == 1)
+        def _():
             for shift in range(1, fronts):
                 over_copy(shift).wait_recv()
             total = from_fronts[0]
@@ -571,9 +561,8 @@
             for shift in range(1, panels):
                 inward_copy(shift).start()
 
-        @pl.when(index == 4)
-        def _():
-            third(1)
+        @pl.when(index == 2)
+        def _():
             for shift in range(1, panels):
                 piece_copy(shift).wait_recv()
             total = pieces[0]
@@ -583,9 +572,17 @@
             for shift in range(1, panels):
                 sum_copy(shift).start()
 
+        @pl.when(index == 3)
+        def _():
+            relay(1, 1)
+
+        @pl.when(index == 5)
+        def _():
+            relay(1, 3)
+
         @pl.when(index == 6)
         def _():
-            relay(1, 0)
+            relay(1, 2)
 
         return carry
 
@@ -612,18 +609,15 @@
     chosen_in[front] = chosen[front]
     front_values[...] = jnp.where(below, known[...], jnp.where(me == 0, solved0, solved1))
 
-    relay(1, 1)
     factor0 = product(columns[:, 0:K], inverse0, 1, 1, HIGH)
     current = columns[:, K:] - product(factor0.astype(BF16), lower.astype(BF16), 1, 1, None)
     factor1 = jnp.where(me >= 1, product(current, inverse1, 1, 1, HIGH), 0.0)
     factor[:, 0:K] = factor0
     factor[:, K:] = factor1
-    relay(1, 3)
     weight1 = product(factor1, inverse1, 1, 0, HIGH)
     weight0 = product(factor0 - product(weight1, lower, 1, 0, HIGH), inverse0, 1, 0, HIGH)
     weights[0] = weight0.astype(BF16)
     weights[1] = weight1.astype(BF16)
-    relay(1, 2)
 
     for shift in range(1, panels):
         inward_copy(shift).wait_recv()
@@ -637,8 +631,9 @@
     cap = child_values.shape[1]
     for lead in range(size // cap):
         child_values[lead] = total[lead * cap : (lead + 1) * cap, :]
+    own_late.wait()
     finish(1)
-    for kind in range(3):
+    for kind in range(2):
         drain(kind)
     for shift in range(1, panels):
         piece_copy(shift).wait_send()
@@ -711,8 +706,8 @@
             sem((3, panels)),
             sem((3,)),
         ]
-        + [sem((3, 2, 2))] * 4
-        + [sem((3, 2, 4, 2))] * 4
+        + [sem((2, 2, 2))] * 4
+        + [sem((2, 2, 4, 2))] * 4
         + [sem((panels,))] * 6
         + [sem((fronts,))] * 6
         + [sem((6,))],
@@ -770,7 +765,7 @@
         ],
         out_specs=[pl.BlockSpec((rows, K), lambda j: (0, j))] + [anywhere] * 3,
         scratch_shapes=[pltpu.SemaphoreType.DMA((3,))],
-        compiler_params=pltpu.CompilerParams(vmem_limit_bytes=56 << 20),
+        compiler_params=pltpu.CompilerParams(vmem_limit_bytes=40 << 20),
     )(late_all, blocks, weights, onehot, factor, front_values, child_values)
 
 

time: 289 us -> 200 us (0.69)
  Pallas kernels: 275 us -> 189 us
    pallas_call x1, Pallas kernels: 76.2 us -> 19.2 us  [update_step(): pl.pallas_call(update_kernel, name='update', grid=(steps,), out_shape=[ja...]
    pallas_call x1, Pallas kernels: 166 us -> 137 us  [panel_step(): pl.pallas_call(lambda *refs: panel_kernel((panels, fronts), side, *refs),...]
    unnamed x20 -> x12, local copies, waits for them, and re-layouts: 9.94 us -> 8.54 us
where the time goes in v5:
time: 200 us; the launch traced here: 199 us
  Pallas kernels  189 us (94%)
  local copies, waits for them, and re-layouts  9.37 us (5%)
    pallas_call x1, Pallas kernels, panel_step(): pl.pallas_call(lambda *refs: panel_kernel((panels, fronts), side, *refs),...  137 us
    pallas_call x1, Pallas kernels, exchange_rows(): pl.pallas_call(lambda *refs: exchange_kernel((panels, fronts), *refs), na...  32.8 us
    pallas_call x1, Pallas kernels, update_step(): pl.pallas_call(update_kernel, name='update', grid=(steps,), out_shape=[ja...  19.2 us
    unnamed x12, local copies, waits for them, and re-layouts  8.54 us

profile of v5, /device:TPU:1, one launch (start us, length us, event | category | flops | bytes accessed | tf_op | source)
XLA Modules:
  0.0 199.1 jit_solution(11138259085187837409)
XLA Ops:
  0.6 0.8 copy.10
  1.4 0.1 broadcast_in_dim.20.refs_1_
  1.5 0.0 copy-start.2
  1.5 1.2 copy-done.2
  2.7 32.8 %exchange.1 = (bf16[8,8,16,4,128]{4,3,2,1,0:T(4,128)(2,1)S(1)}, bf16[56,16,4,128]{3,2,1,0:T(4,128)(2,1)S(1)}, s32[8,16,4,128]{3,2,1,0:T(4,128)S(1)}, s32[8,2,4,128]{3,2,1,0:T(4,128)S(1)}) custom-call(bf16[16,64,4,128]{3,2,1,0:T(4,128)(2,1)S(1)} %bitcast.17, s32[16,4,128]{2,1,0:T(4,128)S(1)} %broadcast_in_dim.20.refs_1_), custom_call_target="tpu_custom_call" | custom-call | tf_op jit(solution)/shard_map/exchange/pallas_call | solution.py:190
  35.5 0.0 copy-start.1
  35.5 1.6 copy-done.1
  37.1 0.0 copy-start.3
  37.1 1.0 copy-done.3
  38.1 0.0 copy-start.4
  38.1 0.9 copy-done.4
  39.1 0.0 copy-start.5
  39.1 0.7 copy-done.5
  39.7 136.9 %panel_step.1 = (bf16[2,16,512,512]{3,2,1,0:T(8,128)(2,1)}, bf16[8,56,16,4,128]{4,3,2,1,0:T(4,128)(2,1)}, f32[512,1024]{1,0:T(8,128)S(1)}, bf16[2,512,512]{2,1,0...) custom-call(s32[8]{0:T(128)S(1)} %copy-done.5, ...), custom_call_target="tpu_custom_call" | custom-call | tf_op jit(solution)/shard_map/panel_step/pallas_call | solution.py:671
  176.6 0.0 copy-start
  176.7 3.1 %copy-done = bf16[8,56,16,4,128]{4,3,2,1,0:T(4,128)(2,1)S(1)} copy-done((bf16[8,56,16,4,128]{4,3,2,1,0:T(4,128)(2,1)S(1)}, bf16[8,56,16,4,128]{4,3,2,1,0:T(4,128)(2,1)}, u32[]{:S(2)}) %copy-start) | copy-done | bytes 7340056
  179.7 19.2 %update.1 = (bf16[512,7168]{1,0:T(8,128)(2,1)}, f32[512,1024]{1,0:T(8,128)}, f32[512,128]{1,0:T(8,128)}, f32[16,4,128]{2,1,0:T(4,128)}) custom-call(bf16[8,56,64,128]{3,2,1,0:T(8,128)(2,1)S(1)} %bitcast.15, bf16[2,16,512,512]{3,2,1,0:T(8,128)(2,1)} %get-tuple-element.24.blocks, bf16[2,512,512]{2,1,0:T(8,128)(2,1)S(1)} %get-tuple-element.25.weights, ...), custom_call_target="tpu_custom_call" | custom-call | tf_op jit(solution)/shard_map/update/pallas_call | solution.py:752
Async XLA Ops:
  1.5 1.2 copy-start.2
  35.5 1.6 copy-start.1
  37.1 1.0 copy-start.3
  38.1 0.9 copy-start.4
  39.1 0.7 copy-start.5
  176.6 3.1 %copy-start = (bf16[8,56,16,4,128]{4,3,2,1,0:T(4,128)(2,1)S(1)}, bf16[8,56,16,4,128]{4,3,2,1,0:T(4,128)(2,1)}, u32[]{:S(2)}) copy-start(bf16[8,56,16,4,128]{4,3,2,1,0:T(4,128)(2,1)} %get-tuple-element.23) | copy-start | bytes 22020100

commit v6 on v5

--- a/solution.py
+++ b/solution.py
@@ -78,14 +78,14 @@
     base_work[...] = joined[rows, rows]
     base_inverse(base_work, base_out)
     base = base_out[...]
-    solved = product(base, joined[rows, :], 1, 0)
+    solved = product(base, joined[rows, :], 1, 0, HIGH)
     lane = lax.broadcasted_iota(jnp.int32, solved.shape, 1)
     upper = jnp.where(lane >= high, solved, 0.0)
     staged[...] = solved
     staged[:, rows] = base
     strip = joined[:, rows]
     joined[:, rows] = jnp.where(lax.broadcasted_iota(jnp.int32, strip.shape, 0) >= high, 0.0, strip)
-    joined[...] = joined[...] - product(upper, staged[...], 0, 0)
+    joined[...] = joined[...] - product(upper, staged[...], 0, 0, HIGH)
     joined[rows, :] = jnp.where(lane < high, staged[...], 0.0)
 
 
@@ -196,7 +196,7 @@
             jax.ShapeDtypeStruct((fronts, panels, cap, lanes), jnp.int32),
             jax.ShapeDtypeStruct((fronts, lead, cap, lanes), jnp.int32),
         ),
-        in_specs=[pl.BlockSpec(memory_space=pl.ANY)] * 2,
+        in_specs=[pl.BlockSpec(memory_space=pltpu.HBM)] * 2,
         out_specs=[pl.BlockSpec(memory_space=space) for space in (pltpu.VMEM, pl.ANY, pltpu.VMEM, pltpu.VMEM)],
         scratch_shapes=[sem((panels,))] * 6 + [sem((fronts,))] * 6 + [sem((4,))],
         compiler_params=pltpu.CompilerParams(collective_id=1, has_side_effects=True, vmem_limit_bytes=8 << 20),
@@ -219,7 +219,7 @@
         [(kept == lane + t * lanes).astype(F32) for t in range(known.shape[0] // lanes)], axis=1
     )
     small = chosen.astype(BF16)
-    onehot[...] = small
+    onehot[...] = chosen.T.astype(BF16)
     half = piv_cols.shape[1] // 2
     for h in range(2):
         tiles = half // lanes
@@ -243,9 +243,9 @@
 
 
 def panel_kernel(
-    counts, side, parents, table, own_table, early, piv_cols, known, right_side, late,
+    counts, side, parents, table, own_table, early, own_columns, known, right_side, late,
     blocks, late_all, factor, weights, front_values, child_values, onehot,
-    columns, halves, pick, picked,
+    piv_cols, columns, halves, pick, picked,
     inverses, factor10, partial, sums, solved, chosen, chosen_in, from_fronts, onward, inward,
     top, chunk, pieces, staged, base_work, base_out,
     scatter_send, scatter_recv, whole_send, whole_recv, half_send, half_recv,
@@ -258,6 +258,8 @@
     front = lax.axis_index("front")
     across, along = me // side, lax.rem(me, side)
     part = top.shape[1] // panels
+    load = pltpu.make_async_copy(own_columns, piv_cols, local_sem.at[6])
+    load.start()
     barrier = pltpu.get_barrier_semaphore()
     for shift in range(1, panels):
         peer = lax.rem(me + shift, panels)
@@ -265,6 +267,7 @@
     for shift in range(1, fronts):
         peer = lax.rem(front + shift, fronts)
         pl.semaphore_signal(barrier, inc=1, device_id={"front": peer}, device_id_type=MESH)
+    load.wait()
     assemble(parents, table, own_table, early, piv_cols, known, columns, halves, onehot, pick, picked)
     below = me >= 2
     boundary = jnp.where(below, known[...], 0.0)
@@ -314,10 +317,10 @@
         return first * side + second if half == 0 else second * side + first
 
     def view(kind, half, who, rows):
-        if kind == 0:
+        if kind != 1:
             size = part if rows is None else part // 2
             low = who * part + (part // 2 if rows == 1 else 0)
-            return top.at[:, pl.ds(pl.multiple_of(low, 8), size), pl.ds(half * (K // 2), K // 2)]
+            return top.at[pl.ds(kind // 2, kind // 2 + 1), pl.ds(pl.multiple_of(low, 8), size), pl.ds(half * (K // 2), K // 2)]
         ref = blocks.at[half, who]
         return ref if rows is None else ref.at[pl.ds(rows * (K // 2), K // 2)]
 
@@ -358,7 +361,7 @@
         return kind, copy, who, place(half, offset, 2)
 
     def guarded(kind, who, act):
-        if kind == 0:
+        if kind != 1:
             act()
         else:
             pl.when(who >= 2)(act)
@@ -495,7 +498,6 @@
     for copy in own:
         copy.wait()
     near(1)
-    own_far(1)
     for shift in range(1, fronts):
         late_copy(shift).start()
 
@@ -512,23 +514,22 @@
         top[index, chunk_rows(me), :] = chunk[index]
 
     own_rows(0, 0)
-    own_rows(1, 1)
-    own_rows(1, 2)
     near(0)
     own_far(0)
-    for shift in range(1, panels):
-        piece_copy(shift).start()
     halves_on(1)
     halves_on(0)
     far_on(0, 1)
     far_on(0, 3)
-    far_on(1, 1)
+    for shift in range(1, panels):
+        piece_copy(shift).start()
     last_far_on(0)
     for offset in (0, 1, 3, 2):
         relay(0, offset)
-    far_on(1, 3)
-    last_far_on(1)
-    relay(1, 0)
+    own_rows(1, 1)
+    own_rows(1, 2)
+    near(2)
+    own_far(2)
+    own_far(1)
     finish(0)
 
     def block_step(index, carry):
@@ -540,7 +541,8 @@
 
         @pl.when(index == K // NB)
         def _():
-            lower = product(top[1], inverses[0], 1, 1)
+            finish(2)
+            lower = product(top[1], inverses[0], 1, 1, HIGH)
             factor10[...] = lower
             packed = lower.astype(BF16)
             inverses[1] = symmetric_part(top[2] - product(packed, packed, 1, 1, None))
@@ -548,8 +550,45 @@
         low = pl.multiple_of((index - which * (K // NB)) * NB, NB)
         factor_block(low, inverses.at[which], staged, base_work, base_out)
 
+        @pl.when(index == 0)
+        def _():
+            halves_on(2)
+            far_on(2, 1)
+            far_on(2, 3)
+            far_on(1, 1)
+
         @pl.when(index == 1)
         def _():
+            last_far_on(2)
+            relay(2, 0)
+
+        @pl.when(index == 2)
+        def _():
+            relay(2, 1)
+            relay(2, 3)
+
+        @pl.when(index == 3)
+        def _():
+            relay(2, 2)
+            far_on(1, 3)
+            last_far_on(1)
+            relay(1, 0)
+
+        @pl.when(index == 4)
+        def _():
+            relay(1, 1)
+            for shift in range(1, panels):
+                piece_copy(shift).wait_recv()
+            total = pieces[0]
+            for who in range(1, panels):
+                total = total + pieces[who]
+            sums[me] = total
+            for shift in range(1, panels):
+                sum_copy(shift).start()
+
+        @pl.when(index == 5)
+        def _():
+            relay(1, 3)
             for shift in range(1, fronts):
                 over_copy(shift).wait_recv()
             total = from_fronts[0]
@@ -560,25 +599,6 @@
                 onward[who] = total[who * cap : (who + 1) * cap, :]
             for shift in range(1, panels):
                 inward_copy(shift).start()
-
-        @pl.when(index == 2)
-        def _():
-            for shift in range(1, panels):
-                piece_copy(shift).wait_recv()
-            total = pieces[0]
-            for who in range(1, panels):
-                total = total + pieces[who]
-            sums[me] = total
-            for shift in range(1, panels):
-                sum_copy(shift).start()
-
-        @pl.when(index == 3)
-        def _():
-            relay(1, 1)
-
-        @pl.when(index == 5)
-        def _():
-            relay(1, 3)
 
         @pl.when(index == 6)
         def _():
@@ -633,7 +653,7 @@
         child_values[lead] = total[lead * cap : (lead + 1) * cap, :]
     own_late.wait()
     finish(1)
-    for kind in range(2):
+    for kind in range(3):
         drain(kind)
     for shift in range(1, panels):
         piece_copy(shift).wait_send()
@@ -678,11 +698,12 @@
             jax.ShapeDtypeStruct((2, K, K), BF16),
             jax.ShapeDtypeStruct((rows, rhs), F32),
             jax.ShapeDtypeStruct((panels, cap, rhs), F32),
-            jax.ShapeDtypeStruct((table.shape[0], rows), BF16),
+            jax.ShapeDtypeStruct((rows, table.shape[0]), BF16),
         ),
-        in_specs=[pl.BlockSpec(memory_space=pltpu.SMEM)] + [vmem] * 6 + [anywhere],
-        out_specs=[anywhere] * 2 + [vmem] * 5,
+        in_specs=[pl.BlockSpec(memory_space=pltpu.SMEM)] + [vmem] * 3 + [pl.BlockSpec(memory_space=pltpu.HBM)] + [vmem] * 2 + [anywhere],
+        out_specs=[anywhere] + [vmem] * 6,
         scratch_shapes=[
+            pltpu.VMEM((rows, pivots), F32),
             pltpu.VMEM((rows, pivots), F32),
             pltpu.VMEM((2, rows, K), BF16),
             pltpu.VMEM((own_table.shape[0], pivots), F32),
@@ -706,13 +727,13 @@
             sem((3, panels)),
             sem((3,)),
         ]
-        + [sem((2, 2, 2))] * 4
-        + [sem((2, 2, 4, 2))] * 4
+        + [sem((3, 2, 2))] * 4
+        + [sem((3, 2, 4, 2))] * 4
         + [sem((panels,))] * 6
         + [sem((fronts,))] * 6
-        + [sem((6,))],
+        + [sem((7,))],
         compiler_params=pltpu.CompilerParams(
-            collective_id=2, has_side_effects=True, vmem_limit_bytes=40 << 20
+            collective_id=2, has_side_effects=True, vmem_limit_bytes=28 << 20
         ),
     )(parents, table, own_table, early, piv_cols, known, right_side, late)
 
@@ -728,11 +749,17 @@
             pltpu.make_async_copy(results[i], outs[i], sem.at[i]).start()
 
     fronts, tiles, each, lanes = late.shape
-    rows = jnp.concatenate([late[:, t].reshape(fronts * each, lanes) for t in range(tiles)], axis=1)
-    value = product(onehot[...], rows, 0, 0, None)
-    for half in range(2):
-        value = value - product(weights[half], blocks[half, 0], 1, 1, None)
-    update[...] = jnp.where(lax.axis_index("panel") >= 2, value, 0.0).astype(BF16)
+    below = lax.axis_index("panel") >= 2
+    count = blocks.shape[1]
+    for block in range(count):
+        low = block * tiles // count
+        rows = jnp.concatenate(
+            [late[:, low + t].reshape(fronts * each, lanes) for t in range(tiles // count)], axis=1
+        )
+        value = product(onehot[...], rows, 1, 0, None)
+        for half in range(2):
+            value = value - product(weights[half], blocks[half, block], 1, 1, None)
+        update[:, block * K : (block + 1) * K] = jnp.where(below, value, 0.0).astype(BF16)
 
     @pl.when(step == pl.num_programs(0) - 1)
     def _():
@@ -742,9 +769,9 @@
 
 def update_step(late_all, blocks, weights, onehot, factor, front_values, child_values):
     fronts, all_tiles, each, lanes = late_all.shape
-    tiles = K // lanes
+    tiles = 2 * K // lanes
     steps = all_tiles // tiles
-    first = blocks.shape[1] - steps
+    first = blocks.shape[1] // 2 - steps
     rows = weights.shape[1]
     anywhere = pl.BlockSpec(memory_space=pl.ANY)
     fixed = pl.BlockSpec(memory_space=pltpu.VMEM)
@@ -753,17 +780,17 @@
         update_kernel,
         name="update",
         grid=(steps,),
-        out_shape=[jax.ShapeDtypeStruct((rows, steps * K), BF16)] + like,
+        out_shape=[jax.ShapeDtypeStruct((rows, steps * 2 * K), BF16)] + like,
         in_specs=[
             pl.BlockSpec((fronts, tiles, each, lanes), lambda j: (0, j, 0, 0)),
-            pl.BlockSpec((2, 1, K, K), lambda j: (0, j + first, 0, 0)),
+            pl.BlockSpec((2, 2, K, K), lambda j: (0, j + first, 0, 0)),
             fixed,
             fixed,
             anywhere,
             anywhere,
             anywhere,
         ],
-        out_specs=[pl.BlockSpec((rows, K), lambda j: (0, j))] + [anywhere] * 3,
+        out_specs=[pl.BlockSpec((rows, 2 * K), lambda j: (0, j))] + [anywhere] * 3,
         scratch_shapes=[pltpu.SemaphoreType.DMA((3,))],
         compiler_params=pltpu.CompilerParams(vmem_limit_bytes=40 << 20),
     )(late_all, blocks, weights, onehot, factor, front_values, child_values)

time: 200 us -> 193 us (0.965)
  local copies, waits for them, and re-layouts: 9.37 us -> 6.3 us
  Pallas kernels: 189 us -> 186 us
    pallas_call x1, Pallas kernels: 19.2 us -> 16.1 us  [update_step(): pl.pallas_call(update_kernel, name='update', grid=(steps,), out_shape=[ja...]
    unnamed x12 -> x10, local copies, waits for them, and re-layouts: 8.54 us -> 5.46 us
where the time goes in v6:
time: 193 us
  Pallas kernels  186 us (96%)
  local copies, waits for them, and re-layouts  6.3 us (3%)
    pallas_call x1, Pallas kernels, panel_step(): pl.pallas_call(lambda *refs: panel_kernel((panels, fronts), side, *refs),...  137 us
    pallas_call x1, Pallas kernels, exchange_rows(): pl.pallas_call(lambda *refs: exchange_kernel((panels, fronts), *refs), na...  32.8 us
    pallas_call x1, Pallas kernels, update_step(): pl.pallas_call(update_kernel, name='update', grid=(steps,), out_shape=[ja...  16.1 us
    unnamed x10, local copies, waits for them, and re-layouts  5.46 us

profile of v6, /device:TPU:1, one launch (start us, length us, event | category | flops | bytes accessed | tf_op | source)
XLA Modules:
  0.0 193.0 jit_solution(12121915638439999485)
XLA Ops:
  0.6 0.8 copy.10
  1.4 0.1 broadcast_in_dim.20.refs_1_
  1.5 0.0 copy-start.1
  1.5 1.2 copy-done.1
  2.7 32.8 %exchange.1 = (bf16[8,8,16,4,128]{4,3,2,1,0:T(4,128)(2,1)S(1)}, bf16[56,16,4,128]{3,2,1,0:T(4,128)(2,1)S(1)}, s32[8,16,4,128]{3,2,1,0:T(4,128)S(1)}, s32[8,2,4,128]{3,2,1,0:T(4,128)S(1)}) custom-call(bf16[16,64,4,128]{3,2,1,0:T(4,128)(2,1)S(1)} %bitcast.17, s32[16,4,128]{2,1,0:T(4,128)S(1)} %broadcast_in_dim.20.refs_1_), custom_call_target="tpu_custom_call" | custom-call | tf_op jit(solution)/shard_map/exchange/pallas_call | solution.py:190
  35.5 0.0 copy-start
  35.5 1.6 copy-done
  37.1 0.0 copy-start.2
  37.1 1.0 copy-done.2
  38.1 0.0 copy-start.3
  38.1 0.9 copy-done.3
  39.1 0.0 copy-start.4
  39.1 0.7 copy-done.4
  39.7 137.0 %panel_step.1 = (bf16[2,16,512,512]{3,2,1,0:T(8,128)(2,1)}, bf16[8,56,16,4,128]{4,3,2,1,0:T(4,128)(2,1)S(1)}, f32[512,1024]{1,0:T(8,128)S(1)}, bf16[2,512,512]{2...) custom-call(s32[8]{0:T(128)S(1)} %copy-done.4, ...), custom_call_target="tpu_custom_call" | custom-call | tf_op jit(solution)/shard_map/panel_step/pallas_call | solution.py:691
  176.7 16.1 %update.1 = (bf16[512,7168]{1,0:T(8,128)(2,1)}, f32[512,1024]{1,0:T(8,128)}, f32[512,128]{1,0:T(8,128)}, f32[16,4,128]{2,1,0:T(4,128)}) custom-call(bf16[8,56,64,128]{3,2,1,0:T(8,128)(2,1)S(1)} %bitcast.15, bf16[2,16,512,512]{3,2,1,0:T(8,128)(2,1)} %get-tuple-element.24.blocks, bf16[2,512,512]{2,1,0:T(8,128)(2,1)S(1)} %get-tuple-element.25.weights, ...), custom_call_target="tpu_custom_call" | custom-call | tf_op jit(solution)/shard_map/update/pallas_call | solution.py:779
Async XLA Ops:
  1.5 1.2 copy-start.1
  35.5 1.6 copy-start
  37.1 1.0 copy-start.2
  38.1 0.9 copy-start.3
  39.1 0.7 copy-start.4

commit v7 on v6

--- a/solution.py
+++ b/solution.py
@@ -199,27 +199,27 @@
         in_specs=[pl.BlockSpec(memory_space=pltpu.HBM)] * 2,
         out_specs=[pl.BlockSpec(memory_space=space) for space in (pltpu.VMEM, pl.ANY, pltpu.VMEM, pltpu.VMEM)],
         scratch_shapes=[sem((panels,))] * 6 + [sem((fronts,))] * 6 + [sem((4,))],
+        cost_estimate=pl.CostEstimate(flops=20_000_000_000, bytes_accessed=60_000_000, transcendentals=0),
         compiler_params=pltpu.CompilerParams(collective_id=1, has_side_effects=True, vmem_limit_bytes=8 << 20),
     )(rows, slots)
 
 
-def assemble(parents, table, own_table, early, piv_cols, known, columns, halves, onehot, pick, picked):
+def masked_slots(parents, ref, fronts):
     front = lax.axis_index("front")
+    size = ref.shape[0] // fronts
+    return jnp.concatenate(
+        [jnp.where(parents[c] == front, ref[c * size : (c + 1) * size, :], -1) for c in range(fronts)], axis=0
+    )
+
+
+def assemble(parents, table, early, piv_cols, columns, halves):
     fronts, _, each, lanes = early.shape
-    owners = [parents[child] == front for child in range(fronts)]
-
-    def masked(ref, size):
-        return jnp.concatenate(
-            [jnp.where(owners[c], ref[c * size : (c + 1) * size, :], -1) for c in range(fronts)], axis=0
-        )
-
-    kept = masked(table, each)
+    kept = masked_slots(parents, table, fronts)
     lane = lax.broadcasted_iota(jnp.int32, kept.shape, 1)
     chosen = jnp.concatenate(
-        [(kept == lane + t * lanes).astype(F32) for t in range(known.shape[0] // lanes)], axis=1
+        [(kept == lane + t * lanes).astype(F32) for t in range(piv_cols.shape[0] // lanes)], axis=1
     )
     small = chosen.astype(BF16)
-    onehot[...] = chosen.T.astype(BF16)
     half = piv_cols.shape[1] // 2
     for h in range(2):
         tiles = half // lanes
@@ -229,12 +229,19 @@
         value = piv_cols[:, h * half : (h + 1) * half] + product(small, rows, 0, 0, None)
         columns[:, h * half : (h + 1) * half] = value
         halves[h] = value.astype(BF16)
+    return chosen
+
+
+def select_values(parents, own_table, chosen, known, fronts, onehot, pick, picked):
+    each = chosen.shape[0] // fronts
+    lanes = own_table.shape[1]
+    onehot[...] = chosen.T.astype(BF16)
     found = product(chosen, known[...], 1, 0)
     for child in range(fronts):
         picked[child] = found[child * each : (child + 1) * each, :]
     size = own_table.shape[0] // fronts
-    own = masked(own_table, size)
-    cap = size * K // piv_cols.shape[1]
+    own = masked_slots(parents, own_table, fronts)
+    cap = size * K // pick.shape[1]
     where = lax.rem(lax.broadcasted_iota(jnp.int32, own.shape, 0), size) // cap
     target = jnp.where(own >= 0, own + where * K, -1)
     lane = lax.broadcasted_iota(jnp.int32, own.shape, 1)
@@ -268,7 +275,227 @@
         peer = lax.rem(front + shift, fronts)
         pl.semaphore_signal(barrier, inc=1, device_id={"front": peer}, device_id_type=MESH)
     load.wait()
-    assemble(parents, table, own_table, early, piv_cols, known, columns, halves, onehot, pick, picked)
+    chosen_rows = assemble(parents, table, early, piv_cols, columns, halves)
+    pl.semaphore_wait(barrier, panels + fronts - 2)
+
+    def chunk_rows(who):
+        return pl.ds(pl.multiple_of(who * part, 8), part)
+
+    def scatter(shift, index):
+        peer = lax.rem(me + shift, panels)
+        lanes = pl.ds(K if index == 2 else 0, K)
+        return pltpu.make_async_remote_copy(
+            src_ref=columns.at[chunk_rows(peer), lanes],
+            dst_ref=chunk.at[index],
+            send_sem=scatter_send.at[index, shift],
+            recv_sem=scatter_recv.at[index],
+            device_id={"panel": peer},
+            device_id_type=MESH,
+        )
+
+    def own_chunk(index):
+        lanes = pl.ds(K if index == 2 else 0, K)
+        return pltpu.make_async_copy(columns.at[chunk_rows(me), lanes], chunk.at[index], local_sem.at[index])
+
+    roots = ((0, (0,)), (1, (1, 2)))
+    for root, indices in roots:
+
+        @pl.when(me == root)
+        def _():
+            for shift in range(1, panels):
+                for index in indices:
+                    scatter(shift, index).start()
+            for index in indices:
+                own_chunk(index).start()
+
+    coords = [[lax.rem(at + step, side) for step in range(side)] for at in (across, along)]
+
+    def place(half, first, second):
+        near_axis, far_axis = (coords[0], coords[1]) if half == 0 else (coords[1], coords[0])
+        first, second = near_axis[first % side], far_axis[second % side]
+        return first * side + second if half == 0 else second * side + first
+
+    def view(kind, half, who, rows):
+        if kind != 1:
+            size = part if rows is None else part // 2
+            low = who * part + (part // 2 if rows == 1 else 0)
+            return top.at[pl.ds(kind // 2, kind // 2 + 1), pl.ds(pl.multiple_of(low, 8), size), pl.ds(half * (K // 2), K // 2)]
+        ref = blocks.at[half, who]
+        return ref if rows is None else ref.at[pl.ds(rows * (K // 2), K // 2)]
+
+    def move(kind, half, who, rows, target, send, recv, slot):
+        ref = view(kind, half, who, rows)
+        return pltpu.make_async_remote_copy(
+            src_ref=ref,
+            dst_ref=ref,
+            send_sem=send.at[slot],
+            recv_sem=recv.at[slot],
+            device_id={"panel": target},
+            device_id_type=MESH,
+        )
+
+    def whole(kind, half, way):
+        step = 1 if way == 0 else -1
+        copy = move(kind, half, me, None, place(half, step, 0), whole_send, whole_recv, (kind, half, way))
+        return kind, copy, me, place(half, -step, 0)
+
+    def halved(kind, half, way):
+        step = 1 if way == 0 else -1
+        who = place(half, -step, 0)
+        copy = move(kind, half, who, way, place(half, step, 0), half_send, half_recv, (kind, half, way))
+        return kind, copy, who, place(half, 2, 0)
+
+    def far(kind, half, offset, way):
+        step = 1 if way == 0 else -1
+        who = place(half, offset, 0)
+        copy = move(kind, half, who, None, place(half, 0, step), far_send, far_recv, (kind, half, offset, way))
+        return kind, copy, who, place(half, offset, -step)
+
+    def farther(kind, half, offset, way):
+        step = 1 if way == 0 else -1
+        who = place(half, offset, -step)
+        copy = move(
+            kind, half, who, way, place(half, 0, step), farther_send, farther_recv, (kind, half, offset, way)
+        )
+        return kind, copy, who, place(half, offset, 2)
+
+    def guarded(kind, who, act):
+        if kind != 1:
+            act()
+        else:
+            pl.when(who >= 2)(act)
+
+    def start(hop):
+        guarded(hop[0], hop[2], hop[1].start)
+
+    def sent(hop):
+        guarded(hop[0], hop[2], hop[1].wait_send)
+
+    def arrived(hop):
+        guarded(hop[0], hop[3], hop[1].wait_recv)
+
+    both = [(half, way) for half in range(2) for way in range(2)]
+
+    def near(kind):
+        for half, way in both:
+            start(whole(kind, half, way))
+
+    def own_far(kind):
+        for half, way in both:
+            start(far(kind, half, 0, way))
+
+    def halves_on(kind):
+        for half, way in both:
+            arrived(whole(kind, half, way))
+            start(halved(kind, half, way))
+
+    def far_on(kind, offset):
+        for half, way in both:
+            start(far(kind, half, offset, way))
+
+    def last_far_on(kind):
+        for half in range(2):
+            for way in range(2):
+                arrived(halved(kind, half, way))
+            for way in range(2):
+                start(far(kind, half, 2, way))
+
+    def relay(kind, offset):
+        for half, way in both:
+            arrived(far(kind, half, offset, way))
+            start(farther(kind, half, offset, way))
+
+    def finish(kind):
+        for half, way in both:
+            for offset in range(4):
+                arrived(farther(kind, half, offset, way))
+
+    def drain(kind):
+        for half, way in both:
+            sent(whole(kind, half, way))
+            sent(halved(kind, half, way))
+            for offset in range(4):
+                sent(far(kind, half, offset, way))
+                sent(farther(kind, half, offset, way))
+
+    def over_copy(shift):
+        peer = lax.rem(front + shift, fronts)
+        return pltpu.make_async_remote_copy(
+            src_ref=picked.at[peer],
+            dst_ref=from_fronts.at[front],
+            send_sem=over_send.at[shift],
+            recv_sem=over_recv.at[shift],
+            device_id={"front": peer},
+            device_id_type=MESH,
+        )
+
+    def inward_copy(shift):
+        peer = lax.rem(me + shift, panels)
+        return pltpu.make_async_remote_copy(
+            src_ref=onward.at[peer],
+            dst_ref=inward.at[me],
+            send_sem=inward_send.at[shift],
+            recv_sem=inward_recv.at[shift],
+            device_id={"panel": peer},
+            device_id_type=MESH,
+        )
+
+    def pick_copy(shift):
+        peer = lax.rem(front + shift, fronts)
+        return pltpu.make_async_remote_copy(
+            src_ref=chosen.at[peer],
+            dst_ref=chosen_in.at[front],
+            send_sem=pick_send.at[shift],
+            recv_sem=pick_recv.at[shift],
+            device_id={"front": peer},
+            device_id_type=MESH,
+        )
+
+    def late_copy(shift):
+        peer = lax.rem(front + shift, fronts)
+        return pltpu.make_async_remote_copy(
+            src_ref=late,
+            dst_ref=late_all.at[front],
+            send_sem=late_send.at[shift],
+            recv_sem=late_recv.at[shift],
+            device_id={"front": peer},
+            device_id_type=MESH,
+        )
+
+    def piece_copy(shift):
+        peer = lax.rem(me + shift, panels)
+        return pltpu.make_async_remote_copy(
+            src_ref=partial.at[peer],
+            dst_ref=pieces.at[me],
+            send_sem=piece_send.at[shift],
+            recv_sem=piece_recv.at[shift],
+            device_id={"panel": peer},
+            device_id_type=MESH,
+        )
+
+    def sum_copy(shift):
+        peer = lax.rem(me + shift, panels)
+        return pltpu.make_async_remote_copy(
+            src_ref=sums.at[me],
+            dst_ref=sums.at[me],
+            send_sem=sum_send.at[shift],
+            recv_sem=sum_recv.at[shift],
+            device_id={"panel": peer},
+            device_id_type=MESH,
+        )
+
+    own_halves = pltpu.make_async_copy(halves, blocks.at[:, me], local_sem.at[3])
+    own_late = pltpu.make_async_copy(late, late_all.at[front], local_sem.at[5])
+    own_halves.start()
+    own_late.start()
+    own_halves.wait()
+    near(1)
+    select_values(parents, own_table, chosen_rows, known, fronts, onehot, pick, picked)
+    for shift in range(1, fronts):
+        over_copy(shift).start()
+    for shift in range(1, fronts):
+        late_copy(shift).start()
+    from_fronts[front] = picked[front]
     below = me >= 2
     boundary = jnp.where(below, known[...], 0.0)
     width = partial.shape[1]
@@ -277,229 +504,6 @@
         for piece in range(panels // 2):
             partial[half * (panels // 2) + piece] = value[piece * width : (piece + 1) * width, :]
     pieces[me] = partial[me]
-    pl.semaphore_wait(barrier, panels + fronts - 2)
-
-    def chunk_rows(who):
-        return pl.ds(pl.multiple_of(who * part, 8), part)
-
-    def scatter(shift, index):
-        peer = lax.rem(me + shift, panels)
-        lanes = pl.ds(K if index == 2 else 0, K)
-        return pltpu.make_async_remote_copy(
-            src_ref=columns.at[chunk_rows(peer), lanes],
-            dst_ref=chunk.at[index],
-            send_sem=scatter_send.at[index, shift],
-            recv_sem=scatter_recv.at[index],
-            device_id={"panel": peer},
-            device_id_type=MESH,
-        )
-
-    def own_chunk(index):
-        lanes = pl.ds(K if index == 2 else 0, K)
-        return pltpu.make_async_copy(columns.at[chunk_rows(me), lanes], chunk.at[index], local_sem.at[index])
-
-    roots = ((0, (0,)), (1, (1, 2)))
-    for root, indices in roots:
-
-        @pl.when(me == root)
-        def _():
-            for shift in range(1, panels):
-                for index in indices:
-                    scatter(shift, index).start()
-            for index in indices:
-                own_chunk(index).start()
-
-    coords = [[lax.rem(at + step, side) for step in range(side)] for at in (across, along)]
-
-    def place(half, first, second):
-        near_axis, far_axis = (coords[0], coords[1]) if half == 0 else (coords[1], coords[0])
-        first, second = near_axis[first % side], far_axis[second % side]
-        return first * side + second if half == 0 else second * side + first
-
-    def view(kind, half, who, rows):
-        if kind != 1:
-            size = part if rows is None else part // 2
-            low = who * part + (part // 2 if rows == 1 else 0)
-            return top.at[pl.ds(kind // 2, kind // 2 + 1), pl.ds(pl.multiple_of(low, 8), size), pl.ds(half * (K // 2), K // 2)]
-        ref = blocks.at[half, who]
-        return ref if rows is None else ref.at[pl.ds(rows * (K // 2), K // 2)]
-
-    def move(kind, half, who, rows, target, send, recv, slot):
-        ref = view(kind, half, who, rows)
-        return pltpu.make_async_remote_copy(
-            src_ref=ref,
-            dst_ref=ref,
-            send_sem=send.at[slot],
-            recv_sem=recv.at[slot],
-            device_id={"panel": target},
-            device_id_type=MESH,
-        )
-
-    def whole(kind, half, way):
-        step = 1 if way == 0 else -1
-        copy = move(kind, half, me, None, place(half, step, 0), whole_send, whole_recv, (kind, half, way))
-        return kind, copy, me, place(half, -step, 0)
-
-    def halved(kind, half, way):
-        step = 1 if way == 0 else -1
-        who = place(half, -step, 0)
-        copy = move(kind, half, who, way, place(half, step, 0), half_send, half_recv, (kind, half, way))
-        return kind, copy, who, place(half, 2, 0)
-
-    def far(kind, half, offset, way):
-        step = 1 if way == 0 else -1
-        who = place(half, offset, 0)
-        copy = move(kind, half, who, None, place(half, 0, step), far_send, far_recv, (kind, half, offset, way))
-        return kind, copy, who, place(half, offset, -step)
-
-    def farther(kind, half, offset, way):
-        step = 1 if way == 0 else -1
-        who = place(half, offset, -step)
-        copy = move(
-            kind, half, who, way, place(half, 0, step), farther_send, farther_recv, (kind, half, offset, way)
-        )
-        return kind, copy, who, place(half, offset, 2)
-
-    def guarded(kind, who, act):
-        if kind != 1:
-            act()
-        else:
-            pl.when(who >= 2)(act)
-
-    def start(hop):
-        guarded(hop[0], hop[2], hop[1].start)
-
-    def sent(hop):
-        guarded(hop[0], hop[2], hop[1].wait_send)
-
-    def arrived(hop):
-        guarded(hop[0], hop[3], hop[1].wait_recv)
-
-    both = [(half, way) for half in range(2) for way in range(2)]
-
-    def near(kind):
-        for half, way in both:
-            start(whole(kind, half, way))
-
-    def own_far(kind):
-        for half, way in both:
-            start(far(kind, half, 0, way))
-
-    def halves_on(kind):
-        for half, way in both:
-            arrived(whole(kind, half, way))
-            start(halved(kind, half, way))
-
-    def far_on(kind, offset):
-        for half, way in both:
-            start(far(kind, half, offset, way))
-
-    def last_far_on(kind):
-        for half in range(2):
-            for way in range(2):
-                arrived(halved(kind, half, way))
-            for way in range(2):
-                start(far(kind, half, 2, way))
-
-    def relay(kind, offset):
-        for half, way in both:
-            arrived(far(kind, half, offset, way))
-            start(farther(kind, half, offset, way))
-
-    def finish(kind):
-        for half, way in both:
-            for offset in range(4):
-                arrived(farther(kind, half, offset, way))
-
-    def drain(kind):
-        for half, way in both:
-            sent(whole(kind, half, way))
-            sent(halved(kind, half, way))
-            for offset in range(4):
-                sent(far(kind, half, offset, way))
-                sent(farther(kind, half, offset, way))
-
-    def over_copy(shift):
-        peer = lax.rem(front + shift, fronts)
-        return pltpu.make_async_remote_copy(
-            src_ref=picked.at[peer],
-            dst_ref=from_fronts.at[front],
-            send_sem=over_send.at[shift],
-            recv_sem=over_recv.at[shift],
-            device_id={"front": peer},
-            device_id_type=MESH,
-        )
-
-    def inward_copy(shift):
-        peer = lax.rem(me + shift, panels)
-        return pltpu.make_async_remote_copy(
-            src_ref=onward.at[peer],
-            dst_ref=inward.at[me],
-            send_sem=inward_send.at[shift],
-            recv_sem=inward_recv.at[shift],
-            device_id={"panel": peer},
-            device_id_type=MESH,
-        )
-
-    def pick_copy(shift):
-        peer = lax.rem(front + shift, fronts)
-        return pltpu.make_async_remote_copy(
-            src_ref=chosen.at[peer],
-            dst_ref=chosen_in.at[front],
-            send_sem=pick_send.at[shift],
-            recv_sem=pick_recv.at[shift],
-            device_id={"front": peer},
-            device_id_type=MESH,
-        )
-
-    def late_copy(shift):
-        peer = lax.rem(front + shift, fronts)
-        return pltpu.make_async_remote_copy(
-            src_ref=late,
-            dst_ref=late_all.at[front],
-            send_sem=late_send.at[shift],
-            recv_sem=late_recv.at[shift],
-            device_id={"front": peer},
-            device_id_type=MESH,
-        )
-
-    def piece_copy(shift):
-        peer = lax.rem(me + shift, panels)
-        return pltpu.make_async_remote_copy(
-            src_ref=partial.at[peer],
-            dst_ref=pieces.at[me],
-            send_sem=piece_send.at[shift],
-            recv_sem=piece_recv.at[shift],
-            device_id={"panel": peer},
-            device_id_type=MESH,
-        )
-
-    def sum_copy(shift):
-        peer = lax.rem(me + shift, panels)
-        return pltpu.make_async_remote_copy(
-            src_ref=sums.at[me],
-            dst_ref=sums.at[me],
-            send_sem=sum_send.at[shift],
-            recv_sem=sum_recv.at[shift],
-            device_id={"panel": peer},
-            device_id_type=MESH,
-        )
-
-    own = [
-        pltpu.make_async_copy(halves, blocks.at[:, me], local_sem.at[3]),
-        pltpu.make_async_copy(picked.at[front], from_fronts.at[front], local_sem.at[4]),
-    ]
-    own_late = pltpu.make_async_copy(late, late_all.at[front], local_sem.at[5])
-    for copy in own:
-        copy.start()
-    own_late.start()
-    for shift in range(1, fronts):
-        over_copy(shift).start()
-    for copy in own:
-        copy.wait()
-    near(1)
-    for shift in range(1, fronts):
-        late_copy(shift).start()
 
     def own_rows(root, index):
 

time: 193 us -> 189 us (0.979)
  local copies, waits for them, and re-layouts: 6.3 us -> 2.08 us
    unnamed x10, local copies, waits for them, and re-layouts: 5.46 us -> 1.24 us
where the time goes in v7:
time: 189 us
  Pallas kernels  186 us (98%)
  local copies, waits for them, and re-layouts  2.08 us (1%)
    pallas_call x1, Pallas kernels, panel_step(): pl.pallas_call(lambda *refs: panel_kernel((panels, fronts), side, *refs),...  137 us
    pallas_call x1, Pallas kernels, exchange_rows(): pl.pallas_call(lambda *refs: exchange_kernel((panels, fronts), *refs), na...  32.9 us
    pallas_call x1, Pallas kernels, update_step(): pl.pallas_call(update_kernel, name='update', grid=(steps,), out_shape=[ja...  16.1 us

profile of v7, /device:TPU:1, one launch (start us, length us, event | category | flops | bytes accessed | tf_op | source)
XLA Modules:
  0.0 189.0 jit_solution(18150493134444845206)
XLA Ops:
  0.6 0.8 copy.10
  1.4 0.1 broadcast_in_dim.20.refs_1_
  1.5 0.0 copy-start.4
  1.5 1.2 copy-done.4
  2.7 0.0 copy-start
  2.7 0.0 copy-start.1
  2.7 0.0 copy-start.2
  2.7 0.0 copy-start.3
  2.7 32.9 %exchange.1 = (bf16[8,8,16,4,128]{4,3,2,1,0:T(4,128)(2,1)S(1)}, bf16[56,16,4,128]{3,2,1,0:T(4,128)(2,1)S(1)}, s32[8,16,4,128]{3,2,1,0:T(4,128)S(1)}, s32[8,2,4,128]{3,2,1,0:T(4,128)S(1)}) custom-call(bf16[16,64,4,128]{3,2,1,0:T(4,128)(2,1)S(1)} %bitcast.22, s32[16,4,128]{2,1,0:T(4,128)S(1)} %broadcast_in_dim.20.refs_1_), custom_call_target="tpu_custom_call" | custom-call | flops 20000000000 | bytes 60000000 | tf_op jit(solution)/shard_map/exchange/pallas_call | solution.py:190
  35.6 0.0 copy-done
  35.6 0.0 copy-done.1
  35.7 0.0 copy-done.2
  35.7 0.0 copy-done.3
  35.7 137.0 %panel_step.1 = (bf16[2,16,512,512]{3,2,1,0:T(8,128)(2,1)}, bf16[8,56,16,4,128]{4,3,2,1,0:T(4,128)(2,1)S(1)}, f32[512,1024]{1,0:T(8,128)S(1)}, bf16[2,512,512]{2...) custom-call(s32[8]{0:T(128)S(1)} %copy-done.3, ...), custom_call_target="tpu_custom_call" | custom-call | tf_op jit(solution)/shard_map/panel_step/pallas_call | solution.py:695
  172.7 16.1 %update.1 = (bf16[512,7168]{1,0:T(8,128)(2,1)}, f32[512,1024]{1,0:T(8,128)}, f32[512,128]{1,0:T(8,128)}, f32[16,4,128]{2,1,0:T(4,128)}) custom-call(bf16[8,56,64,128]{3,2,1,0:T(8,128)(2,1)S(1)} %bitcast.15, bf16[2,16,512,512]{3,2,1,0:T(8,128)(2,1)} %get-tuple-element.24.blocks, bf16[2,512,512]{2,1,0:T(8,128)(2,1)S(1)} %get-tuple-element.25.weights, ...), custom_call_target="tpu_custom_call" | custom-call | tf_op jit(solution)/shard_map/update/pallas_call | solution.py:783
Async XLA Ops:
  1.5 1.2 copy-start.4
  2.7 32.9 %copy-start = (f32[1,512,1024]{2,1,0:T(8,128)S(1)}, f32[1,512,1024]{2,1,0:T(8,128)}, u32[]{:S(2)}) copy-start(f32[1,512,1024]{2,1,0:T(8,128)} %param.6) | copy-start | bytes 6291460
  2.7 32.9 %copy-start.1 = (f32[1,1024,128]{2,1,0:T(8,128)S(1)}, f32[1,1024,128]{2,1,0:T(8,128)}, u32[]{:S(2)}) copy-start(f32[1,1024,128]{2,1,0:T(8,128)} %param.10) | copy-start | bytes 1572868
  2.7 33.0 %copy-start.2 = (f32[1,512,128]{2,1,0:T(8,128)S(1)}, f32[1,512,128]{2,1,0:T(8,128)}, u32[]{:S(2)}) copy-start(f32[1,512,128]{2,1,0:T(8,128)} %param.11) | copy-start | bytes 786436
  2.7 33.0 %copy-start.3 = (s32[8]{0:T(128)S(1)}, s32[8]{0:T(128)}, u32[]{:S(2)}) copy-start(s32[8]{0:T(128)} %refs_0_.1) | copy-start | bytes 100

commit v8 on v7

--- a/solution.py
+++ b/solution.py
@@ -152,8 +152,6 @@
     ]
     for copy in own:
         copy.start()
-    for shift in range(1, panels):
-        late_copy(shift).start()
     for copy in own:
         copy.wait()
     for shift in range(1, panels):
@@ -174,6 +172,8 @@
     for shift in range(1, fronts):
         to_front(table, front_send_s, front_recv_s, shift).start()
         to_front(early, front_send, front_recv, shift).start()
+    for shift in range(1, panels):
+        late_copy(shift).start()
     for shift in range(1, panels):
         slot_copy(shift).wait_send()
         early_copy(shift).wait_send()

time: 189 us -> 183 us (0.968)
  Pallas kernels: 186 us -> 180 us
    pallas_call x1, Pallas kernels: 137 us -> 133 us  [panel_step(): pl.pallas_call(lambda *refs: panel_kernel((panels, fronts), side, *refs),...]
    pallas_call x1, Pallas kernels: 32.9 us -> 30.1 us  [exchange_rows(): pl.pallas_call(lambda *refs: exchange_kernel((panels, fronts), *refs), na...]
where the time goes in v8:
time: 183 us
  Pallas kernels  180 us (98%)
  local copies, waits for them, and re-layouts  2.08 us (1%)
    pallas_call x1, Pallas kernels, panel_step(): pl.pallas_call(lambda *refs: panel_kernel((panels, fronts), side, *refs),...  133 us
    pallas_call x1, Pallas kernels, exchange_rows(): pl.pallas_call(lambda *refs: exchange_kernel((panels, fronts), *refs), na...  30.1 us
    pallas_call x1, Pallas kernels, update_step(): pl.pallas_call(update_kernel, name='update', grid=(steps,), out_shape=[ja...  16.1 us

profile of v8, /device:TPU:1, one launch (start us, length us, event | category | flops | bytes accessed | tf_op | source)
XLA Modules:
  0.0 182.6 jit_solution(8356720397081866381)
XLA Ops:
  0.6 0.8 copy.10
  1.4 0.1 broadcast_in_dim.20.refs_1_
  1.5 0.0 copy-start.4
  1.5 1.2 copy-done.4
  2.7 0.0 copy-start
  2.7 0.0 copy-start.1
  2.7 0.0 copy-start.2
  2.7 0.0 copy-start.3
  2.7 30.1 %exchange.1 = (bf16[8,8,16,4,128]{4,3,2,1,0:T(4,128)(2,1)S(1)}, bf16[56,16,4,128]{3,2,1,0:T(4,128)(2,1)S(1)}, s32[8,16,4,128]{3,2,1,0:T(4,128)S(1)}, s32[8,2,4,128]{3,2,1,0:T(4,128)S(1)}) custom-call(bf16[16,64,4,128]{3,2,1,0:T(4,128)(2,1)S(1)} %bitcast.22, s32[16,4,128]{2,1,0:T(4,128)S(1)} %broadcast_in_dim.20.refs_1_), custom_call_target="tpu_custom_call" | custom-call | flops 20000000000 | bytes 60000000 | tf_op jit(solution)/shard_map/exchange/pallas_call | solution.py:190
  32.8 0.0 copy-done
  32.8 0.0 copy-done.1
  32.8 0.0 copy-done.2
  32.8 0.0 copy-done.3
  32.9 133.5 %panel_step.1 = (bf16[2,16,512,512]{3,2,1,0:T(8,128)(2,1)}, bf16[8,56,16,4,128]{4,3,2,1,0:T(4,128)(2,1)S(1)}, f32[512,1024]{1,0:T(8,128)S(1)}, bf16[2,512,512]{2...) custom-call(s32[8]{0:T(128)S(1)} %copy-done.3, ...), custom_call_target="tpu_custom_call" | custom-call | tf_op jit(solution)/shard_map/panel_step/pallas_call | solution.py:695
  166.3 16.1 %update.1 = (bf16[512,7168]{1,0:T(8,128)(2,1)}, f32[512,1024]{1,0:T(8,128)}, f32[512,128]{1,0:T(8,128)}, f32[16,4,128]{2,1,0:T(4,128)}) custom-call(bf16[8,56,64,128]{3,2,1,0:T(8,128)(2,1)S(1)} %bitcast.15, bf16[2,16,512,512]{3,2,1,0:T(8,128)(2,1)} %get-tuple-element.24.blocks, bf16[2,512,512]{2,1,0:T(8,128)(2,1)S(1)} %get-tuple-element.25.weights, ...), custom_call_target="tpu_custom_call" | custom-call | tf_op jit(solution)/shard_map/update/pallas_call | solution.py:783
Async XLA Ops:
  1.5 1.2 copy-start.4
  2.7 30.1 %copy-start = (f32[1,512,1024]{2,1,0:T(8,128)S(1)}, f32[1,512,1024]{2,1,0:T(8,128)}, u32[]{:S(2)}) copy-start(f32[1,512,1024]{2,1,0:T(8,128)} %param.6) | copy-start | bytes 6291460
  2.7 30.1 %copy-start.1 = (f32[1,1024,128]{2,1,0:T(8,128)S(1)}, f32[1,1024,128]{2,1,0:T(8,128)}, u32[]{:S(2)}) copy-start(f32[1,1024,128]{2,1,0:T(8,128)} %param.10) | copy-start | bytes 1572868
  2.7 30.1 %copy-start.2 = (f32[1,512,128]{2,1,0:T(8,128)S(1)}, f32[1,512,128]{2,1,0:T(8,128)}, u32[]{:S(2)}) copy-start(f32[1,512,128]{2,1,0:T(8,128)} %param.11) | copy-start | bytes 786436
  2.7 30.1 %copy-start.3 = (s32[8]{0:T(128)S(1)}, s32[8]{0:T(128)}, u32[]{:S(2)}) copy-start(s32[8]{0:T(128)} %refs_0_.1) | copy-start | bytes 100
